TPU v7x, 256 devices: a whole 4x4x8 slice. The times are simulated.
256 devices in a mesh: dp: 2 (over core), seq: 4 (over y), expert: 32 (over x, z).
Axes of the slice: x: 4, y: 4, z: 8, core: 2. Of those that a mesh axis runs over, the one named last changes fastest.
Arguments:
- query_input: bfloat16 [64, 512, 1024], P(('dp', 'expert'), 'seq'), may hold values from -6 to 6
- key_input: bfloat16 [64, 512, 1024], P(('dp', 'expert'), 'seq'), may hold values from -6 to 6
- value_input: bfloat16 [64, 512, 1024], P(('dp', 'expert'), 'seq'), may hold values from -6 to 6
- routes: int32 [64, 512, 2], P(('dp', 'expert'), 'seq'), may hold values from 0 to 31, all different within a row; in each aligned block of 128 rows (0 to 127, 128 to 255, ..., all dimensions but the last counted through in order) at most 12 rows name the same one
- gate_values: float32 [64, 512, 2], P(('dp', 'expert'), 'seq'), may hold values from 0.2 to 1
- up_weight: bfloat16 [32, 1024, 2048], P('expert'), may hold values from -0.1875 to 0.1875
- down_weight: bfloat16 [32, 2048, 1024], P('expert'), may hold values from -0.125 to 0.125
- cotangent: bfloat16 [64, 512, 1024], P(('dp', 'expert'), 'seq'), may hold values from -6 to 6
Outputs:
- layer_output: bfloat16 [64, 512, 1024], P(('dp', 'expert'), 'seq')
- grad_queries: bfloat16 [64, 512, 1024], P(('dp', 'expert'), 'seq')
- grad_keys: bfloat16 [64, 512, 1024], P(('dp', 'expert'), 'seq')
- grad_values: bfloat16 [64, 512, 1024], P(('dp', 'expert'), 'seq')
- grad_up: float32 [32, 1024, 2048], P('expert', ('dp', 'seq'))
- grad_down: float32 [32, 2048, 1024], P('expert', None, ('dp', 'seq'))
Inputs may be any that keep to these rules, and one draw needn't show every extreme that they name: `routes`: each token names 2 different experts. The 128 tokens of one device (aligned blocks of rows) name any one expert at most 12 times, and in every draw some device's tokens name some expert exactly 12 times.
All inputs are finite; a program needn't handle non-finite values.
Results may differ from a plain program's by a relative error of at most 0.017.
Values may be sent and summed in bfloat16 or wider, within the bound.
No kernel may reach another device: no remote copies, remote signals or barrier semaphores. Data moves between devices by JAX's collectives and lax.ppermute only.
A program may use at most 128 MiB of HBM per device.

v0:
```python
import math

import jax
import jax.numpy as jnp
from jax import lax
from jax.sharding import PartitionSpec as P

DH = 128
TOP = 2


EPSILON = 1e-06
GELU_COEF = math.sqrt(2.0 / math.pi)


def gelu_pair(inputs):
    cubic = inputs + 0.044715 * inputs * inputs * inputs
    hyper = jnp.tanh(GELU_COEF * cubic)
    result = 0.5 * inputs * (1.0 + hyper)
    slope_value = 0.5 * (1.0 + hyper) + 0.5 * inputs * (1.0 - hyper * hyper) * GELU_COEF * (
        1.0 + 3.0 * 0.044715 * inputs * inputs
    )
    return (result, slope_value)


def prob_table(query_piece, key_rows):
    scaling = 1.0 / math.sqrt(query_piece.shape[2])
    scores = (
        jnp.einsum("qhd,khd->hqk", query_piece, key_rows, preferred_element_type=jnp.float32)
        * scaling
    )
    highest = jnp.max(scores, axis=-1, keepdims=True)
    exponent = jnp.exp(scores - highest)
    return exponent / jnp.sum(exponent, axis=-1, keepdims=True)


def query_blocks(tensor):
    row_count = tensor.shape[0]
    block_rows = min(512, row_count)
    return tensor.reshape((row_count // block_rows, block_rows) + tensor.shape[1:])


def attention_forward(query_rows, key_rows, value_rows):

    def one_block(query_piece):
        prob_rows = prob_table(query_piece, key_rows)
        prob_bf = prob_rows.astype(jnp.bfloat16)
        return jnp.einsum(
            "hqk,khd->qhd", prob_bf, value_rows, preferred_element_type=jnp.float32
        ).astype(jnp.bfloat16)

    return lax.map(one_block, query_blocks(query_rows)).reshape(query_rows.shape)


def attention_backward(query_rows, key_rows, value_rows, upstream):
    scaling = 1.0 / math.sqrt(query_rows.shape[2])

    def one_block(running, pieces):
        query_piece, grad_piece = pieces
        prob_rows = prob_table(query_piece, key_rows)
        prob_bf = prob_rows.astype(jnp.bfloat16)
        grad_probs = jnp.einsum(
            "qhd,khd->hqk", grad_piece, value_rows, preferred_element_type=jnp.float32
        )
        row_delta = jnp.sum(prob_rows * grad_probs, axis=-1, keepdims=True)
        grad_scores = (prob_rows * (grad_probs - row_delta) * scaling).astype(jnp.bfloat16)
        grad_query = jnp.einsum(
            "hqk,khd->qhd", grad_scores, key_rows, preferred_element_type=jnp.float32
        ).astype(jnp.bfloat16)
        grad_key = running[0] + jnp.einsum(
            "hqk,qhd->khd", grad_scores, query_piece, preferred_element_type=jnp.float32
        )
        grad_value = running[1] + jnp.einsum(
            "hqk,qhd->khd", prob_bf, grad_piece, preferred_element_type=jnp.float32
        )
        return ((grad_key, grad_value), grad_query)

    zero_grads = jnp.zeros(key_rows.shape, jnp.float32)
    (grad_key, grad_value), grad_query = lax.scan(
        one_block, (zero_grads, zero_grads), (query_blocks(query_rows), query_blocks(upstream))
    )
    return (grad_query.reshape(query_rows.shape), grad_key, grad_value)


def shards(
    query_input, key_input, value_input, routes, gate_values, up_weight, down_weight, cotangent
):
    tok_rows = query_input.shape[1]
    model_width = query_input.shape[2]
    owners = lax.axis_size("expert")
    local_experts = up_weight.shape[0]
    experts_all = local_experts * owners
    capacity = tok_rows * TOP * 3 // (2 * experts_all)
    query_local = query_input[0]
    key_local = key_input[0]
    value_local = value_input[0]
    query_heads, key_heads, value_heads = (
        lax.all_to_all(query_local, "seq", split_axis=1, concat_axis=0, tiled=True),
        lax.all_to_all(key_local, "seq", split_axis=1, concat_axis=0, tiled=True),
        lax.all_to_all(value_local, "seq", split_axis=1, concat_axis=0, tiled=True),
    )
    head_shape = (query_heads.shape[0], query_heads.shape[1] // DH, DH)
    query_split = query_heads.reshape(head_shape)
    key_split = key_heads.reshape(head_shape)
    value_split = value_heads.reshape(head_shape)
    out_heads = attention_forward(query_split, key_split, value_split).reshape(query_heads.shape)
    attended = lax.all_to_all(out_heads, "seq", split_axis=0, concat_axis=1, tiled=True)
    chosen = routes[0].reshape(-1)
    expert_ids = jnp.arange(experts_all, dtype=jnp.int32)
    hit_table = (chosen[:, None] == expert_ids[None, :]).astype(jnp.int32)
    slot_rank = jnp.sum((jnp.cumsum(hit_table, axis=0) - hit_table) * hit_table, axis=1)
    slot_index = chosen * capacity + slot_rank
    slot_ids = jnp.arange(experts_all * capacity, dtype=jnp.int32)
    placer = (slot_index[:, None] == slot_ids[None, :]).astype(jnp.bfloat16)

    def send_rows(assigned):
        packed = lax.dot_general(
            placer, assigned, (((0,), (0,)), ((), ())), preferred_element_type=jnp.float32
        ).astype(jnp.bfloat16)
        arrived_rows = lax.all_to_all(
            packed.reshape(owners, local_experts * capacity, model_width),
            "expert",
            split_axis=0,
            concat_axis=0,
            tiled=True,
        )
        return arrived_rows.reshape(owners, local_experts, capacity, model_width)

    def return_rows(results):
        returned_rows = lax.all_to_all(
            results.reshape(owners, local_experts * capacity, model_width),
            "expert",
            split_axis=0,
            concat_axis=0,
            tiled=True,
        )
        flat_rows = returned_rows.reshape(experts_all * capacity, model_width)
        return jnp.dot(placer, flat_rows, preferred_element_type=jnp.float32).reshape(
            tok_rows, TOP, model_width
        )

    attended_f = attended.astype(jnp.float32)
    inverse_rms = lax.rsqrt(jnp.mean(attended_f * attended_f, axis=-1, keepdims=True) + EPSILON)
    unit_rows = attended_f * inverse_rms
    normed = unit_rows.astype(jnp.bfloat16)
    arrived = send_rows(jnp.repeat(normed, TOP, axis=0))
    pre_act = jnp.einsum("gxcd,xdh->gxch", arrived, up_weight, preferred_element_type=jnp.float32)
    act_value, act_slope = gelu_pair(pre_act)
    activated = act_value.astype(jnp.bfloat16)
    produced = jnp.einsum(
        "gxch,xhd->gxcd", activated, down_weight, preferred_element_type=jnp.float32
    ).astype(jnp.bfloat16)
    gate_rows = gate_values[0]
    expert_mix = jnp.sum(gate_rows[:, :, None] * return_rows(produced), axis=1)
    layer_output = (attended_f + expert_mix).astype(jnp.bfloat16)
    upstream = cotangent[0].astype(jnp.float32)
    grad_out_rows = (
        (gate_rows[:, :, None] * upstream[:, None, :])
        .astype(jnp.bfloat16)
        .reshape(tok_rows * TOP, model_width)
    )
    grad_arrived = send_rows(grad_out_rows)
    grad_act = jnp.einsum(
        "gxcd,xhd->gxch", grad_arrived, down_weight, preferred_element_type=jnp.float32
    )
    grad_pre = (grad_act * act_slope).astype(jnp.bfloat16)
    down_local = jnp.einsum(
        "gxch,gxcd->xhd", activated, grad_arrived, preferred_element_type=jnp.float32
    )
    up_local = jnp.einsum("gxcd,gxch->xdh", arrived, grad_pre, preferred_element_type=jnp.float32)
    grad_normed = jnp.einsum(
        "gxch,xdh->gxcd", grad_pre, up_weight, preferred_element_type=jnp.float32
    ).astype(jnp.bfloat16)
    grad_unit = jnp.sum(return_rows(grad_normed), axis=1)
    grad_attended = upstream + inverse_rms * (
        grad_unit - unit_rows * jnp.mean(grad_unit * unit_rows, axis=-1, keepdims=True)
    )
    grad_attended = grad_attended.astype(jnp.bfloat16)
    grad_heads = lax.all_to_all(
        grad_attended, "seq", split_axis=1, concat_axis=0, tiled=True
    ).reshape(head_shape)
    grad_q, grad_k, grad_v = attention_backward(query_split, key_split, value_split, grad_heads)
    flat_shape = (head_shape[0], head_shape[1] * DH)
    grad_queries, grad_keys, grad_values = (
        lax.all_to_all(grad_q.reshape(flat_shape), "seq", split_axis=0, concat_axis=1, tiled=True),
        lax.all_to_all(
            grad_k.astype(jnp.bfloat16).reshape(flat_shape),
            "seq",
            split_axis=0,
            concat_axis=1,
            tiled=True,
        ),
        lax.all_to_all(
            grad_v.astype(jnp.bfloat16).reshape(flat_shape),
            "seq",
            split_axis=0,
            concat_axis=1,
            tiled=True,
        ),
    )
    grad_up, grad_down = (
        lax.psum_scatter(
            up_local.astype(jnp.bfloat16), ("dp", "seq"), scatter_dimension=1, tiled=True
        ).astype(jnp.float32),
        lax.psum_scatter(
            down_local.astype(jnp.bfloat16), ("dp", "seq"), scatter_dimension=2, tiled=True
        ).astype(jnp.float32),
    )
    return (
        layer_output[None],
        grad_queries[None],
        grad_keys[None],
        grad_values[None],
        grad_up,
        grad_down,
    )


def solution(mesh):
    in_specs = (
        P(("dp", "expert"), "seq", None),
        P(("dp", "expert"), "seq", None),
        P(("dp", "expert"), "seq", None),
        P(("dp", "expert"), "seq", None),
        P(("dp", "expert"), "seq", None),
        P("expert", None, None),
        P("expert", None, None),
        P(("dp", "expert"), "seq", None),
    )
    out_specs = (
        P(("dp", "expert"), "seq", None),
        P(("dp", "expert"), "seq", None),
        P(("dp", "expert"), "seq", None),
        P(("dp", "expert"), "seq", None),
        P("expert", ("dp", "seq"), None),
        P("expert", None, ("dp", "seq")),
    )
    return jax.shard_map(shards, mesh=mesh, in_specs=in_specs, out_specs=out_specs, check_vma=False)
```

profile of v0, /device:TPU:2, one launch (start us, length us, event | category | flops | bytes accessed | tf_op | source)
XLA Modules:
  0.0 297.5 jit_solution(12446347084722007181)
XLA Ops:
  9.0 4.5 %all-to-all-start.1 = ((bf16[128,4,256]{2,0,1:T(8,128)(2,1)}), bf16[128,4,256]{2,0,1:T(8,128)(2,1)S(1)}, u32[]{:S(2)}, u32[]{:S(2)}) async-start(bf16[128,4,256]{2,0,1:T(8,128)(2,1)} %copy.91), calls=%async_computation.1 | async-start | bytes 524288 | tf_op jit(solution)/shard_map/all_to_all | solution.py:99
  24.2 6.0 %all-to-all-done = bf16[128,4,256]{2,0,1:T(8,128)(2,1)S(1)} async-done(((bf16[128,4,256]{2,0,1:T(8,128)(2,1)}), bf16[128,4,256]{2,0,1:T(8,128)(2,1)S(1)}, u32[]{:S(2)}, u32[]{:S(2)}) %all-to-all-start) | async-done | bytes 262176 | tf_op jit(solution)/shard_map/all_to_all | solution.py:98
  34.2 6.2 %all-to-all-done.2 = bf16[128,4,256]{2,0,1:T(8,128)(2,1)S(1)} async-done(((bf16[128,4,256]{2,0,1:T(8,128)(2,1)}), bf16[128,4,256]{2,0,1:T(8,128)(2,1)S(1)}, u32[]{:S(2)}, u32[]{:S(2)}) %all-to-all-start.2) | async-done | bytes 262176 | tf_op jit(solution)/shard_map/all_to_all | solution.py:100
  49.3 6.6 %all-to-all-done.3 = bf16[4,128,256]{2,1,0:T(8,128)(2,1)S(1)} async-done(((bf16[4,128,256]{2,1,0:T(8,128)(2,1)}), bf16[4,128,256]{2,1,0:T(8,128)(2,1)S(1)}, u32[]{:S(2)}, u32[]{:S(2)}) %all-to-all-start.3) | async-done | bytes 262176 | tf_op jit(solution)/shard_map/all_to_all | solution.py:107
  58.6 11.7 %all-to-all-start.4 = ((bf16[32,12,1024]{2,1,0:T(8,128)(2,1)}), bf16[32,12,1024]{2,1,0:T(8,128)(2,1)}, u32[]{:S(2)}, u32[]{:S(2)}) async-start(bf16[32,12,1024]{2,1,0:T(8,128)(2,1)} %reshape.263), calls=%async_computation.4 | async-start | bytes 2097152 | tf_op jit(solution)/shard_map/all_to_all | solution.py:120
  73.8 17.9 %all-to-all-done.4 = bf16[32,12,1024]{2,1,0:T(8,128)(2,1)} async-done(((bf16[32,12,1024]{2,1,0:T(8,128)(2,1)}), bf16[32,12,1024]{2,1,0:T(8,128)(2,1)}, u32[]{:S(2)}, u32[]{:S(2)}) %all-to-all-start.4) | async-done | bytes 786464 | tf_op jit(solution)/shard_map/all_to_all | solution.py:120
  91.6 7.7 %all-to-all-start.6 = ((bf16[32,12,1024]{2,1,0:T(8,128)(2,1)}), bf16[32,12,1024]{2,1,0:T(8,128)(2,1)S(1)}, u32[]{:S(2)}, u32[]{:S(2)}) async-start(bf16[32,12,1024]{2,1,0:T(8,128)(2,1)} %reshape.268), calls=%async_computation.6 | async-start | bytes 2097152 | tf_op jit(solution)/shard_map/all_to_all | solution.py:120
  99.6 6.3 %fusion.8 = f32[32,12,2048]{2,0,1:T(8,128)} fusion(bf16[1,1024,2048]{2,1,0:T(8,128)(2,1)} %param.13, bf16[32,12,1024]{2,1,0:T(8,128)(2,1)} %all-to-all-done.4), kind=kOutput, calls=%fused_computation.13 | convolution fusion | flops 1610612736 | bytes 8126464 | tf_op jit(solution)/shard_map/gxcd,xdh->gxch/dot_general | solution.py:147
  105.9 14.5 %all-to-all-done.6 = bf16[32,12,1024]{2,1,0:T(8,128)(2,1)S(1)} async-done(((bf16[32,12,1024]{2,1,0:T(8,128)(2,1)}), bf16[32,12,1024]{2,1,0:T(8,128)(2,1)S(1)}, u32[]{:S(2)}, u32[]{:S(2)}) %all-to-all-start.6) | async-done | bytes 786464 | tf_op jit(solution)/shard_map/all_to_all | solution.py:120
  120.4 7.0 %fusion.11 = bf16[1,2048,1024]{2,1,0:T(8,128)(2,1)} fusion(bf16[32,12,1024]{2,1,0:T(8,128)(2,1)S(1)} %all-to-all-done.6, f32[32,12,2048]{2,0,1:T(8,128)} %fusion.8), kind=kOutput, calls=%fused_computation.16 | convolution fusion | flops 1619787776 | bytes 8126464 | tf_op jit(solution)/shard_map/gxch,gxcd->xhd/dot_general | solution.py:167
  127.3 20.6 %copy.138 = bf16[1,2048,1024]{1,0,2:T(2,128)(2,1)} copy(bf16[1,2048,1024]{2,1,0:T(8,128)(2,1)} %fusion.11) | data formatting | bytes 8388608
  147.9 8.0 %copy.180 = bf16[1024,1,2048]{2,0,1:T(8,128)(2,1)} copy(bf16[1024,1,2048]{2,1,0:T(2,128)(2,1)} %bitcast.167) | data formatting | bytes 8388608
  156.2 7.0 %fusion.21 = bf16[32,12,2048]{2,0,1:T(8,128)(2,1)S(1)} fusion(f32[32,12,2048]{2,0,1:T(8,128)} %fusion.8, bf16[1,2048,1024]{2,1,0:T(8,128)(2,1)} %param.14, bf16[32,12,1024]{2,1,0:T(8,128)(2,1)S(1)} %all-to-all-done.6), kind=kOutput, calls=%fused_computation.26 | convolution fusion | flops 1625554944 | bytes 9699328 | tf_op jit(solution)/shard_map/gxcd,xhd->gxch/dot_general | solution.py:163
  164.4 5.7 %fusion.10 = bf16[1,1024,2048]{2,1,0:T(8,128)(2,1)} fusion(bf16[32,12,2048]{2,0,1:T(8,128)(2,1)S(1)} %fusion.21, bf16[32,12,1024]{2,1,0:T(8,128)(2,1)} %all-to-all-done.4), kind=kOutput, calls=%fused_computation.15 | convolution fusion | flops 1612709888 | bytes 6553600 | tf_op jit(solution)/shard_map/gxcd,gxch->xdh/dot_general | solution.py:170
  170.1 4.6 %fusion.36 = bf16[32,12,1024]{2,0,1:T(8,128)(2,1)S(1)} fusion(bf16[32,12,2048]{2,0,1:T(8,128)(2,1)} %copy-done.8, bf16[1,1024,2048]{2,1,0:T(8,128)(2,1)} %param.13), kind=kOutput, calls=%fused_computation.37 | convolution fusion | flops 1611005952 | bytes 6553600 | tf_op jit(solution)/shard_map/gxch,xdh->gxcd/dot_general | solution.py:171
  176.0 7.7 %all-to-all-start.7 = ((bf16[32,12,1024]{2,1,0:T(8,128)(2,1)}), bf16[32,12,1024]{2,1,0:T(8,128)(2,1)S(1)}, u32[]{:S(2)}, u32[]{:S(2)}) async-start(bf16[32,12,1024]{2,1,0:T(8,128)(2,1)} %copy.113), calls=%async_computation.7 | async-start | bytes 2097152 | tf_op jit(solution)/shard_map/all_to_all | solution.py:130
  183.8 5.3 %fusion.39 = bf16[32,12,1024]{2,0,1:T(8,128)(2,1)S(1)} fusion(bf16[1,2048,1024]{2,1,0:T(8,128)(2,1)} %param.14, f32[32,12,2048]{2,0,1:T(8,128)} %fusion.8), kind=kOutput, calls=%fused_computation.38 | convolution fusion | flops 1618083840 | bytes 8126464 | tf_op jit(solution)/shard_map/gxch,xhd->gxcd/dot_general | solution.py:150
  190.5 13.3 %all-to-all-done.7 = bf16[32,12,1024]{2,1,0:T(8,128)(2,1)S(1)} async-done(((bf16[32,12,1024]{2,1,0:T(8,128)(2,1)}), bf16[32,12,1024]{2,1,0:T(8,128)(2,1)S(1)}, u32[]{:S(2)}, u32[]{:S(2)}) %all-to-all-start.7) | async-done | bytes 786464 | tf_op jit(solution)/shard_map/all_to_all | solution.py:130
  203.7 8.0 %all-to-all-start.5 = ((bf16[32,12,1024]{2,1,0:T(8,128)(2,1)}), bf16[32,12,1024]{2,1,0:T(8,128)(2,1)S(1)}, u32[]{:S(2)}, u32[]{:S(2)}) async-start(bf16[32,12,1024]{2,1,0:T(8,128)(2,1)} %copy.107), calls=%async_computation.5 | async-start | bytes 2097152 | tf_op jit(solution)/shard_map/all_to_all | solution.py:130
  217.2 13.9 %all-to-all-done.5 = bf16[32,12,1024]{2,1,0:T(8,128)(2,1)S(1)} async-done(((bf16[32,12,1024]{2,1,0:T(8,128)(2,1)}), bf16[32,12,1024]{2,1,0:T(8,128)(2,1)S(1)}, u32[]{:S(2)}, u32[]{:S(2)}) %all-to-all-start.5) | async-done | bytes 786464 | tf_op jit(solution)/shard_map/all_to_all | solution.py:130
  236.4 7.7 %all-to-all-done.8 = bf16[128,4,256]{2,0,1:T(8,128)(2,1)S(1)} async-done(((bf16[128,4,256]{2,0,1:T(8,128)(2,1)}), bf16[128,4,256]{2,0,1:T(8,128)(2,1)S(1)}, u32[]{:S(2)}, u32[]{:S(2)}) %all-to-all-start.8) | async-done | bytes 262176 | tf_op jit(solution)/shard_map/all_to_all | solution.py:179
  251.2 4.0 %fusion.51 = bf16[512,2,128]{2,0,1:T(8,128)(2,1)} fusion(f32[2,512,512]{1,2,0:T(8,128)S(1)} %fusion.83, bf16[512,2,128]{2,1,0:T(2,128)(2,1)} %copy-done.6, f32[2,512,512]{1,2,0:T(8,128)} %get-tuple-element.58, f32[2,512]{1,0:T(2,128)S(1)} %get-tuple-element.57), kind=kOutput, calls=%fused_computation.48 | convolution fusion | flops 138020352 | bytes 4722688 | tf_op jit(solution)/shard_map/while/body/eval_jaxpr/hqk,qhd->khd/dot_general | solution.py:70
  257.3 4.5 %all-to-all-done.11 = bf16[4,128,256]{1,2,0:T(8,128)(2,1)S(1)} async-done(((bf16[4,128,256]{1,2,0:T(8,128)(2,1)}), bf16[4,128,256]{1,2,0:T(8,128)(2,1)S(1)}, u32[]{:S(2)}, u32[]{:S(2)}) %all-to-all-start.11) | async-done | bytes 262176 | tf_op jit(solution)/shard_map/all_to_all | solution.py:193
  265.2 4.1 %fusion.54 = bf16[512,2,128]{2,0,1:T(8,128)(2,1)} fusion(f32[2,512,512]{1,2,0:T(8,128)S(1)} %fusion.83, bf16[512,2,128]{2,1,0:T(2,128)(2,1)S(1)} %copy-done.5, f32[2,512,512]{1,2,0:T(8,128)} %get-tuple-element.58, f32[2,512]{1,0:T(2,128)S(1)} %get-tuple-element.57), kind=kOutput, calls=%fused_computation.49 | convolution fusion | flops 138020352 | bytes 4722688 | tf_op jit(solution)/shard_map/while/body/eval_jaxpr/hqk,khd->qhd/dot_general | solution.py:67
  (112 shorter events, 80.5 us)
Async XLA Ops:
  9.0 11.1 %all-to-all-start.1 = ((bf16[128,4,256]{2,0,1:T(8,128)(2,1)}), bf16[128,4,256]{2,0,1:T(8,128)(2,1)S(1)}, u32[]{:S(2)}, u32[]{:S(2)}) async-start(bf16[128,4,256]{2,0,1:T(8,128)(2,1)} %copy.91), calls=%async_computation.1 | async-start | bytes 524288 | tf_op jit(solution)/shard_map/all_to_all | solution.py:99
  20.2 10.1 %all-to-all-start = ((bf16[128,4,256]{2,0,1:T(8,128)(2,1)}), bf16[128,4,256]{2,0,1:T(8,128)(2,1)S(1)}, u32[]{:S(2)}, u32[]{:S(2)}) async-start(bf16[128,4,256]{2,0,1:T(8,128)(2,1)} %copy.90), calls=%async_computation | async-start | bytes 524288 | tf_op jit(solution)/shard_map/all_to_all | solution.py:98
  30.2 10.1 %all-to-all-start.2 = ((bf16[128,4,256]{2,0,1:T(8,128)(2,1)}), bf16[128,4,256]{2,0,1:T(8,128)(2,1)S(1)}, u32[]{:S(2)}, u32[]{:S(2)}) async-start(bf16[128,4,256]{2,0,1:T(8,128)(2,1)} %copy.94), calls=%async_computation.2 | async-start | bytes 524288 | tf_op jit(solution)/shard_map/all_to_all | solution.py:100
  34.1 10.6 %copy-start.4 = (bf16[512,2,128]{2,1,0:T(2,128)(2,1)}, bf16[512,2,128]{2,1,0:T(2,128)(2,1)S(1)}, u32[]{:S(2)}) copy-start(bf16[512,2,128]{2,1,0:T(2,128)(2,1)S(1)} %reshape.259) | copy-start | bytes 786436
  34.1 10.6 %copy-start.6 = (bf16[512,2,128]{2,1,0:T(2,128)(2,1)}, bf16[512,2,128]{2,1,0:T(2,128)(2,1)S(1)}, u32[]{:S(2)}) copy-start(bf16[512,2,128]{2,1,0:T(2,128)(2,1)S(1)} %squeeze.15) | copy-start | bytes 786436
  40.4 4.3 %copy-start.1 = (bf16[512,2,128]{2,1,0:T(2,128)(2,1)}, bf16[512,2,128]{2,1,0:T(2,128)(2,1)S(1)}, u32[]{:S(2)}) copy-start(bf16[512,2,128]{2,1,0:T(2,128)(2,1)S(1)} %reshape.260) | copy-start | bytes 786436
  45.9 10.1 %all-to-all-start.3 = ((bf16[4,128,256]{2,1,0:T(8,128)(2,1)}), bf16[4,128,256]{2,1,0:T(8,128)(2,1)S(1)}, u32[]{:S(2)}, u32[]{:S(2)}) async-start(bf16[4,128,256]{2,1,0:T(8,128)(2,1)} %all_to_all.113), calls=%async_computation.3 | async-start | bytes 524288 | tf_op jit(solution)/shard_map/all_to_all | solution.py:107
  56.8 13.5 %copy-start.3 = (bf16[1,128,1024]{2,1,0:T(8,128)(2,1)S(1)}, bf16[1,128,1024]{2,1,0:T(8,128)(2,1)}, u32[]{:S(2)}) copy-start(bf16[1,128,1024]{2,1,0:T(8,128)(2,1)} %param.15) | copy-start | bytes 786436
  58.6 33.0 %all-to-all-start.4 = ((bf16[32,12,1024]{2,1,0:T(8,128)(2,1)}), bf16[32,12,1024]{2,1,0:T(8,128)(2,1)}, u32[]{:S(2)}, u32[]{:S(2)}) async-start(bf16[32,12,1024]{2,1,0:T(8,128)(2,1)} %reshape.263), calls=%async_computation.4 | async-start | bytes 2097152 | tf_op jit(solution)/shard_map/all_to_all | solution.py:120
  70.3 1.5 copy-start.7
  91.6 28.7 %all-to-all-start.6 = ((bf16[32,12,1024]{2,1,0:T(8,128)(2,1)}), bf16[32,12,1024]{2,1,0:T(8,128)(2,1)S(1)}, u32[]{:S(2)}, u32[]{:S(2)}) async-start(bf16[32,12,1024]{2,1,0:T(8,128)(2,1)} %reshape.268), calls=%async_computation.6 | async-start | bytes 2097152 | tf_op jit(solution)/shard_map/all_to_all | solution.py:120
  99.4 185.6 %reduce-scatter.7.cloned.1.call-start = ((), (), s32[]{:S(2)}) async-start(), calls=%async_computation.15 | async-start | bytes 4718592
  155.9 132.6 %reduce-scatter.5.cloned.1.call-start = ((), (), s32[]{:S(2)}) async-start(), calls=%async_computation.14 | async-start | bytes 4718592 | tf_op jit(solution)/shard_map/reduce_scatter | solution.py:202
  163.2 1.2 copy-start.8
  176.0 27.7 %all-to-all-start.7 = ((bf16[32,12,1024]{2,1,0:T(8,128)(2,1)}), bf16[32,12,1024]{2,1,0:T(8,128)(2,1)S(1)}, u32[]{:S(2)}, u32[]{:S(2)}) async-start(bf16[32,12,1024]{2,1,0:T(8,128)(2,1)} %copy.113), calls=%async_computation.7 | async-start | bytes 2097152 | tf_op jit(solution)/shard_map/all_to_all | solution.py:130
  203.7 27.3 %all-to-all-start.5 = ((bf16[32,12,1024]{2,1,0:T(8,128)(2,1)}), bf16[32,12,1024]{2,1,0:T(8,128)(2,1)S(1)}, u32[]{:S(2)}, u32[]{:S(2)}) async-start(bf16[32,12,1024]{2,1,0:T(8,128)(2,1)} %copy.107), calls=%async_computation.5 | async-start | bytes 2097152 | tf_op jit(solution)/shard_map/all_to_all | solution.py:130
  212.9 3.3 %copy-start = (f32[128,4,256]{2,0,1:T(8,128)S(1)}, f32[128,4,256]{2,0,1:T(8,128)}, u32[]{:S(2)}) copy-start(f32[128,4,256]{2,0,1:T(8,128)} %copy.117) | copy-start | bytes 1572868
  231.1 13.0 %all-to-all-start.8 = ((bf16[128,4,256]{2,0,1:T(8,128)(2,1)}), bf16[128,4,256]{2,0,1:T(8,128)(2,1)S(1)}, u32[]{:S(2)}, u32[]{:S(2)}) async-start(bf16[128,4,256]{2,0,1:T(8,128)(2,1)} %fusion.74), calls=%async_computation.8 | async-start | bytes 524288 | tf_op jit(solution)/shard_map/all_to_all | solution.py:179
  244.3 6.4 %copy-start.2 = (bf16[512,2,128]{2,1,0:T(2,128)(2,1)S(1)}, bf16[512,2,128]{2,1,0:T(2,128)(2,1)}, u32[]{:S(2)}) copy-start(bf16[512,2,128]{2,1,0:T(2,128)(2,1)} %copy-done.1) | copy-start | bytes 786436
  247.3 14.4 %all-to-all-start.11 = ((bf16[4,128,256]{1,2,0:T(8,128)(2,1)}), bf16[4,128,256]{1,2,0:T(8,128)(2,1)S(1)}, u32[]{:S(2)}, u32[]{:S(2)}) async-start(bf16[4,128,256]{1,2,0:T(8,128)(2,1)} %copy.129), calls=%async_computation.11 | async-start | bytes 524288 | tf_op jit(solution)/shard_map/all_to_all | solution.py:193
  251.2 14.0 %copy-start.5 = (bf16[512,2,128]{2,1,0:T(2,128)(2,1)S(1)}, bf16[512,2,128]{2,1,0:T(2,128)(2,1)}, u32[]{:S(2)}) copy-start(bf16[512,2,128]{2,1,0:T(2,128)(2,1)} %copy-done.4) | copy-start | bytes 786436
  261.8 12.1 %all-to-all-start.10 = ((bf16[4,128,256]{2,1,0:T(8,128)(2,1)}), bf16[4,128,256]{2,1,0:T(8,128)(2,1)S(1)}, u32[]{:S(2)}, u32[]{:S(2)}) async-start(bf16[4,128,256]{2,1,0:T(8,128)(2,1)} %all_to_all.124), calls=%async_computation.10 | async-start | bytes 524288 | tf_op jit(solution)/shard_map/all_to_all | solution.py:186
  273.8 10.1 %all-to-all-start.9 = ((bf16[4,128,256]{2,1,0:T(8,128)(2,1)}), bf16[4,128,256]{2,1,0:T(8,128)(2,1)S(1)}, u32[]{:S(2)}, u32[]{:S(2)}) async-start(bf16[4,128,256]{2,1,0:T(8,128)(2,1)} %all_to_all.121), calls=%async_computation.9 | async-start | bytes 524288 | tf_op jit(solution)/shard_map/all_to_all | solution.py:185
Sparse Core Ops, SparseCore 0:
  156.1 51.4 reduce-scatter.6
  210.1 62.3 reduce-scatter.4
where the time goes:
time: 300 us; the launch traced here: 297 us
  waiting for transfers between devices  97.8 us (33%)
  starting transfers between devices  64.2 us (21%)
  local copies, waits for them, and re-layouts  59.2 us (20%)
  matrix products  54.5 us (18%)
  between operations  14.6 us (5%)
  other arithmetic  7.13 us (2%)
    unnamed x28, local copies, waits for them, and re-layouts  35.9 us
    all_to_all x2, waiting for transfers between devices, send_rows(): lax.all_to_all(packed.reshape(owners, local_experts * capacity, model_wid...  32.4 us
    all_to_all x2, waiting for transfers between devices, return_rows(): lax.all_to_all(results.reshape(owners, local_experts * capacity, model_wi...  27.1 us
    all_to_all x2, starting transfers between devices, send_rows(): lax.all_to_all(packed.reshape(owners, local_experts * capacity, model_wid...  19.4 us
    all_to_all x2, starting transfers between devices, return_rows(): lax.all_to_all(results.reshape(owners, local_experts * capacity, model_wi...  15.7 us
    all_to_all x1, waiting for transfers between devices, shards(): lax.all_to_all(grad_attended, 'seq', split_axis=1, concat_axis=0, tiled=T...  7.69 us
    dot_general x1, matrix products, shards(): jnp.einsum('gxcd,xhd->gxch', grad_arrived, down_weight, preferred_element...  6.97 us
    dot_general x1, matrix products, shards(): jnp.einsum('gxch,gxcd->xhd', activated, grad_arrived, preferred_element_t...  6.97 us
  transfers between devices with their start and end apart: 14, of which 12 were waited for; matrix products, arithmetic and copies ran while one was open for 23% of the time, Pallas kernels for 0%

commit v1 on v0

v1 whole, which is shorter than its diff:
```python
import functools
import math

import jax
import jax.numpy as jnp
from jax import lax
from jax.experimental import pallas as pl
from jax.experimental.pallas import tpu as pltpu
from jax.sharding import PartitionSpec as P

DH = 128
TOP = 2
EPSILON = 1e-06
GELU_COEF = math.sqrt(2.0 / math.pi)
BF = jnp.bfloat16
F32 = jnp.float32
VMEM = pl.BlockSpec(memory_space=pltpu.VMEM)
SMEM = pl.BlockSpec(memory_space=pltpu.SMEM)
NN = (((1,), (0,)), ((), ()))
NT = (((1,), (1,)), ((), ()))
TN = (((0,), (0,)), ((), ()))
HEAVY = pl.CostEstimate(flops=1_000_000_000_000, transcendentals=0, bytes_accessed=1_000_000)
BIG = pltpu.CompilerParams(vmem_limit_bytes=56 * 1024 * 1024)


def dot(a, b, dims=NN):
    return lax.dot_general(a, b, dims, preferred_element_type=F32)


def sds(shape, dtype):
    return jax.ShapeDtypeStruct(shape, dtype)


def lane_block(me, step, parts, width):
    return pl.ds(pl.multiple_of(lax.rem(me + step, parts) * width, width), width)


def split_kernel(parts, me_ref, q_ref, k_ref, v_ref, *outs):
    me = me_ref[0]
    rows = q_ref.shape[0]
    width = q_ref.shape[1] // parts
    for step in range(parts):
        lanes = lane_block(me, step, parts, width)
        for i, ref in enumerate((q_ref, k_ref, v_ref)):
            outs[step][i * rows:(i + 1) * rows, :] = ref[:, lanes]


def join_kernel(parts, me_ref, *refs):
    me = me_ref[0]
    pieces, outs = refs[:parts], refs[parts:]
    rows = outs[0].shape[0]
    width = outs[0].shape[1] // parts
    for step in range(parts):
        lanes = lane_block(me, step, parts, width)
        for i, ref in enumerate(outs):
            ref[:, lanes] = pieces[step][i * rows:(i + 1) * rows, :]


def attend_kernel(parts, *refs):
    pieces = refs[:parts]
    outs = refs[parts:2 * parts]
    probs_ref, keys, values = refs[2 * parts:]
    rows = outs[0].shape[0]
    width = outs[0].shape[1]
    scaling = 1.0 / math.sqrt(DH)
    for step in range(parts):
        keys[step * rows:(step + 1) * rows, :] = pieces[step][rows:2 * rows, :]
        values[step * rows:(step + 1) * rows, :] = pieces[step][2 * rows:3 * rows, :]
    for head in range(width // DH):
        lanes = slice(head * DH, (head + 1) * DH)
        for step in range(parts):
            scores = dot(pieces[step][0:rows, lanes], keys[:, lanes], NT) * scaling
            exponent = jnp.exp(scores - jnp.max(scores, axis=-1, keepdims=True))
            probs = exponent / jnp.sum(exponent, axis=-1, keepdims=True)
            probs_ref[head, step * rows:(step + 1) * rows, :] = probs
            outs[step][:, lanes] = dot(probs.astype(BF), values[:, lanes]).astype(BF)


def attend_back_kernel(parts, *refs):
    pieces = refs[:parts]
    grads = refs[parts:2 * parts]
    probs_ref = refs[2 * parts]
    outs = refs[2 * parts + 1:3 * parts + 1]
    keys, values, grad_keys, grad_values = refs[3 * parts + 1:]
    rows = grads[0].shape[0]
    width = grads[0].shape[1]
    scaling = 1.0 / math.sqrt(DH)
    for step in range(parts):
        keys[step * rows:(step + 1) * rows, :] = pieces[step][rows:2 * rows, :]
        values[step * rows:(step + 1) * rows, :] = pieces[step][2 * rows:3 * rows, :]
    for head in range(width // DH):
        lanes = slice(head * DH, (head + 1) * DH)
        for step in range(parts):
            query = pieces[step][0:rows, lanes]
            grad = grads[step][:, lanes]
            probs = probs_ref[head, step * rows:(step + 1) * rows, :]
            grad_probs = dot(grad, values[:, lanes], NT)
            delta = jnp.sum(probs * grad_probs, axis=-1, keepdims=True)
            grad_scores = (probs * (grad_probs - delta) * scaling).astype(BF)
            outs[step][0:rows, lanes] = dot(grad_scores, keys[:, lanes]).astype(BF)
            key_part = dot(grad_scores, query, TN)
            value_part = dot(probs.astype(BF), grad, TN)
            if step == 0:
                grad_keys[:, lanes] = key_part
                grad_values[:, lanes] = value_part
            else:
                grad_keys[:, lanes] += key_part
                grad_values[:, lanes] += value_part
    for step in range(parts):
        outs[step][rows:2 * rows, :] = grad_keys[step * rows:(step + 1) * rows, :].astype(BF)
        outs[step][2 * rows:3 * rows, :] = grad_values[step * rows:(step + 1) * rows, :].astype(BF)


def chunk_of(array, c):
    return array[:, c * 128:(c + 1) * 128]


def lane_cat(pieces):
    return jnp.concatenate(pieces, axis=1)


def half_pickers(owners):
    shape = (owners * 4, owners * 8)
    row = lax.broadcasted_iota(jnp.int32, shape, 0)
    col = lax.broadcasted_iota(jnp.int32, shape, 1)
    first = lax.shift_left(lax.shift_right_logical(row, 2), 3) + lax.bitwise_and(row, 3)
    return [(col == first + 4 * half).astype(F32).astype(BF) for half in range(2)]


def read_tiles(ref):
    owners, lines, _ = ref.shape
    tiles = [
        ref[:, 8 * t:8 * t + 8, :].astype(F32).reshape(owners * 8, 128).astype(BF)
        for t in range(lines // 8)
    ]
    count = len(tiles) * 2 // 3
    return tiles[:count], lane_cat(tiles[count:])


def write_tiles(ref, low, high):
    owners = ref.shape[0]
    count = low.shape[1] // 128
    for c in range(count):
        ref[:, 8 * c:8 * c + 8, :] = chunk_of(low, c).reshape(owners, 8, 128).astype(BF)
    for c in range(count // 2):
        start = 8 * (count + c)
        ref[:, start:start + 8, :] = chunk_of(high, c).reshape(owners, 8, 128).astype(BF)


def split_parity(array):
    count = array.shape[1] // 128
    return [lane_cat([chunk_of(array, c) for c in range(half, count, 2)]) for half in range(2)]


def merge_parity(even, odd):
    count = even.shape[1] // 128
    return lane_cat([chunk_of(part, c) for c in range(count) for part in (even, odd)])


def unpack_rows(ref, out_ref):
    low, high = read_tiles(ref)
    owners = ref.shape[0]
    even, odd = [dot(pick, high).astype(BF) for pick in half_pickers(owners)]
    out_ref[0:owners * 8, :] = lane_cat(low)
    out_ref[owners * 8:, :] = merge_parity(even, odd)


def pack_rows(rows, ref):
    owners = ref.shape[0]
    pickers = half_pickers(owners)
    parts = split_parity(rows[owners * 8:, :].astype(BF))
    high = dot(pickers[0], parts[0], TN) + dot(pickers[1], parts[1], TN)
    write_tiles(ref, rows[0:owners * 8, :], high)


def pack_tokens(places, arrays, ref):
    low = sum([dot(place[0], x) for place, x in zip(places, arrays)])
    high = None
    for place, x in zip(places, arrays):
        for half, part in enumerate(split_parity(x)):
            term = dot(place[1 + half], part)
            high = term if high is None else high + term
    write_tiles(ref, low, high)


def unpack_tokens(place, low, high):
    even, odd = [dot(place[1 + half], high, TN) for half in range(2)]
    return dot(place[0], lane_cat(low), TN) + merge_parity(even, odd)


def column(row):
    side = row.shape[1]
    return jnp.broadcast_to(row, (side, side)).T[:, 0:1]


def place_kernel(experts, routes_ref, gates_ref, cot_ref, place_ref, packed_ref):
    tokens = cot_ref.shape[0]
    first = lax.broadcasted_iota(jnp.int32, (tokens, tokens), 0)
    second = lax.broadcasted_iota(jnp.int32, (tokens, tokens), 1)
    earlier = (first < second).astype(F32).astype(BF)
    expert_ids = lax.broadcasted_iota(jnp.int32, (experts, tokens), 0)
    line_ids = lax.broadcasted_iota(jnp.int32, (experts * 8, tokens), 0)
    routes = [routes_ref[j:j + 1, :] for j in range(TOP)]
    hits = [(route == expert_ids).astype(F32) for route in routes]
    before = dot(sum(hits[1:], hits[0]).astype(BF), earlier)
    upstream = cot_ref[...].astype(F32)
    places, arrays = [], []
    for j in range(TOP):
        rank = jnp.sum(before * hits[j], axis=0, keepdims=True).astype(jnp.int32)
        line = routes[j] * 8 + rank
        targets = (
            jnp.where(rank < 8, line, -1),
            jnp.where(rank >= 8, line - 8, -1),
            jnp.where(rank >= 8, line - 4, -1),
        )
        place = [(line_ids == target).astype(F32).astype(BF) for target in targets]
        for i, part in enumerate(place):
            place_ref[j, i] = part
        places.append(place)
        arrays.append((column(gates_ref[j:j + 1, :]) * upstream).astype(BF))
    pack_tokens(places, arrays, packed_ref)


def inverse_rms_of(attended):
    return lax.rsqrt(jnp.mean(attended * attended, axis=-1, keepdims=True) + EPSILON)


def joint_place(place_ref):
    joint = []
    for i in range(3):
        part = place_ref[0, i]
        for j in range(1, TOP):
            part = part + place_ref[j, i]
        joint.append(part)
    return joint


def norm_kernel(parts, me_ref, place_ref, *refs):
    pieces, (attended_ref, packed_ref) = refs[:parts], refs[parts:]
    me = me_ref[0]
    width = pieces[0].shape[1]
    for step in range(parts):
        attended_ref[:, lane_block(me, step, parts, width)] = pieces[step][...]
    attended = attended_ref[...].astype(F32)
    normed = (attended * inverse_rms_of(attended)).astype(BF)
    pack_tokens([joint_place(place_ref)], [normed], packed_ref)


def turn_rows(pairs, parts, rows_ref, turned_ref):
    band = rows_ref.shape[1] // (pairs * parts)
    for s in range(pairs * parts):
        block = (s % pairs) * parts + s // pairs
        turned_ref[s * band:(s + 1) * band, :] = rows_ref[:, block * band:(block + 1) * band].T


def dact_kernel(pairs, parts, packed_ref, down_ref, out_ref, turned_ref, rows):
    @pl.when(pl.program_id(0) == 0)
    def _():
        unpack_rows(packed_ref, rows)
        turn_rows(pairs, parts, rows, turned_ref)

    out_ref[...] = dot(rows[...], down_ref[...], NT)


def expert_kernel(packed_ref, up_ref, dact_ref, hidden_ref, rows_ref, dnormed_ref, total):
    step = pl.program_id(0)

    @pl.when(step == 0)
    def _():
        unpack_rows(packed_ref, rows_ref)

    chunk = up_ref.shape[1]
    part = None
    for start in range(0, chunk, 256):
        lanes = slice(start, start + 256)
        weights = up_ref[:, lanes]
        pre = dot(rows_ref[...], weights)
        square = pre * pre
        hyper = jnp.tanh(GELU_COEF * (pre + 0.044715 * pre * square))
        hidden_ref[0, :, lanes] = (0.5 * pre * (1.0 + hyper)).astype(BF)
        slope = 0.5 * (1.0 + hyper) + 0.5 * pre * (1.0 - hyper * hyper) * GELU_COEF * (
            1.0 + 3.0 * 0.044715 * square
        )
        dpre = (dact_ref[:, lanes] * slope).astype(BF)
        hidden_ref[1, :, lanes] = dpre
        term = dot(dpre, weights, NT)
        part = term if part is None else part + term

    @pl.when(step == 0)
    def _():
        total[...] = part

    @pl.when(step > 0)
    def _():
        total[...] += part

    @pl.when(step == pl.num_programs(0) - 1)
    def _():
        pack_rows(total[...], dnormed_ref)


def tail_kernel(pairs, parts, blocks, hidden_ref, down_ref, turned_ref, rows_ref, grads_ref, packed_ref, turned, total):
    step = pl.program_id(0)

    @pl.when(step < blocks)
    def _():
        act = hidden_ref[0]
        grads_ref[...] = dot(turned_ref[...], act).astype(BF)
        part = dot(act, down_ref[...])

        @pl.when(step == 0)
        def _():
            total[...] = part

        @pl.when(step > 0)
        def _():
            total[...] += part

    @pl.when(step == blocks)
    def _():
        pack_rows(total[...], packed_ref)
        turn_rows(pairs, parts, rows_ref, turned)

    @pl.when(step >= blocks)
    def _():
        grads_ref[...] = dot(turned[...], hidden_ref[0]).astype(BF)


def dattended_kernel(parts, me_ref, place_ref, back_ref, attended_ref, cot_ref, *refs):
    outs, full = refs[:parts], refs[parts]
    me = me_ref[0]
    low, high = read_tiles(back_ref)
    grad_unit = unpack_tokens(joint_place(place_ref), low, high)
    attended = attended_ref[...].astype(F32)
    inverse_rms = inverse_rms_of(attended)
    unit = attended * inverse_rms
    grad = cot_ref[...].astype(F32) + inverse_rms * (
        grad_unit - unit * jnp.mean(grad_unit * unit, axis=-1, keepdims=True)
    )
    full[...] = grad.astype(BF)
    width = outs[0].shape[1]
    for step in range(parts):
        outs[step][...] = full[:, lane_block(me, step, parts, width)]


def mix_kernel(place_ref, back_ref, attended_ref, gates_ref, out_ref):
    low, high = read_tiles(back_ref)
    mix = None
    for j in range(TOP):
        place = [place_ref[j, i] for i in range(3)]
        term = column(gates_ref[j:j + 1, :]) * unpack_tokens(place, low, high)
        mix = term if mix is None else mix + term
    out_ref[...] = (attended_ref[...].astype(F32) + mix).astype(BF)


def widen_kernel(sums_ref, up_out, down_out):
    hidden = up_out.shape[1]
    down_out[...] = sums_ref[:, 0:hidden].astype(F32).T
    up_out[...] = sums_ref[:, hidden:].astype(F32)


def shards(query, key, value, routes, gates, up, down, cotangent):
    tokens, model = query.shape[1:]
    owners = lax.axis_size("expert")
    parts = lax.axis_size("seq")
    pairs = lax.axis_size("dp")
    capacity = tokens * TOP * 3 // (2 * owners)
    slots = owners * capacity
    hidden = up.shape[2]
    width = model // parts
    length = tokens * parts
    heads = width // DH
    up, down = up[0], down[0]
    cot = cotangent[0]
    route, gate = routes[0].T, gates[0].T
    me = jnp.reshape(lax.axis_index("seq"), (1,)).astype(jnp.int32)

    def shift(piece, step):
        pairs_of = [(i, (i + step) % parts) for i in range(parts)]
        return lax.ppermute(piece, "seq", pairs_of)

    def swap(packed):
        return lax.all_to_all(packed, "expert", split_axis=0, concat_axis=0, tiled=True)

    order = (2, 1, 3) if parts == 4 else tuple(range(1, parts))

    def exchange(pieces, sign):
        moved = {step: shift(pieces[step], sign * step) for step in order}
        return [pieces[0]] + [moved[step] for step in range(1, parts)]

    triple = sds((3 * tokens, width), BF)
    single = sds((tokens, width), BF)
    wire = sds((owners, capacity * model // 128, 128), BF)
    sent = pl.pallas_call(
        functools.partial(split_kernel, parts),
        out_shape=[triple] * parts,
        in_specs=[SMEM] + [VMEM] * 3,
        out_specs=[VMEM] * parts,
        name="split_qkv",
    )(me, query[0], key[0], value[0])
    pieces = exchange(sent, 1)

    cot_late, _ = lax.optimization_barrier((cot, sent[0]))
    place, packed_grads = pl.pallas_call(
        functools.partial(place_kernel, owners),
        out_shape=[sds((TOP, 3, owners * 8, tokens), BF), wire],
        in_specs=[VMEM] * 3,
        out_specs=[VMEM] * 2,
        name="place",
    )(route, gate, cot_late)
    grad_wire = swap(packed_grads)

    attended_pieces = pl.pallas_call(
        functools.partial(attend_kernel, parts),
        out_shape=[single] * parts + [sds((heads, length, length), F32)],
        in_specs=[VMEM] * parts,
        out_specs=[VMEM] * (parts + 1),
        scratch_shapes=[pltpu.VMEM((length, width), BF)] * 2,
        compiler_params=BIG,
        name="attend",
    )(*pieces)
    probs = attended_pieces[parts]
    attended_pieces = exchange(attended_pieces[:parts], -1)

    attended, packed = pl.pallas_call(
        functools.partial(norm_kernel, parts),
        out_shape=[sds((tokens, model), BF), wire],
        in_specs=[SMEM] + [VMEM] * (parts + 1),
        out_specs=[VMEM] * 2,
        name="norm_pack",
    )(me, place, *attended_pieces)
    wire_rows = swap(packed)

    blocks = 4
    chunk = hidden // blocks
    whole_wire = pl.BlockSpec(wire.shape, lambda i: (0, 0, 0))
    dact, turned = pl.pallas_call(
        functools.partial(dact_kernel, pairs, parts),
        grid=(blocks,),
        out_shape=[sds((slots, hidden), F32), sds((model, slots), BF)],
        in_specs=[whole_wire, pl.BlockSpec((chunk, model), lambda i: (i, 0))],
        out_specs=[
            pl.BlockSpec((slots, chunk), lambda i: (0, i)),
            pl.BlockSpec((model, slots), lambda i: (0, 0)),
        ],
        scratch_shapes=[pltpu.VMEM((slots, model), BF)],
        compiler_params=BIG,
        name="dact",
    )(grad_wire, down)
    both, rows, dnormed = pl.pallas_call(
        expert_kernel,
        grid=(blocks,),
        out_shape=[sds((2, slots, hidden), BF), sds((slots, model), BF), wire],
        in_specs=[
            whole_wire,
            pl.BlockSpec((model, chunk), lambda i: (0, i)),
            pl.BlockSpec((slots, chunk), lambda i: (0, i)),
        ],
        out_specs=[
            pl.BlockSpec((2, slots, chunk), lambda i: (0, 0, i)),
            pl.BlockSpec((slots, model), lambda i: (0, 0)),
            whole_wire,
        ],
        scratch_shapes=[pltpu.VMEM((slots, model), F32)],
        compiler_params=BIG,
        name="expert",
    )(wire_rows, up, dact)
    dnormed_back = swap(dnormed)

    partial_grads, produced = pl.pallas_call(
        functools.partial(tail_kernel, pairs, parts, blocks),
        grid=(2 * blocks,),
        out_shape=[sds((model, 2 * hidden), BF), wire],
        in_specs=[
            pl.BlockSpec((1, slots, chunk), lambda i: (lax.div(i, blocks), 0, lax.rem(i, blocks))),
            pl.BlockSpec((chunk, model), lambda i: (jnp.minimum(i, blocks - 1), 0)),
            pl.BlockSpec((model, slots), lambda i: (0, 0)),
            pl.BlockSpec((slots, model), lambda i: (0, 0)),
        ],
        out_specs=[pl.BlockSpec((model, chunk), lambda i: (0, i)), whole_wire],
        scratch_shapes=[pltpu.VMEM((model, slots), BF), pltpu.VMEM((slots, model), F32)],
        compiler_params=BIG,
        name="weight_grads",
    )(both, down, turned, rows)
    sums = lax.psum_scatter(partial_grads, ("seq", "dp"), scatter_dimension=0, tiled=True)

    grad_pieces = pl.pallas_call(
        functools.partial(dattended_kernel, parts),
        out_shape=[single] * parts,
        in_specs=[SMEM] + [VMEM] * 4,
        out_specs=[VMEM] * parts,
        scratch_shapes=[pltpu.VMEM((tokens, model), BF)],
        cost_estimate=HEAVY,
        name="dattended",
    )(me, place, dnormed_back, attended, cot)
    grad_pieces = exchange(grad_pieces, 1)

    produced, _ = lax.optimization_barrier((produced, dnormed_back))
    produced_back = swap(produced)

    back_pieces = pl.pallas_call(
        functools.partial(attend_back_kernel, parts),
        out_shape=[triple] * parts,
        in_specs=[VMEM] * (2 * parts + 1),
        out_specs=[VMEM] * parts,
        scratch_shapes=[pltpu.VMEM((length, width), BF)] * 2
        + [pltpu.VMEM((length, width), F32)] * 2,
        compiler_params=BIG,
        name="attend_back",
    )(*pieces, *grad_pieces, probs)
    back_pieces = exchange(back_pieces, -1)

    layer_output = pl.pallas_call(
        mix_kernel,
        out_shape=sds((tokens, model), BF),
        in_specs=[VMEM] * 4,
        out_specs=VMEM,
        name="mix",
    )(place, produced_back, attended, gate)
    grad_queries, grad_keys, grad_values = pl.pallas_call(
        functools.partial(join_kernel, parts),
        out_shape=[sds((tokens, model), BF)] * 3,
        in_specs=[SMEM] + [VMEM] * parts,
        out_specs=[VMEM] * 3,
        name="join_grads",
    )(me, *back_pieces)
    band = model // (pairs * parts)
    grad_up, grad_down = pl.pallas_call(
        widen_kernel,
        out_shape=[sds((band, hidden), F32), sds((hidden, band), F32)],
        in_specs=[VMEM],
        out_specs=[VMEM] * 2,
        name="widen",
    )(sums)
    return (
        layer_output[None],
        grad_queries[None],
        grad_keys[None],
        grad_values[None],
        grad_up[None],
        grad_down[None],
    )


def solution(mesh):
    rows = P(("dp", "expert"), "seq", None)
    weight = P("expert", None, None)
    return jax.shard_map(
        shards,
        mesh=mesh,
        in_specs=(rows, rows, rows, rows, rows, weight, weight, rows),
        out_specs=(rows, rows, rows, rows, P("expert", ("dp", "seq"), None), P("expert", None, ("dp", "seq"))),
        check_vma=False,
    )
```

time: 300 us -> 191 us (0.64)
  Pallas kernels: 0 us -> 58.2 us
  local copies, waits for them, and re-layouts: 59.2 us -> 4.16 us
  matrix products: 54.5 us -> 0 us
  waiting for transfers between devices: 97.8 us -> 60 us
  starting transfers between devices: 64.2 us -> 53.6 us
  other arithmetic: 7.13 us -> 0 us
    all_to_all x12 -> x4, waiting for transfers between devices: 97.8 us -> 16.4 us  [swap(): lax.all_to_all(packed, 'expert', split_axis=0, concat_axis=0, tiled=True)]
    pallas_call x0 -> x12, Pallas kernels: none -> 58.2 us  [the longest x1 12.8 us: shards(): pl.pallas_call(functools.partial(tail_kernel, pairs, parts, blocks), grid...]
    dot_general x15 -> x0, matrix products: 52.4 us -> none  [the longest x1 6.97 us: shards(): jnp.einsum('gxcd,xhd->gxch', grad_arrived, down_weight, preferred_element...]
    unnamed x28 -> x30, local copies, waits for them, and re-layouts: 35.9 us -> 4.16 us
    ppermute x0 -> x12, waiting for transfers between devices: none -> 27.7 us  [shift(): return lax.ppermute(piece, 'seq', pairs_of)]
    all_to_all x12 -> x4, starting transfers between devices: 63.7 us -> 36.8 us  [swap(): lax.all_to_all(packed, 'expert', split_axis=0, concat_axis=0, tiled=True)]
    ppermute x0 -> x12, starting transfers between devices: none -> 16.6 us  [shift(): return lax.ppermute(piece, 'seq', pairs_of)]
    reduce_scatter x1, waiting for transfers between devices: 0.01 us -> 15.9 us  [shards(): lax.psum_scatter(partial_grads, ('seq', 'dp'), scatter_dimension=0, tiled...]
  transfers between devices with their start and end apart: 14 -> 17, of which waited for: 12 -> 14; matrix products, arithmetic and copies ran while one was open for 23% -> 0% of each run, Pallas kernels for 0% -> 21%
where the time goes in v1:
time: 191 us; the launch traced here: 190 us
  waiting for transfers between devices  60 us (31%)
  Pallas kernels  58.2 us (30%)
  starting transfers between devices  53.6 us (28%)
  between operations  14.1 us (7%)
  local copies, waits for them, and re-layouts  4.16 us (2%)
    all_to_all x4, starting transfers between devices, swap(): lax.all_to_all(packed, 'expert', split_axis=0, concat_axis=0, tiled=True)  36.8 us
    ppermute x12, waiting for transfers between devices, shift(): return lax.ppermute(piece, 'seq', pairs_of)  27.7 us
    ppermute x12, starting transfers between devices, shift(): return lax.ppermute(piece, 'seq', pairs_of)  16.6 us
    all_to_all x4, waiting for transfers between devices, swap(): lax.all_to_all(packed, 'expert', split_axis=0, concat_axis=0, tiled=True)  16.4 us
    reduce_scatter x1, waiting for transfers between devices, shards(): lax.psum_scatter(partial_grads, ('seq', 'dp'), scatter_dimension=0, tiled...  15.9 us
    pallas_call x1, Pallas kernels, shards(): pl.pallas_call(functools.partial(tail_kernel, pairs, parts, blocks), grid...  12.8 us
    pallas_call x1, Pallas kernels, shards(): pl.pallas_call(expert_kernel, grid=(blocks,), out_shape=[sds((2, slots, h...  10.1 us
    pallas_call x1, Pallas kernels, shards(): pl.pallas_call(functools.partial(dact_kernel, pairs, parts), grid=(blocks...  6.2 us
  transfers between devices with their start and end apart: 17, of which 14 were waited for; matrix products, arithmetic and copies ran while one was open for 0% of the time, Pallas kernels for 21%

profile of v1, /device:TPU:2, one launch (start us, length us, event | category | flops | bytes accessed | tf_op | source)
XLA Modules:
  0.0 190.0 jit_solution(3642362361163739434)
XLA Ops:
  9.3 2.8 %place.1 = (bf16[2,3,256,128]{3,2,1,0:T(8,128)(2,1)}, bf16[32,96,128]{2,1,0:T(8,128)(2,1)}) custom-call(s32[2,128]{1,0:T(2,128)} %bitcast.30, f32[2,128]{1,0:T(2,128)} %bitcast.28, bf16[128,1024]{1,0:T(8,128)(2,1)} %bitcast.22), custom_call_target="tpu_custom_call" | custom-call | tf_op jit(solution)/shard_map/place/pallas_call | solution.py:404
  12.1 11.6 %all-to-all-start.1 = ((bf16[32,96,128]{2,1,0:T(8,128)(2,1)}), bf16[32,96,128]{2,1,0:T(8,128)(2,1)S(1)}, u32[]{:S(2)}, u32[]{:S(2)}) async-start(bf16[32,96,128]{2,1,0:T(8,128)(2,1)} %get-tuple-element.52), calls=%async_computation.1 | async-start | bytes 1572864 | tf_op jit(solution)/shard_map/all_to_all | solution.py:383
  25.4 2.9 %collective-permute-start.1 = (bf16[384,256]{1,0:T(8,128)(2,1)}, bf16[384,256]{1,0:T(8,128)(2,1)S(1)}, u32[]{:S(2)}, u32[]{:S(2)}) collective-permute-start(bf16[384,256]{1,0:T(8,128)(2,1)} %get-tuple-element.45), channel_id=1, source_target_pairs={{0,64},{32,96},{64,0},{96,32},{1,65},{33,97},{65,1},{97,33},{2,66}... | collective-permute-start | bytes 589832 | tf_op jit(solution)/shard_map/ppermute | solution.py:380
  32.0 4.8 %collective-permute-done.1.refs_2_ = bf16[384,256]{1,0:T(8,128)(2,1)S(1)} collective-permute-done((bf16[384,256]{1,0:T(8,128)(2,1)}, bf16[384,256]{1,0:T(8,128)(2,1)S(1)}, u32[]{:S(2)}, u32[]{:S(2)}) %collective-permute-start.1) | collective-permute-done | bytes 196640 | tf_op jit(solution)/shard_map/ppermute | solution.py:380
  38.1 5.5 %attend.1 = (bf16[128,256]{1,0:T(8,128)(2,1)}, bf16[128,256]{1,0:T(8,128)(2,1)}, bf16[128,256]{1,0:T(8,128)(2,1)}, bf16[128,256]{1,0:T(8,128)(2,1)}, f32[2,512,512]{2,1,0:T(8,128)}) custom-call(bf16[384,256]{1,0:T(8,128)(2,1)} %get-tuple-element.41.refs_0_, bf16[384,256]{1,0:T(8,128)(2,1)} %copy-done.3, bf16[384,256]{1,0:T(8,128)(2,1)} %copy-done.4, ...), custom_call_target="tpu_custom_call" | custom-call | tf_op jit(solution)/shard_map/attend/pallas_call | solution.py:413
  48.1 3.0 %collective-permute-done.4.refs_2_ = bf16[128,256]{1,0:T(8,128)(2,1)S(1)} collective-permute-done((bf16[128,256]{1,0:T(8,128)(2,1)}, bf16[128,256]{1,0:T(8,128)(2,1)S(1)}, u32[]{:S(2)}, u32[]{:S(2)}) %collective-permute-start.4) | collective-permute-done | bytes 65568 | tf_op jit(solution)/shard_map/ppermute | solution.py:380
  52.6 2.6 %norm_pack.1 = (bf16[128,1024]{1,0:T(8,128)(2,1)}, bf16[32,96,128]{2,1,0:T(8,128)(2,1)}) custom-call(s32[1]{0:T(128)} %bitcast.5.me_ref, bf16[2,3,256,128]{3,2,1,0:T(8,128)(2,1)} %get-tuple-element.43.place_ref, bf16[128,256]{1,0:T(8,128)(2,1)} %get-tuple-element.47.refs_0_, bf16[128,256]{1,0:T(8,128)(2,1)} %copy-done.12, bf16[128,256]{1,0:T(8,128)(2,1)} %copy-done.13, ...), custom_call_target="tpu_custom_call" | custom-call | tf_op jit(solution)/shard_map/norm_pack/pallas_call | solution.py:425
  55.2 9.8 %all-to-all-start = ((bf16[32,96,128]{2,1,0:T(8,128)(2,1)}), bf16[32,96,128]{2,1,0:T(8,128)(2,1)S(1)}, u32[]{:S(2)}, u32[]{:S(2)}) async-start(bf16[32,96,128]{2,1,0:T(8,128)(2,1)} %get-tuple-element.51), calls=%async_computation | async-start | bytes 1572864 | tf_op jit(solution)/shard_map/all_to_all | solution.py:383
  65.0 6.2 %dact.1 = (f32[384,2048]{1,0:T(8,128)}, bf16[1024,384]{1,0:T(8,128)(2,1)}) custom-call(bf16[32,96,128]{2,1,0:T(8,128)(2,1)} %copy-done, bf16[2048,1024]{1,0:T(8,128)(2,1)} %bitcast.19), custom_call_target="tpu_custom_call" | custom-call | tf_op jit(solution)/shard_map/dact/pallas_call | solution.py:437
  71.2 11.9 %all-to-all-done.packed_ref = bf16[32,96,128]{2,1,0:T(8,128)(2,1)S(1)} async-done(((bf16[32,96,128]{2,1,0:T(8,128)(2,1)}), bf16[32,96,128]{2,1,0:T(8,128)(2,1)S(1)}, u32[]{:S(2)}, u32[]{:S(2)}) %all-to-all-start) | async-done | bytes 786464 | tf_op jit(solution)/shard_map/all_to_all | solution.py:383
  83.9 10.1 %expert.1 = (bf16[2,384,2048]{2,1,0:T(8,128)(2,1)}, bf16[384,1024]{1,0:T(8,128)(2,1)}, bf16[32,96,128]{2,1,0:T(8,128)(2,1)}) custom-call(bf16[32,96,128]{2,1,0:T(8,128)(2,1)} %copy-done.1, bf16[1024,2048]{1,0:T(8,128)(2,1)} %bitcast.21, f32[384,2048]{1,0:T(8,128)} %get-tuple-element.53.dact_ref), custom_call_target="tpu_custom_call" | custom-call | tf_op jit(solution)/shard_map/expert/pallas_call | solution.py:450
  94.0 7.7 %all-to-all-start.2 = ((bf16[32,96,128]{2,1,0:T(8,128)(2,1)}), bf16[32,96,128]{2,1,0:T(8,128)(2,1)S(1)}, u32[]{:S(2)}, u32[]{:S(2)}) async-start(bf16[32,96,128]{2,1,0:T(8,128)(2,1)} %get-tuple-element.58), calls=%async_computation.2 | async-start | bytes 1572864 | tf_op jit(solution)/shard_map/all_to_all | solution.py:383
  102.0 12.8 %weight_grads.1 = (bf16[1024,4096]{1,0:T(8,128)(2,1)}, bf16[32,96,128]{2,1,0:T(8,128)(2,1)}) custom-call(bf16[2,384,2048]{2,1,0:T(8,128)(2,1)} %get-tuple-element.54.hidden_ref, bf16[2048,1024]{1,0:T(8,128)(2,1)} %bitcast.20, bf16[1024,384]{1,0:T(8,128)(2,1)} %get-tuple-element.55.turned_ref, bf16[384,1024]{1,0:T(8,128)(2,1)} %get-tuple-element.56.rows_ref), custom_call_target="tpu_custom_call" | custom-call | tf_op jit(solution)/shard_map/weight_grads/pallas_call | solution.py:470
  114.8 4.5 %all-to-all-done.2.back_ref = bf16[32,96,128]{2,1,0:T(8,128)(2,1)S(1)} async-done(((bf16[32,96,128]{2,1,0:T(8,128)(2,1)}), bf16[32,96,128]{2,1,0:T(8,128)(2,1)S(1)}, u32[]{:S(2)}, u32[]{:S(2)}) %all-to-all-start.2) | async-done | bytes 786464 | tf_op jit(solution)/shard_map/all_to_all | solution.py:383
  119.3 7.7 %all-to-all-start.3 = ((bf16[32,96,128]{2,1,0:T(8,128)(2,1)}), bf16[32,96,128]{2,1,0:T(8,128)(2,1)}, u32[]{:S(2)}, u32[]{:S(2)}) async-start(bf16[32,96,128]{2,1,0:T(8,128)(2,1)} %get-tuple-element.59), calls=%async_computation.3 | async-start | bytes 1572864 | tf_op jit(solution)/shard_map/all_to_all | solution.py:383
  127.0 2.6 %dattended.1 = (bf16[128,256]{1,0:T(8,128)(2,1)}, bf16[128,256]{1,0:T(8,128)(2,1)}, bf16[128,256]{1,0:T(8,128)(2,1)}, bf16[128,256]{1,0:T(8,128)(2,1)}) custom-call(s32[1]{0:T(128)} %bitcast.5.me_ref, bf16[2,3,256,128]{3,2,1,0:T(8,128)(2,1)} %get-tuple-element.43.place_ref, bf16[32,96,128]{2,1,0:T(8,128)(2,1)} %copy-done.2, ...), custom_call_target="tpu_custom_call" | custom-call | flops 999999995904 | bytes 1000000 | tf_op jit(solution)/shard_map/dattended/pallas_call | solution.py:487
  129.9 2.3 %collective-permute-start.7 = (bf16[128,256]{1,0:T(8,128)(2,1)}, bf16[128,256]{1,0:T(8,128)(2,1)S(1)}, u32[]{:S(2)}, u32[]{:S(2)}) collective-permute-start(bf16[128,256]{1,0:T(8,128)(2,1)} %get-tuple-element.63), channel_id=1, source_target_pairs={{0,64},{32,96},{64,0},{96,32},{1,65},{33,97},{65,1},{97,33},{2,66}... | collective-permute-start | bytes 196616 | tf_op jit(solution)/shard_map/ppermute | solution.py:380
  133.8 2.8 %collective-permute-done.6.refs_5_ = bf16[128,256]{1,0:T(8,128)(2,1)S(1)} collective-permute-done((bf16[128,256]{1,0:T(8,128)(2,1)}, bf16[128,256]{1,0:T(8,128)(2,1)S(1)}, u32[]{:S(2)}, u32[]{:S(2)}) %collective-permute-start.6) | collective-permute-done | bytes 65568 | tf_op jit(solution)/shard_map/ppermute | solution.py:380
  138.9 6.0 %attend_back.1 = (bf16[384,256]{1,0:T(8,128)(2,1)}, bf16[384,256]{1,0:T(8,128)(2,1)}, bf16[384,256]{1,0:T(8,128)(2,1)}, bf16[384,256]{1,0:T(8,128)(2,1)}) custom-call(bf16[384,256]{1,0:T(8,128)(2,1)} %get-tuple-element.41.refs_0_, bf16[384,256]{1,0:T(8,128)(2,1)} %copy-done.3, bf16[384,256]{1,0:T(8,128)(2,1)} %copy-done.4, bf16[384,256]{1,0:T(8,128)(2,1)} %copy-done.5, ...), custom_call_target="tpu_custom_call" | custom-call | tf_op jit(solution)/shard_map/attend_back/pallas_call | solution.py:501
  148.0 5.9 %collective-permute-done.9.refs_1_ = bf16[384,256]{1,0:T(8,128)(2,1)S(1)} collective-permute-done((bf16[384,256]{1,0:T(8,128)(2,1)}, bf16[384,256]{1,0:T(8,128)(2,1)S(1)}, u32[]{:S(2)}, u32[]{:S(2)}) %collective-permute-start.9) | collective-permute-done | bytes 196640 | tf_op jit(solution)/shard_map/ppermute | solution.py:380
  153.9 3.5 %collective-permute-done.10.refs_2_ = bf16[384,256]{1,0:T(8,128)(2,1)S(1)} collective-permute-done((bf16[384,256]{1,0:T(8,128)(2,1)}, bf16[384,256]{1,0:T(8,128)(2,1)S(1)}, u32[]{:S(2)}, u32[]{:S(2)}) %collective-permute-start.10) | collective-permute-done | bytes 196640 | tf_op jit(solution)/shard_map/ppermute | solution.py:380
  162.0 2.5 %mix.1 = bf16[128,1024]{1,0:T(8,128)(2,1)} custom-call(bf16[2,3,256,128]{3,2,1,0:T(8,128)(2,1)} %get-tuple-element.43.place_ref, bf16[32,96,128]{2,1,0:T(8,128)(2,1)} %all-to-all-done.3.back_ref, bf16[128,1024]{1,0:T(8,128)(2,1)} %get-tuple-element.60.attended_ref, f32[2,128]{1,0:T(2,128)} %bitcast.29), custom_call_target="tpu_custom_call" | custom-call | tf_op jit(solution)/shard_map/mix/pallas_call | solution.py:513
  164.5 15.9 %reduce-scatter.2.cloned.1.call-done.sums_ref = bf16[128,4096]{1,0:T(8,128)(2,1)} async-done(((bf16[1024,4096]{1,0:T(8,128)(2,1)}), bf16[128,4096]{1,0:T(8,128)(2,1)}) %reduce-scatter.2.cloned.1.call-update) | async-done | bytes 1048592 | tf_op jit(solution)/shard_map/reduce_scatter | solution.py:485
  180.4 2.8 %widen.1 = (f32[128,2048]{1,0:T(8,128)}, f32[2048,128]{1,0:T(8,128)}) custom-call(bf16[128,4096]{1,0:T(8,128)(2,1)} %reduce-scatter.2.cloned.1.call-done.sums_ref), custom_call_target="tpu_custom_call" | custom-call | tf_op jit(solution)/shard_map/widen/pallas_call | solution.py:528
  (53 shorter events, 27.7 us)
Async XLA Ops:
  12.1 43.1 %all-to-all-start.1 = ((bf16[32,96,128]{2,1,0:T(8,128)(2,1)}), bf16[32,96,128]{2,1,0:T(8,128)(2,1)S(1)}, u32[]{:S(2)}, u32[]{:S(2)}) async-start(bf16[32,96,128]{2,1,0:T(8,128)(2,1)} %get-tuple-element.52), calls=%async_computation.1 | async-start | bytes 1572864 | tf_op jit(solution)/shard_map/all_to_all | solution.py:383
  23.7 8.2 %collective-permute-start = (bf16[384,256]{1,0:T(8,128)(2,1)}, bf16[384,256]{1,0:T(8,128)(2,1)S(1)}, u32[]{:S(2)}, u32[]{:S(2)}) collective-permute-start(bf16[384,256]{1,0:T(8,128)(2,1)} %get-tuple-element.44), channel_id=1, source_target_pairs={{0,32},{32,64},{64,96},{96,0},{1,33},{33,65},{65,97},{97,1},{2,34}... | collective-permute-start | bytes 589832 | tf_op jit(solution)/shard_map/ppermute | solution.py:380
  25.4 11.4 %collective-permute-start.1 = (bf16[384,256]{1,0:T(8,128)(2,1)}, bf16[384,256]{1,0:T(8,128)(2,1)S(1)}, u32[]{:S(2)}, u32[]{:S(2)}) collective-permute-start(bf16[384,256]{1,0:T(8,128)(2,1)} %get-tuple-element.45), channel_id=1, source_target_pairs={{0,64},{32,96},{64,0},{96,32},{1,65},{33,97},{65,1},{97,33},{2,66}... | collective-permute-start | bytes 589832 | tf_op jit(solution)/shard_map/ppermute | solution.py:380
  28.3 8.5 %collective-permute-start.2 = (bf16[384,256]{1,0:T(8,128)(2,1)}, bf16[384,256]{1,0:T(8,128)(2,1)S(1)}, u32[]{:S(2)}, u32[]{:S(2)}) collective-permute-start(bf16[384,256]{1,0:T(8,128)(2,1)} %get-tuple-element.46), channel_id=1, source_target_pairs={{0,96},{32,0},{64,32},{96,64},{1,97},{33,1},{65,33},{97,65},{2,98}... | collective-permute-start | bytes 589832 | tf_op jit(solution)/shard_map/ppermute | solution.py:380
  32.0 4.8 %copy-start.3 = (bf16[384,256]{1,0:T(8,128)(2,1)}, bf16[384,256]{1,0:T(8,128)(2,1)S(1)}, u32[]{:S(2)}) copy-start(bf16[384,256]{1,0:T(8,128)(2,1)S(1)} %collective-permute-done.refs_1_) | copy-start | bytes 589828
  43.6 4.5 %collective-permute-start.3 = (bf16[128,256]{1,0:T(8,128)(2,1)}, bf16[128,256]{1,0:T(8,128)(2,1)S(1)}, u32[]{:S(2)}, u32[]{:S(2)}) collective-permute-start(bf16[128,256]{1,0:T(8,128)(2,1)} %get-tuple-element.48), channel_id=1, source_target_pairs={{0,96},{32,0},{64,32},{96,64},{1,97},{33,1},{65,33},{97,65},{2,98}... | collective-permute-start | bytes 196616 | tf_op jit(solution)/shard_map/ppermute | solution.py:380
  45.2 6.0 %collective-permute-start.4 = (bf16[128,256]{1,0:T(8,128)(2,1)}, bf16[128,256]{1,0:T(8,128)(2,1)S(1)}, u32[]{:S(2)}, u32[]{:S(2)}) collective-permute-start(bf16[128,256]{1,0:T(8,128)(2,1)} %get-tuple-element.49), channel_id=1, source_target_pairs={{0,64},{32,96},{64,0},{96,32},{1,65},{33,97},{65,1},{97,33},{2,66}... | collective-permute-start | bytes 196616 | tf_op jit(solution)/shard_map/ppermute | solution.py:380
  46.3 5.7 %collective-permute-start.5 = (bf16[128,256]{1,0:T(8,128)(2,1)}, bf16[128,256]{1,0:T(8,128)(2,1)S(1)}, u32[]{:S(2)}, u32[]{:S(2)}) collective-permute-start(bf16[128,256]{1,0:T(8,128)(2,1)} %get-tuple-element.50), channel_id=1, source_target_pairs={{0,32},{32,64},{64,96},{96,0},{1,33},{33,65},{65,97},{97,1},{2,34}... | collective-permute-start | bytes 196616 | tf_op jit(solution)/shard_map/ppermute | solution.py:380
  48.1 3.9 %copy-start.12 = (bf16[128,256]{1,0:T(8,128)(2,1)}, bf16[128,256]{1,0:T(8,128)(2,1)S(1)}, u32[]{:S(2)}) copy-start(bf16[128,256]{1,0:T(8,128)(2,1)S(1)} %collective-permute-done.3.refs_1_) | copy-start | bytes 196612
  55.2 9.8 %copy-start = (bf16[32,96,128]{2,1,0:T(8,128)(2,1)}, bf16[32,96,128]{2,1,0:T(8,128)(2,1)S(1)}, u32[]{:S(2)}) copy-start(bf16[32,96,128]{2,1,0:T(8,128)(2,1)S(1)} %all-to-all-done.1.packed_ref) | copy-start | bytes 2359300
  55.2 27.9 %all-to-all-start = ((bf16[32,96,128]{2,1,0:T(8,128)(2,1)}), bf16[32,96,128]{2,1,0:T(8,128)(2,1)S(1)}, u32[]{:S(2)}, u32[]{:S(2)}) async-start(bf16[32,96,128]{2,1,0:T(8,128)(2,1)} %get-tuple-element.51), calls=%async_computation | async-start | bytes 1572864 | tf_op jit(solution)/shard_map/all_to_all | solution.py:383
  94.0 25.2 %all-to-all-start.2 = ((bf16[32,96,128]{2,1,0:T(8,128)(2,1)}), bf16[32,96,128]{2,1,0:T(8,128)(2,1)S(1)}, u32[]{:S(2)}, u32[]{:S(2)}) async-start(bf16[32,96,128]{2,1,0:T(8,128)(2,1)} %get-tuple-element.58), calls=%async_computation.2 | async-start | bytes 1572864 | tf_op jit(solution)/shard_map/all_to_all | solution.py:383
  101.8 78.7 %reduce-scatter.2.cloned.1.call-start = ((), (), s32[]{:S(2)}) async-start(), calls=%async_computation.5 | async-start | bytes 9437184 | tf_op jit(solution)/shard_map/reduce_scatter | solution.py:485
  119.3 7.7 %copy-start.2 = (bf16[32,96,128]{2,1,0:T(8,128)(2,1)}, bf16[32,96,128]{2,1,0:T(8,128)(2,1)S(1)}, u32[]{:S(2)}) copy-start(bf16[32,96,128]{2,1,0:T(8,128)(2,1)S(1)} %all-to-all-done.2.back_ref) | copy-start | bytes 2359300
  119.3 42.7 %all-to-all-start.3 = ((bf16[32,96,128]{2,1,0:T(8,128)(2,1)}), bf16[32,96,128]{2,1,0:T(8,128)(2,1)}, u32[]{:S(2)}, u32[]{:S(2)}) async-start(bf16[32,96,128]{2,1,0:T(8,128)(2,1)} %get-tuple-element.59), calls=%async_computation.3 | async-start | bytes 1572864 | tf_op jit(solution)/shard_map/all_to_all | solution.py:383
  129.6 7.0 %collective-permute-start.6 = (bf16[128,256]{1,0:T(8,128)(2,1)}, bf16[128,256]{1,0:T(8,128)(2,1)S(1)}, u32[]{:S(2)}, u32[]{:S(2)}) collective-permute-start(bf16[128,256]{1,0:T(8,128)(2,1)} %get-tuple-element.62), channel_id=1, source_target_pairs={{0,32},{32,64},{64,96},{96,0},{1,33},{33,65},{65,97},{97,1},{2,34}... | collective-permute-start | bytes 196616 | tf_op jit(solution)/shard_map/ppermute | solution.py:380
  129.9 6.9 %collective-permute-start.7 = (bf16[128,256]{1,0:T(8,128)(2,1)}, bf16[128,256]{1,0:T(8,128)(2,1)S(1)}, u32[]{:S(2)}, u32[]{:S(2)}) collective-permute-start(bf16[128,256]{1,0:T(8,128)(2,1)} %get-tuple-element.63), channel_id=1, source_target_pairs={{0,64},{32,96},{64,0},{96,32},{1,65},{33,97},{65,1},{97,33},{2,66}... | collective-permute-start | bytes 196616 | tf_op jit(solution)/shard_map/ppermute | solution.py:380
  132.2 6.1 %collective-permute-start.8 = (bf16[128,256]{1,0:T(8,128)(2,1)}, bf16[128,256]{1,0:T(8,128)(2,1)S(1)}, u32[]{:S(2)}, u32[]{:S(2)}) collective-permute-start(bf16[128,256]{1,0:T(8,128)(2,1)} %get-tuple-element.64), channel_id=1, source_target_pairs={{0,96},{32,0},{64,32},{96,64},{1,97},{33,1},{65,33},{97,65},{2,98}... | collective-permute-start | bytes 196616 | tf_op jit(solution)/shard_map/ppermute | solution.py:380
  136.5 1.8 copy-start.9
  144.9 9.0 %collective-permute-start.9 = (bf16[384,256]{1,0:T(8,128)(2,1)}, bf16[384,256]{1,0:T(8,128)(2,1)S(1)}, u32[]{:S(2)}, u32[]{:S(2)}) collective-permute-start(bf16[384,256]{1,0:T(8,128)(2,1)} %get-tuple-element.67), channel_id=1, source_target_pairs={{0,96},{32,0},{64,32},{96,64},{1,97},{33,1},{65,33},{97,65},{2,98}... | collective-permute-start | bytes 589832 | tf_op jit(solution)/shard_map/ppermute | solution.py:380
  147.1 10.3 %collective-permute-start.10 = (bf16[384,256]{1,0:T(8,128)(2,1)}, bf16[384,256]{1,0:T(8,128)(2,1)S(1)}, u32[]{:S(2)}, u32[]{:S(2)}) collective-permute-start(bf16[384,256]{1,0:T(8,128)(2,1)} %get-tuple-element.68), channel_id=1, source_target_pairs={{0,64},{32,96},{64,0},{96,32},{1,65},{33,97},{65,1},{97,33},{2,66}... | collective-permute-start | bytes 589832 | tf_op jit(solution)/shard_map/ppermute | solution.py:380
  147.8 11.3 %collective-permute-start.11 = (bf16[384,256]{1,0:T(8,128)(2,1)}, bf16[384,256]{1,0:T(8,128)(2,1)S(1)}, u32[]{:S(2)}, u32[]{:S(2)}) collective-permute-start(bf16[384,256]{1,0:T(8,128)(2,1)} %get-tuple-element.69), channel_id=1, source_target_pairs={{0,32},{32,64},{64,96},{96,0},{1,33},{33,65},{65,97},{97,1},{2,34}... | collective-permute-start | bytes 589832 | tf_op jit(solution)/shard_map/ppermute | solution.py:380
  153.9 5.2 %copy-start.6 = (bf16[384,256]{1,0:T(8,128)(2,1)}, bf16[384,256]{1,0:T(8,128)(2,1)S(1)}, u32[]{:S(2)}) copy-start(bf16[384,256]{1,0:T(8,128)(2,1)S(1)} %collective-permute-done.9.refs_1_) | copy-start | bytes 589828
  157.4 1.7 copy-start.7
  (8 other events, 6.6 us)
Sparse Core Ops, SparseCore 0:
  114.9 65.4 reduce-scatter.1

commit v2 on v1

--- a/solution.py
+++ b/solution.py
@@ -20,6 +20,7 @@
 NT = (((1,), (1,)), ((), ()))
 TN = (((0,), (0,)), ((), ()))
 HEAVY = pl.CostEstimate(flops=1_000_000_000_000, transcendentals=0, bytes_accessed=1_000_000)
+MIDDLE = pl.CostEstimate(flops=40_000_000_000, transcendentals=0, bytes_accessed=1_000_000)
 BIG = pltpu.CompilerParams(vmem_limit_bytes=56 * 1024 * 1024)
 
 
@@ -29,6 +30,10 @@
 
 def sds(shape, dtype):
     return jax.ShapeDtypeStruct(shape, dtype)
+
+
+def near(array):
+    return pltpu.with_memory_space_constraint(array, pltpu.VMEM)
 
 
 def lane_block(me, step, parts, width):
@@ -262,29 +267,39 @@
     out_ref[...] = dot(rows[...], down_ref[...], NT)
 
 
-def expert_kernel(packed_ref, up_ref, dact_ref, hidden_ref, rows_ref, dnormed_ref, total):
+def hidden_kernel(packed_ref, up_ref, dact_ref, hidden_ref, rows_ref):
+    @pl.when(pl.program_id(0) == 0)
+    def _():
+        unpack_rows(packed_ref, rows_ref)
+
+    pre = dot(rows_ref[...], up_ref[...])
+    square = pre * pre
+    half = 0.5 + 0.5 * jnp.tanh(pre * (GELU_COEF + (GELU_COEF * 0.044715) * square))
+    act = pre * half
+    hidden_ref[0] = act.astype(BF)
+    slope = half + act * (1.0 - half) * (2.0 * GELU_COEF + (6.0 * GELU_COEF * 0.044715) * square)
+    hidden_ref[1] = (dact_ref[...] * slope).astype(BF)
+
+
+def weight_grad_kernel(pairs, parts, blocks, hidden_ref, turned_ref, rows_ref, grads_ref, turned):
     step = pl.program_id(0)
 
+    @pl.when(step < blocks)
+    def _():
+        grads_ref[...] = dot(turned_ref[...], hidden_ref[0]).astype(BF)
+
     @pl.when(step == 0)
     def _():
-        unpack_rows(packed_ref, rows_ref)
-
-    chunk = up_ref.shape[1]
-    part = None
-    for start in range(0, chunk, 256):
-        lanes = slice(start, start + 256)
-        weights = up_ref[:, lanes]
-        pre = dot(rows_ref[...], weights)
-        square = pre * pre
-        hyper = jnp.tanh(GELU_COEF * (pre + 0.044715 * pre * square))
-        hidden_ref[0, :, lanes] = (0.5 * pre * (1.0 + hyper)).astype(BF)
-        slope = 0.5 * (1.0 + hyper) + 0.5 * pre * (1.0 - hyper * hyper) * GELU_COEF * (
-            1.0 + 3.0 * 0.044715 * square
-        )
-        dpre = (dact_ref[:, lanes] * slope).astype(BF)
-        hidden_ref[1, :, lanes] = dpre
-        term = dot(dpre, weights, NT)
-        part = term if part is None else part + term
+        turn_rows(pairs, parts, rows_ref, turned)
+
+    @pl.when(step >= blocks)
+    def _():
+        grads_ref[...] = dot(turned[...], hidden_ref[0]).astype(BF)
+
+
+def project_kernel(dims, hidden_ref, weight_ref, packed_ref, total):
+    step = pl.program_id(0)
+    part = dot(hidden_ref[0], weight_ref[...], dims)
 
     @pl.when(step == 0)
     def _():
@@ -296,34 +311,7 @@
 
     @pl.when(step == pl.num_programs(0) - 1)
     def _():
-        pack_rows(total[...], dnormed_ref)
-
-
-def tail_kernel(pairs, parts, blocks, hidden_ref, down_ref, turned_ref, rows_ref, grads_ref, packed_ref, turned, total):
-    step = pl.program_id(0)
-
-    @pl.when(step < blocks)
-    def _():
-        act = hidden_ref[0]
-        grads_ref[...] = dot(turned_ref[...], act).astype(BF)
-        part = dot(act, down_ref[...])
-
-        @pl.when(step == 0)
-        def _():
-            total[...] = part
-
-        @pl.when(step > 0)
-        def _():
-            total[...] += part
-
-    @pl.when(step == blocks)
-    def _():
         pack_rows(total[...], packed_ref)
-        turn_rows(pairs, parts, rows_ref, turned)
-
-    @pl.when(step >= blocks)
-    def _():
-        grads_ref[...] = dot(turned[...], hidden_ref[0]).astype(BF)
 
 
 def dattended_kernel(parts, me_ref, place_ref, back_ref, attended_ref, cot_ref, *refs):
@@ -377,10 +365,10 @@
 
     def shift(piece, step):
         pairs_of = [(i, (i + step) % parts) for i in range(parts)]
-        return lax.ppermute(piece, "seq", pairs_of)
+        return near(lax.ppermute(piece, "seq", pairs_of))
 
     def swap(packed):
-        return lax.all_to_all(packed, "expert", split_axis=0, concat_axis=0, tiled=True)
+        return near(lax.all_to_all(packed, "expert", split_axis=0, concat_axis=0, tiled=True))
 
     order = (2, 1, 3) if parts == 4 else tuple(range(1, parts))
 
@@ -417,6 +405,7 @@
         out_specs=[VMEM] * (parts + 1),
         scratch_shapes=[pltpu.VMEM((length, width), BF)] * 2,
         compiler_params=BIG,
+        cost_estimate=HEAVY,
         name="attend",
     )(*pieces)
     probs = attended_pieces[parts]
@@ -438,7 +427,7 @@
         functools.partial(dact_kernel, pairs, parts),
         grid=(blocks,),
         out_shape=[sds((slots, hidden), F32), sds((model, slots), BF)],
-        in_specs=[whole_wire, pl.BlockSpec((chunk, model), lambda i: (i, 0))],
+        in_specs=[VMEM, pl.BlockSpec((chunk, model), lambda i: (i, 0))],
         out_specs=[
             pl.BlockSpec((slots, chunk), lambda i: (0, i)),
             pl.BlockSpec((model, slots), lambda i: (0, 0)),
@@ -447,55 +436,74 @@
         compiler_params=BIG,
         name="dact",
     )(grad_wire, down)
-    both, rows, dnormed = pl.pallas_call(
-        expert_kernel,
+    both, rows = pl.pallas_call(
+        hidden_kernel,
         grid=(blocks,),
-        out_shape=[sds((2, slots, hidden), BF), sds((slots, model), BF), wire],
+        out_shape=[sds((2, slots, hidden), BF), sds((slots, model), BF)],
         in_specs=[
-            whole_wire,
+            VMEM,
             pl.BlockSpec((model, chunk), lambda i: (0, i)),
             pl.BlockSpec((slots, chunk), lambda i: (0, i)),
         ],
         out_specs=[
             pl.BlockSpec((2, slots, chunk), lambda i: (0, 0, i)),
             pl.BlockSpec((slots, model), lambda i: (0, 0)),
-            whole_wire,
         ],
-        scratch_shapes=[pltpu.VMEM((slots, model), F32)],
         compiler_params=BIG,
-        name="expert",
+        name="expert_hidden",
     )(wire_rows, up, dact)
-    dnormed_back = swap(dnormed)
-
-    partial_grads, produced = pl.pallas_call(
-        functools.partial(tail_kernel, pairs, parts, blocks),
-        grid=(2 * blocks,),
-        out_shape=[sds((model, 2 * hidden), BF), wire],
+
+    half = hidden // 2
+    partial_grads = pl.pallas_call(
+        functools.partial(weight_grad_kernel, pairs, parts, 2),
+        grid=(4,),
+        out_shape=sds((model, 2 * hidden), BF),
         in_specs=[
-            pl.BlockSpec((1, slots, chunk), lambda i: (lax.div(i, blocks), 0, lax.rem(i, blocks))),
-            pl.BlockSpec((chunk, model), lambda i: (jnp.minimum(i, blocks - 1), 0)),
+            pl.BlockSpec((1, slots, half), lambda i: (lax.div(i, 2), 0, lax.rem(i, 2))),
             pl.BlockSpec((model, slots), lambda i: (0, 0)),
             pl.BlockSpec((slots, model), lambda i: (0, 0)),
         ],
-        out_specs=[pl.BlockSpec((model, chunk), lambda i: (0, i)), whole_wire],
-        scratch_shapes=[pltpu.VMEM((model, slots), BF), pltpu.VMEM((slots, model), F32)],
+        out_specs=pl.BlockSpec((model, half), lambda i: (0, i)),
+        scratch_shapes=[pltpu.VMEM((model, slots), BF)],
         compiler_params=BIG,
         name="weight_grads",
-    )(both, down, turned, rows)
+    )(both, turned, rows)
     sums = lax.psum_scatter(partial_grads, ("seq", "dp"), scatter_dimension=0, tiled=True)
 
+    def project(source, which, weight, weight_spec, dims, cost, name):
+        return pl.pallas_call(
+            functools.partial(project_kernel, dims),
+            grid=(blocks,),
+            out_shape=wire,
+            in_specs=[pl.BlockSpec((1, slots, chunk), lambda i: (which, 0, i)), weight_spec],
+            out_specs=whole_wire,
+            scratch_shapes=[pltpu.VMEM((slots, model), F32)],
+            compiler_params=BIG,
+            cost_estimate=cost,
+            name=name,
+        )(source, weight)
+
+    both_late, _ = lax.optimization_barrier((both, partial_grads))
+    dnormed = project(
+        both_late, 1, up, pl.BlockSpec((model, chunk), lambda i: (0, i)), NT, HEAVY, "dnormed"
+    )
+    both_last, _ = lax.optimization_barrier((both_late, dnormed))
+    dnormed_back = swap(dnormed)
+    produced = project(
+        both_last, 0, down, pl.BlockSpec((chunk, model), lambda i: (i, 0)), NN, None, "expert_out"
+    )
+
+    dnormed_back, produced = lax.optimization_barrier((dnormed_back, produced))
     grad_pieces = pl.pallas_call(
         functools.partial(dattended_kernel, parts),
         out_shape=[single] * parts,
         in_specs=[SMEM] + [VMEM] * 4,
         out_specs=[VMEM] * parts,
         scratch_shapes=[pltpu.VMEM((tokens, model), BF)],
-        cost_estimate=HEAVY,
         name="dattended",
     )(me, place, dnormed_back, attended, cot)
     grad_pieces = exchange(grad_pieces, 1)
 
-    produced, _ = lax.optimization_barrier((produced, dnormed_back))
     produced_back = swap(produced)
 
     back_pieces = pl.pallas_call(
@@ -506,6 +514,7 @@
         scratch_shapes=[pltpu.VMEM((length, width), BF)] * 2
         + [pltpu.VMEM((length, width), F32)] * 2,
         compiler_params=BIG,
+        cost_estimate=MIDDLE,
         name="attend_back",
     )(*pieces, *grad_pieces, probs)
     back_pieces = exchange(back_pieces, -1)

time: 191 us -> 174 us (0.911); the launches traced: 190 us -> 170 us
  waiting for transfers between devices: 60 us -> 42.9 us
  Pallas kernels: 58.2 us -> 62.8 us
  local copies, waits for them, and re-layouts: 4.16 us -> 0.04 us
  starting transfers between devices: 53.6 us -> 50.4 us
    reduce_scatter x1, waiting for transfers between devices: 15.9 us -> 0.01 us  [shards(): lax.psum_scatter(partial_grads, ('seq', 'dp'), scatter_dimension=0, tiled...]
    ppermute x12, waiting for transfers between devices: 27.7 us -> 12.9 us  [shift(): return near(lax.ppermute(piece, 'seq', pairs_of))]
    all_to_all x4, waiting for transfers between devices: 16.4 us -> 30 us  [swap(): lax.all_to_all(packed, 'expert', split_axis=0, concat_axis=0, tiled=True)]
    pallas_call x2 -> x4, Pallas kernels: 22.9 us -> 28.6 us  [the longest x2 12.4 us: project(): pl.pallas_call(functools.partial(project_kernel, dims), grid=(blocks,), o...]
    unnamed x30 -> x12, local copies, waits for them, and re-layouts: 4.16 us -> 0.04 us
    all_to_all x4, starting transfers between devices: 36.8 us -> 33.9 us  [swap(): lax.all_to_all(packed, 'expert', split_axis=0, concat_axis=0, tiled=True)]
  transfers between devices with their start and end apart: 17 -> 17, of which waited for: 14 -> 9; matrix products, arithmetic and copies ran while one was open for 0% -> 0% of each run, Pallas kernels for 21% -> 24%
where the time goes in v2:
time: 174 us; the launch traced here: 170 us
  Pallas kernels  62.8 us (36%)
  starting transfers between devices  50.4 us (29%)
  waiting for transfers between devices  42.9 us (25%)
  between operations  14.2 us (8%)
    all_to_all x4, starting transfers between devices, swap(): lax.all_to_all(packed, 'expert', split_axis=0, concat_axis=0, tiled=True)  33.9 us
    all_to_all x4, waiting for transfers between devices, swap(): lax.all_to_all(packed, 'expert', split_axis=0, concat_axis=0, tiled=True)  30 us
    ppermute x12, starting transfers between devices, shift(): return near(lax.ppermute(piece, 'seq', pairs_of))  16.2 us
    ppermute x12, waiting for transfers between devices, shift(): return near(lax.ppermute(piece, 'seq', pairs_of))  12.9 us
    pallas_call x2, Pallas kernels, project(): pl.pallas_call(functools.partial(project_kernel, dims), grid=(blocks,), o...  12.4 us
    pallas_call x1, Pallas kernels, shards(): pl.pallas_call(functools.partial(weight_grad_kernel, pairs, parts, 2), gr...  8.98 us
    pallas_call x1, Pallas kernels, shards(): pl.pallas_call(hidden_kernel, grid=(blocks,), out_shape=[sds((2, slots, h...  7.22 us
    pallas_call x1, Pallas kernels, shards(): pl.pallas_call(functools.partial(dact_kernel, pairs, parts), grid=(blocks...  6.28 us
  transfers between devices with their start and end apart: 17, of which 9 were waited for; matrix products, arithmetic and copies ran while one was open for 0% of the time, Pallas kernels for 24%

profile of v2, /device:TPU:2, one launch (start us, length us, event | category | flops | bytes accessed | tf_op | source)
XLA Modules:
  0.0 170.3 jit_solution(3033421591153245299)
XLA Ops:
  10.8 2.9 %collective-permute-start.1 = (bf16[384,256]{1,0:T(8,128)(2,1)}, bf16[384,256]{1,0:T(8,128)(2,1)S(1)}, u32[]{:S(2)}, u32[]{:S(2)}) collective-permute-start(bf16[384,256]{1,0:T(8,128)(2,1)} %get-tuple-element.45), channel_id=1, source_target_pairs={{0,64},{32,96},{64,0},{96,32},{1,65},{33,97},{65,1},{97,33},{2,66}... | collective-permute-start | bytes 589832 | tf_op jit(solution)/shard_map/ppermute | solution.py:368
  15.1 2.8 %place.1 = (bf16[2,3,256,128]{3,2,1,0:T(8,128)(2,1)}, bf16[32,96,128]{2,1,0:T(8,128)(2,1)}) custom-call(s32[2,128]{1,0:T(2,128)} %bitcast.31, f32[2,128]{1,0:T(2,128)} %bitcast.29, bf16[128,1024]{1,0:T(8,128)(2,1)} %bitcast.23), custom_call_target="tpu_custom_call" | custom-call | tf_op jit(solution)/shard_map/place/pallas_call | solution.py:392
  17.9 11.7 %all-to-all-start.1 = ((bf16[32,96,128]{2,1,0:T(8,128)(2,1)}), bf16[32,96,128]{2,1,0:T(8,128)(2,1)}, u32[]{:S(2)}, u32[]{:S(2)}) async-start(bf16[32,96,128]{2,1,0:T(8,128)(2,1)} %get-tuple-element.52), calls=%async_computation.1 | async-start | bytes 1572864 | tf_op jit(solution)/shard_map/all_to_all | solution.py:371
  29.7 5.5 %attend.1 = (bf16[128,256]{1,0:T(8,128)(2,1)}, bf16[128,256]{1,0:T(8,128)(2,1)}, bf16[128,256]{1,0:T(8,128)(2,1)}, bf16[128,256]{1,0:T(8,128)(2,1)}, f32[2,512,512]{2,1,0:T(8,128)}) custom-call(bf16[384,256]{1,0:T(8,128)(2,1)} %get-tuple-element.41.refs_0_, bf16[384,256]{1,0:T(8,128)(2,1)S(1)} %collective-permute-done.refs_1_, ...), custom_call_target="tpu_custom_call" | custom-call | flops 999999995904 | bytes 1000000 | tf_op jit(solution)/shard_map/attend/pallas_call | solution.py:401
  35.2 2.7 %collective-permute-start.4 = (bf16[128,256]{1,0:T(8,128)(2,1)}, bf16[128,256]{1,0:T(8,128)(2,1)S(1)}, u32[]{:S(2)}, u32[]{:S(2)}) collective-permute-start(bf16[128,256]{1,0:T(8,128)(2,1)} %get-tuple-element.49), channel_id=1, source_target_pairs={{0,64},{32,96},{64,0},{96,32},{1,65},{33,97},{65,1},{97,33},{2,66}... | collective-permute-start | bytes 196616 | tf_op jit(solution)/shard_map/ppermute | solution.py:368
  41.4 2.2 %collective-permute-done.5.refs_3_ = bf16[128,256]{1,0:T(8,128)(2,1)S(1)} collective-permute-done((bf16[128,256]{1,0:T(8,128)(2,1)}, bf16[128,256]{1,0:T(8,128)(2,1)S(1)}, u32[]{:S(2)}, u32[]{:S(2)}) %collective-permute-start.5) | collective-permute-done | bytes 65568 | tf_op jit(solution)/shard_map/ppermute | solution.py:368
  43.7 2.5 %norm_pack.1 = (bf16[128,1024]{1,0:T(8,128)(2,1)}, bf16[32,96,128]{2,1,0:T(8,128)(2,1)}) custom-call(s32[1]{0:T(128)} %bitcast.5.me_ref, bf16[2,3,256,128]{3,2,1,0:T(8,128)(2,1)} %get-tuple-element.43.place_ref, bf16[128,256]{1,0:T(8,128)(2,1)} %get-tuple-element.47.refs_0_, bf16[128,256]{1,0:T(8,128)(2,1)S(1)} %collective-permute-done.3.refs_1_, ...), custom_call_target="tpu_custom_call" | custom-call | tf_op jit(solution)/shard_map/norm_pack/pallas_call | solution.py:414
  46.1 3.4 %all-to-all-done.1.packed_ref = bf16[32,96,128]{2,1,0:T(8,128)(2,1)} async-done(((bf16[32,96,128]{2,1,0:T(8,128)(2,1)}), bf16[32,96,128]{2,1,0:T(8,128)(2,1)}, u32[]{:S(2)}, u32[]{:S(2)}) %all-to-all-start.1) | async-done | bytes 786464 | tf_op jit(solution)/shard_map/all_to_all | solution.py:371
  49.6 7.4 %all-to-all-start = ((bf16[32,96,128]{2,1,0:T(8,128)(2,1)}), bf16[32,96,128]{2,1,0:T(8,128)(2,1)S(1)}, u32[]{:S(2)}, u32[]{:S(2)}) async-start(bf16[32,96,128]{2,1,0:T(8,128)(2,1)} %get-tuple-element.51), calls=%async_computation | async-start | bytes 1572864 | tf_op jit(solution)/shard_map/all_to_all | solution.py:371
  57.2 6.3 %dact.1 = (f32[384,2048]{1,0:T(8,128)}, bf16[1024,384]{1,0:T(8,128)(2,1)}) custom-call(bf16[32,96,128]{2,1,0:T(8,128)(2,1)} %all-to-all-done.1.packed_ref, bf16[2048,1024]{1,0:T(8,128)(2,1)} %bitcast.19), custom_call_target="tpu_custom_call" | custom-call | tf_op jit(solution)/shard_map/dact/pallas_call | solution.py:426
  63.4 13.2 %all-to-all-done.packed_ref = bf16[32,96,128]{2,1,0:T(8,128)(2,1)S(1)} async-done(((bf16[32,96,128]{2,1,0:T(8,128)(2,1)}), bf16[32,96,128]{2,1,0:T(8,128)(2,1)S(1)}, u32[]{:S(2)}, u32[]{:S(2)}) %all-to-all-start) | async-done | bytes 786464 | tf_op jit(solution)/shard_map/all_to_all | solution.py:371
  76.6 7.2 %expert_hidden.1 = (bf16[2,384,2048]{2,1,0:T(8,128)(2,1)}, bf16[384,1024]{1,0:T(8,128)(2,1)}) custom-call(bf16[32,96,128]{2,1,0:T(8,128)(2,1)S(1)} %all-to-all-done.packed_ref, bf16[1024,2048]{1,0:T(8,128)(2,1)} %bitcast.21, f32[384,2048]{1,0:T(8,128)} %get-tuple-element.53.dact_ref), custom_call_target="tpu_custom_call" | custom-call | tf_op jit(solution)/shard_map/expert_hidden/pallas_call | solution.py:439
  83.8 9.0 %weight_grads.1 = bf16[1024,4096]{1,0:T(8,128)(2,1)} custom-call(bf16[2,384,2048]{2,1,0:T(8,128)(2,1)} %get-tuple-element.58.hidden_ref, bf16[1024,384]{1,0:T(8,128)(2,1)} %get-tuple-element.55.turned_ref, bf16[384,1024]{1,0:T(8,128)(2,1)} %get-tuple-element.56.rows_ref), custom_call_target="tpu_custom_call" | custom-call | tf_op jit(solution)/shard_map/weight_grads/pallas_call | solution.py:457
  92.8 6.2 %dnormed.1 = bf16[32,96,128]{2,1,0:T(8,128)(2,1)} custom-call(bf16[2,384,2048]{2,1,0:T(8,128)(2,1)} %get-tuple-element.58.hidden_ref, bf16[1024,2048]{1,0:T(8,128)(2,1)} %bitcast.22), custom_call_target="tpu_custom_call" | custom-call | flops 999999995904 | bytes 1000000 | tf_op jit(solution)/shard_map/dnormed/pallas_call | solution.py:474
  99.1 7.5 %all-to-all-start.2 = ((bf16[32,96,128]{2,1,0:T(8,128)(2,1)}), bf16[32,96,128]{2,1,0:T(8,128)(2,1)S(1)}, u32[]{:S(2)}, u32[]{:S(2)}) async-start(bf16[32,96,128]{2,1,0:T(8,128)(2,1)} %dnormed.1), calls=%async_computation.2 | async-start | bytes 1572864 | tf_op jit(solution)/shard_map/all_to_all | solution.py:371
  106.6 6.2 %expert_out.1 = bf16[32,96,128]{2,1,0:T(8,128)(2,1)} custom-call(bf16[2,384,2048]{2,1,0:T(8,128)(2,1)} %get-tuple-element.58.hidden_ref, bf16[2048,1024]{1,0:T(8,128)(2,1)} %bitcast.20), custom_call_target="tpu_custom_call" | custom-call | tf_op jit(solution)/shard_map/expert_out/pallas_call | solution.py:474
  112.8 13.4 %all-to-all-done.2.back_ref = bf16[32,96,128]{2,1,0:T(8,128)(2,1)S(1)} async-done(((bf16[32,96,128]{2,1,0:T(8,128)(2,1)}), bf16[32,96,128]{2,1,0:T(8,128)(2,1)S(1)}, u32[]{:S(2)}, u32[]{:S(2)}) %all-to-all-start.2) | async-done | bytes 786464 | tf_op jit(solution)/shard_map/all_to_all | solution.py:371
  126.2 2.4 %dattended.1 = (bf16[128,256]{1,0:T(8,128)(2,1)}, bf16[128,256]{1,0:T(8,128)(2,1)}, bf16[128,256]{1,0:T(8,128)(2,1)}, bf16[128,256]{1,0:T(8,128)(2,1)}) custom-call(s32[1]{0:T(128)} %bitcast.5.me_ref, bf16[2,3,256,128]{3,2,1,0:T(8,128)(2,1)} %get-tuple-element.43.place_ref, bf16[32,96,128]{2,1,0:T(8,128)(2,1)S(1)} %all-to-all-done.2.back_ref, ...), custom_call_target="tpu_custom_call" | custom-call | tf_op jit(solution)/shard_map/dattended/pallas_call | solution.py:497
  132.0 7.5 %all-to-all-start.3 = ((bf16[32,96,128]{2,1,0:T(8,128)(2,1)}), bf16[32,96,128]{2,1,0:T(8,128)(2,1)S(1)}, u32[]{:S(2)}, u32[]{:S(2)}) async-start(bf16[32,96,128]{2,1,0:T(8,128)(2,1)} %expert_out.1), calls=%async_computation.3 | async-start | bytes 1572864 | tf_op jit(solution)/shard_map/all_to_all | solution.py:371
  139.5 5.7 %attend_back.1 = (bf16[384,256]{1,0:T(8,128)(2,1)}, bf16[384,256]{1,0:T(8,128)(2,1)}, bf16[384,256]{1,0:T(8,128)(2,1)}, bf16[384,256]{1,0:T(8,128)(2,1)}) custom-call(bf16[384,256]{1,0:T(8,128)(2,1)} %get-tuple-element.41.refs_0_, bf16[384,256]{1,0:T(8,128)(2,1)S(1)} %copy-done.1, bf16[384,256]{1,0:T(8,128)(2,1)S(1)} %copy-done.3, ...), custom_call_target="tpu_custom_call" | custom-call | flops 40000000000 | bytes 1000000 | tf_op jit(solution)/shard_map/attend_back/pallas_call | solution.py:509
  149.4 2.6 %collective-permute-done.9.refs_1_ = bf16[384,256]{1,0:T(8,128)(2,1)S(1)} collective-permute-done((bf16[384,256]{1,0:T(8,128)(2,1)}, bf16[384,256]{1,0:T(8,128)(2,1)S(1)}, u32[]{:S(2)}, u32[]{:S(2)}) %collective-permute-start.9) | collective-permute-done | bytes 196640 | tf_op jit(solution)/shard_map/ppermute | solution.py:368
  152.0 2.5 %collective-permute-done.10.refs_2_ = bf16[384,256]{1,0:T(8,128)(2,1)S(1)} collective-permute-done((bf16[384,256]{1,0:T(8,128)(2,1)}, bf16[384,256]{1,0:T(8,128)(2,1)S(1)}, u32[]{:S(2)}, u32[]{:S(2)}) %collective-permute-start.10) | collective-permute-done | bytes 196640 | tf_op jit(solution)/shard_map/ppermute | solution.py:368
  158.4 2.3 %mix.1 = bf16[128,1024]{1,0:T(8,128)(2,1)} custom-call(bf16[2,3,256,128]{3,2,1,0:T(8,128)(2,1)} %get-tuple-element.43.place_ref, bf16[32,96,128]{2,1,0:T(8,128)(2,1)S(1)} %all-to-all-done.3.back_ref, bf16[128,1024]{1,0:T(8,128)(2,1)} %get-tuple-element.60.attended_ref, f32[2,128]{1,0:T(2,128)} %bitcast.30), custom_call_target="tpu_custom_call" | custom-call | tf_op jit(solution)/shard_map/mix/pallas_call | solution.py:522
  160.7 2.8 %widen.1 = (f32[128,2048]{1,0:T(8,128)}, f32[2048,128]{1,0:T(8,128)}) custom-call(bf16[128,4096]{1,0:T(8,128)(2,1)} %reduce-scatter.2.cloned.1.call-done.sums_ref), custom_call_target="tpu_custom_call" | custom-call | tf_op jit(solution)/shard_map/widen/pallas_call | solution.py:537
  (37 shorter events, 20.3 us)
Async XLA Ops:
  9.3 20.4 %collective-permute-start = (bf16[384,256]{1,0:T(8,128)(2,1)}, bf16[384,256]{1,0:T(8,128)(2,1)S(1)}, u32[]{:S(2)}, u32[]{:S(2)}) collective-permute-start(bf16[384,256]{1,0:T(8,128)(2,1)} %get-tuple-element.44), channel_id=1, source_target_pairs={{0,32},{32,64},{64,96},{96,0},{1,33},{33,65},{65,97},{97,1},{2,34}... | collective-permute-start | bytes 589832 | tf_op jit(solution)/shard_map/ppermute | solution.py:368
  10.8 18.8 %collective-permute-start.1 = (bf16[384,256]{1,0:T(8,128)(2,1)}, bf16[384,256]{1,0:T(8,128)(2,1)S(1)}, u32[]{:S(2)}, u32[]{:S(2)}) collective-permute-start(bf16[384,256]{1,0:T(8,128)(2,1)} %get-tuple-element.45), channel_id=1, source_target_pairs={{0,64},{32,96},{64,0},{96,32},{1,65},{33,97},{65,1},{97,33},{2,66}... | collective-permute-start | bytes 589832 | tf_op jit(solution)/shard_map/ppermute | solution.py:368
  13.7 15.9 %collective-permute-start.2 = (bf16[384,256]{1,0:T(8,128)(2,1)}, bf16[384,256]{1,0:T(8,128)(2,1)S(1)}, u32[]{:S(2)}, u32[]{:S(2)}) collective-permute-start(bf16[384,256]{1,0:T(8,128)(2,1)} %get-tuple-element.46), channel_id=1, source_target_pairs={{0,96},{32,0},{64,32},{96,64},{1,97},{33,1},{65,33},{97,65},{2,98}... | collective-permute-start | bytes 589832 | tf_op jit(solution)/shard_map/ppermute | solution.py:368
  17.9 31.6 %all-to-all-start.1 = ((bf16[32,96,128]{2,1,0:T(8,128)(2,1)}), bf16[32,96,128]{2,1,0:T(8,128)(2,1)}, u32[]{:S(2)}, u32[]{:S(2)}) async-start(bf16[32,96,128]{2,1,0:T(8,128)(2,1)} %get-tuple-element.52), calls=%async_computation.1 | async-start | bytes 1572864 | tf_op jit(solution)/shard_map/all_to_all | solution.py:371
  29.6 5.5 %copy-start = (bf16[384,256]{1,0:T(8,128)(2,1)}, bf16[384,256]{1,0:T(8,128)(2,1)S(1)}, u32[]{:S(2)}) copy-start(bf16[384,256]{1,0:T(8,128)(2,1)S(1)} %collective-permute-done.refs_1_) | copy-start | bytes 589828
  29.6 5.5 %copy-start.2 = (bf16[384,256]{1,0:T(8,128)(2,1)}, bf16[384,256]{1,0:T(8,128)(2,1)S(1)}, u32[]{:S(2)}) copy-start(bf16[384,256]{1,0:T(8,128)(2,1)S(1)} %collective-permute-done.1.refs_2_) | copy-start | bytes 589828
  29.7 5.5 %copy-start.4 = (bf16[384,256]{1,0:T(8,128)(2,1)}, bf16[384,256]{1,0:T(8,128)(2,1)S(1)}, u32[]{:S(2)}) copy-start(bf16[384,256]{1,0:T(8,128)(2,1)S(1)} %collective-permute-done.2.refs_3_) | copy-start | bytes 589828
  35.1 4.6 %collective-permute-start.3 = (bf16[128,256]{1,0:T(8,128)(2,1)}, bf16[128,256]{1,0:T(8,128)(2,1)S(1)}, u32[]{:S(2)}, u32[]{:S(2)}) collective-permute-start(bf16[128,256]{1,0:T(8,128)(2,1)} %get-tuple-element.48), channel_id=1, source_target_pairs={{0,96},{32,0},{64,32},{96,64},{1,97},{33,1},{65,33},{97,65},{2,98}... | collective-permute-start | bytes 196616 | tf_op jit(solution)/shard_map/ppermute | solution.py:368
  35.2 6.2 %collective-permute-start.4 = (bf16[128,256]{1,0:T(8,128)(2,1)}, bf16[128,256]{1,0:T(8,128)(2,1)S(1)}, u32[]{:S(2)}, u32[]{:S(2)}) collective-permute-start(bf16[128,256]{1,0:T(8,128)(2,1)} %get-tuple-element.49), channel_id=1, source_target_pairs={{0,64},{32,96},{64,0},{96,32},{1,65},{33,97},{65,1},{97,33},{2,66}... | collective-permute-start | bytes 196616 | tf_op jit(solution)/shard_map/ppermute | solution.py:368
  38.0 5.7 %collective-permute-start.5 = (bf16[128,256]{1,0:T(8,128)(2,1)}, bf16[128,256]{1,0:T(8,128)(2,1)S(1)}, u32[]{:S(2)}, u32[]{:S(2)}) collective-permute-start(bf16[128,256]{1,0:T(8,128)(2,1)} %get-tuple-element.50), channel_id=1, source_target_pairs={{0,32},{32,64},{64,96},{96,0},{1,33},{33,65},{65,97},{97,1},{2,34}... | collective-permute-start | bytes 196616 | tf_op jit(solution)/shard_map/ppermute | solution.py:368
  49.6 27.0 %all-to-all-start = ((bf16[32,96,128]{2,1,0:T(8,128)(2,1)}), bf16[32,96,128]{2,1,0:T(8,128)(2,1)S(1)}, u32[]{:S(2)}, u32[]{:S(2)}) async-start(bf16[32,96,128]{2,1,0:T(8,128)(2,1)} %get-tuple-element.51), calls=%async_computation | async-start | bytes 1572864 | tf_op jit(solution)/shard_map/all_to_all | solution.py:371
  56.9 103.8 %reduce-scatter.2.cloned.1.call-start = ((), (), s32[]{:S(2)}) async-start(), calls=%async_computation.5 | async-start | bytes 9437184 | tf_op jit(solution)/shard_map/reduce_scatter | solution.py:471
  99.1 27.1 %all-to-all-start.2 = ((bf16[32,96,128]{2,1,0:T(8,128)(2,1)}), bf16[32,96,128]{2,1,0:T(8,128)(2,1)S(1)}, u32[]{:S(2)}, u32[]{:S(2)}) async-start(bf16[32,96,128]{2,1,0:T(8,128)(2,1)} %dnormed.1), calls=%async_computation.2 | async-start | bytes 1572864 | tf_op jit(solution)/shard_map/all_to_all | solution.py:371
  106.5 32.9 %copy-start.1 = (bf16[384,256]{1,0:T(8,128)(2,1)S(1)}, bf16[384,256]{1,0:T(8,128)(2,1)}, u32[]{:S(2)}) copy-start(bf16[384,256]{1,0:T(8,128)(2,1)} %copy-done) | copy-start | bytes 589828
  106.5 32.9 %copy-start.3 = (bf16[384,256]{1,0:T(8,128)(2,1)S(1)}, bf16[384,256]{1,0:T(8,128)(2,1)}, u32[]{:S(2)}) copy-start(bf16[384,256]{1,0:T(8,128)(2,1)} %copy-done.2) | copy-start | bytes 589828
  106.5 32.9 %copy-start.5 = (bf16[384,256]{1,0:T(8,128)(2,1)S(1)}, bf16[384,256]{1,0:T(8,128)(2,1)}, u32[]{:S(2)}) copy-start(bf16[384,256]{1,0:T(8,128)(2,1)} %copy-done.4) | copy-start | bytes 589828
  128.6 10.9 %collective-permute-start.6 = (bf16[128,256]{1,0:T(8,128)(2,1)}, bf16[128,256]{1,0:T(8,128)(2,1)S(1)}, u32[]{:S(2)}, u32[]{:S(2)}) collective-permute-start(bf16[128,256]{1,0:T(8,128)(2,1)} %get-tuple-element.63), channel_id=1, source_target_pairs={{0,32},{32,64},{64,96},{96,0},{1,33},{33,65},{65,97},{97,1},{2,34}... | collective-permute-start | bytes 196616 | tf_op jit(solution)/shard_map/ppermute | solution.py:368
  129.3 10.2 %collective-permute-start.7 = (bf16[128,256]{1,0:T(8,128)(2,1)}, bf16[128,256]{1,0:T(8,128)(2,1)S(1)}, u32[]{:S(2)}, u32[]{:S(2)}) collective-permute-start(bf16[128,256]{1,0:T(8,128)(2,1)} %get-tuple-element.64), channel_id=1, source_target_pairs={{0,64},{32,96},{64,0},{96,32},{1,65},{33,97},{65,1},{97,33},{2,66}... | collective-permute-start | bytes 196616 | tf_op jit(solution)/shard_map/ppermute | solution.py:368
  130.5 8.9 %collective-permute-start.8 = (bf16[128,256]{1,0:T(8,128)(2,1)}, bf16[128,256]{1,0:T(8,128)(2,1)S(1)}, u32[]{:S(2)}, u32[]{:S(2)}) collective-permute-start(bf16[128,256]{1,0:T(8,128)(2,1)} %get-tuple-element.65), channel_id=1, source_target_pairs={{0,96},{32,0},{64,32},{96,64},{1,97},{33,1},{65,33},{97,65},{2,98}... | collective-permute-start | bytes 196616 | tf_op jit(solution)/shard_map/ppermute | solution.py:368
  132.0 26.5 %all-to-all-start.3 = ((bf16[32,96,128]{2,1,0:T(8,128)(2,1)}), bf16[32,96,128]{2,1,0:T(8,128)(2,1)S(1)}, u32[]{:S(2)}, u32[]{:S(2)}) async-start(bf16[32,96,128]{2,1,0:T(8,128)(2,1)} %expert_out.1), calls=%async_computation.3 | async-start | bytes 1572864 | tf_op jit(solution)/shard_map/all_to_all | solution.py:371
  145.2 6.8 %collective-permute-start.9 = (bf16[384,256]{1,0:T(8,128)(2,1)}, bf16[384,256]{1,0:T(8,128)(2,1)S(1)}, u32[]{:S(2)}, u32[]{:S(2)}) collective-permute-start(bf16[384,256]{1,0:T(8,128)(2,1)} %get-tuple-element.68), channel_id=1, source_target_pairs={{0,96},{32,0},{64,32},{96,64},{1,97},{33,1},{65,33},{97,65},{2,98}... | collective-permute-start | bytes 589832 | tf_op jit(solution)/shard_map/ppermute | solution.py:368
  146.6 8.0 %collective-permute-start.10 = (bf16[384,256]{1,0:T(8,128)(2,1)}, bf16[384,256]{1,0:T(8,128)(2,1)S(1)}, u32[]{:S(2)}, u32[]{:S(2)}) collective-permute-start(bf16[384,256]{1,0:T(8,128)(2,1)} %get-tuple-element.69), channel_id=1, source_target_pairs={{0,64},{32,96},{64,0},{96,32},{1,65},{33,97},{65,1},{97,33},{2,66}... | collective-permute-start | bytes 589832 | tf_op jit(solution)/shard_map/ppermute | solution.py:368
  148.0 8.6 %collective-permute-start.11 = (bf16[384,256]{1,0:T(8,128)(2,1)}, bf16[384,256]{1,0:T(8,128)(2,1)S(1)}, u32[]{:S(2)}, u32[]{:S(2)}) collective-permute-start(bf16[384,256]{1,0:T(8,128)(2,1)} %get-tuple-element.70), channel_id=1, source_target_pairs={{0,32},{32,64},{64,96},{96,0},{1,33},{33,65},{65,97},{97,1},{2,34}... | collective-permute-start | bytes 589832 | tf_op jit(solution)/shard_map/ppermute | solution.py:368
Sparse Core Ops, SparseCore 0:
  93.0 54.0 reduce-scatter.1

commit v3 on v2

--- a/solution.py
+++ b/solution.py
@@ -267,8 +267,10 @@
     out_ref[...] = dot(rows[...], down_ref[...], NT)
 
 
-def hidden_kernel(packed_ref, up_ref, dact_ref, hidden_ref, rows_ref):
-    @pl.when(pl.program_id(0) == 0)
+def expert_kernel(packed_ref, up_ref, dact_ref, hidden_ref, rows_ref, dnormed_ref, total):
+    step = pl.program_id(0)
+
+    @pl.when(step == 0)
     def _():
         unpack_rows(packed_ref, rows_ref)
 
@@ -278,7 +280,21 @@
     act = pre * half
     hidden_ref[0] = act.astype(BF)
     slope = half + act * (1.0 - half) * (2.0 * GELU_COEF + (6.0 * GELU_COEF * 0.044715) * square)
-    hidden_ref[1] = (dact_ref[...] * slope).astype(BF)
+    dpre = (dact_ref[...] * slope).astype(BF)
+    hidden_ref[1] = dpre
+    part = dot(dpre, up_ref[...], NT)
+
+    @pl.when(step == 0)
+    def _():
+        total[...] = part
+
+    @pl.when(step > 0)
+    def _():
+        total[...] += part
+
+    @pl.when(step == pl.num_programs(0) - 1)
+    def _():
+        pack_rows(total[...], dnormed_ref)
 
 
 def weight_grad_kernel(pairs, parts, blocks, hidden_ref, turned_ref, rows_ref, grads_ref, turned):
@@ -297,9 +313,9 @@
         grads_ref[...] = dot(turned[...], hidden_ref[0]).astype(BF)
 
 
-def project_kernel(dims, hidden_ref, weight_ref, packed_ref, total):
+def out_kernel(hidden_ref, weight_ref, packed_ref, total):
     step = pl.program_id(0)
-    part = dot(hidden_ref[0], weight_ref[...], dims)
+    part = dot(hidden_ref[0], weight_ref[...])
 
     @pl.when(step == 0)
     def _():
@@ -436,10 +452,10 @@
         compiler_params=BIG,
         name="dact",
     )(grad_wire, down)
-    both, rows = pl.pallas_call(
-        hidden_kernel,
+    both, rows, dnormed = pl.pallas_call(
+        expert_kernel,
         grid=(blocks,),
-        out_shape=[sds((2, slots, hidden), BF), sds((slots, model), BF)],
+        out_shape=[sds((2, slots, hidden), BF), sds((slots, model), BF), wire],
         in_specs=[
             VMEM,
             pl.BlockSpec((model, chunk), lambda i: (0, i)),
@@ -448,10 +464,13 @@
         out_specs=[
             pl.BlockSpec((2, slots, chunk), lambda i: (0, 0, i)),
             pl.BlockSpec((slots, model), lambda i: (0, 0)),
+            whole_wire,
         ],
+        scratch_shapes=[pltpu.VMEM((slots, model), F32)],
         compiler_params=BIG,
-        name="expert_hidden",
+        name="expert",
     )(wire_rows, up, dact)
+    dnormed_back = swap(dnormed)
 
     half = hidden // 2
     partial_grads = pl.pallas_call(
@@ -470,28 +489,20 @@
     )(both, turned, rows)
     sums = lax.psum_scatter(partial_grads, ("seq", "dp"), scatter_dimension=0, tiled=True)
 
-    def project(source, which, weight, weight_spec, dims, cost, name):
-        return pl.pallas_call(
-            functools.partial(project_kernel, dims),
-            grid=(blocks,),
-            out_shape=wire,
-            in_specs=[pl.BlockSpec((1, slots, chunk), lambda i: (which, 0, i)), weight_spec],
-            out_specs=whole_wire,
-            scratch_shapes=[pltpu.VMEM((slots, model), F32)],
-            compiler_params=BIG,
-            cost_estimate=cost,
-            name=name,
-        )(source, weight)
-
     both_late, _ = lax.optimization_barrier((both, partial_grads))
-    dnormed = project(
-        both_late, 1, up, pl.BlockSpec((model, chunk), lambda i: (0, i)), NT, HEAVY, "dnormed"
-    )
-    both_last, _ = lax.optimization_barrier((both_late, dnormed))
-    dnormed_back = swap(dnormed)
-    produced = project(
-        both_last, 0, down, pl.BlockSpec((chunk, model), lambda i: (i, 0)), NN, None, "expert_out"
-    )
+    produced = pl.pallas_call(
+        out_kernel,
+        grid=(blocks,),
+        out_shape=wire,
+        in_specs=[
+            pl.BlockSpec((1, slots, chunk), lambda i: (0, 0, i)),
+            pl.BlockSpec((chunk, model), lambda i: (i, 0)),
+        ],
+        out_specs=whole_wire,
+        scratch_shapes=[pltpu.VMEM((slots, model), F32)],
+        compiler_params=BIG,
+        name="expert_out",
+    )(both_late, down)
 
     dnormed_back, produced = lax.optimization_barrier((dnormed_back, produced))
     grad_pieces = pl.pallas_call(
@@ -500,6 +511,7 @@
         in_specs=[SMEM] + [VMEM] * 4,
         out_specs=[VMEM] * parts,
         scratch_shapes=[pltpu.VMEM((tokens, model), BF)],
+        cost_estimate=HEAVY,
         name="dattended",
     )(me, place, dnormed_back, attended, cot)
     grad_pieces = exchange(grad_pieces, 1)

time: 174 us -> 179 us (1.029)
  waiting for transfers between devices: 42.9 us -> 52.7 us
  Pallas kernels: 62.8 us -> 59.1 us
    reduce_scatter x1, waiting for transfers between devices: 0.01 us -> 15 us  [shards(): lax.psum_scatter(partial_grads, ('seq', 'dp'), scatter_dimension=0, tiled...]
    all_to_all x4, waiting for transfers between devices: 30 us -> 21.1 us  [swap(): lax.all_to_all(packed, 'expert', split_axis=0, concat_axis=0, tiled=True)]
    pallas_call x3 -> x2, Pallas kernels: 19.7 us -> 15.8 us  [the longest x1 9.63 us: shards(): pl.pallas_call(expert_kernel, grid=(blocks,), out_shape=[sds((2, slots, h...]
    ppermute x12, waiting for transfers between devices: 12.9 us -> 16.6 us  [shift(): return near(lax.ppermute(piece, 'seq', pairs_of))]
  transfers between devices with their start and end apart: 17 -> 17, of which waited for: 9 -> 10; matrix products, arithmetic and copies ran while one was open for 0% -> 0% of each run, Pallas kernels for 24% -> 25%
where the time goes in v3:
time: 179 us; the launch traced here: 176 us
  Pallas kernels  59.1 us (33%)
  waiting for transfers between devices  52.7 us (29%)
  starting transfers between devices  50.5 us (28%)
  between operations  14.2 us (8%)
    all_to_all x4, starting transfers between devices, swap(): lax.all_to_all(packed, 'expert', split_axis=0, concat_axis=0, tiled=True)  34 us
    all_to_all x4, waiting for transfers between devices, swap(): lax.all_to_all(packed, 'expert', split_axis=0, concat_axis=0, tiled=True)  21.1 us
    ppermute x12, waiting for transfers between devices, shift(): return near(lax.ppermute(piece, 'seq', pairs_of))  16.6 us
    ppermute x12, starting transfers between devices, shift(): return near(lax.ppermute(piece, 'seq', pairs_of))  16.2 us
    reduce_scatter x1, waiting for transfers between devices, shards(): lax.psum_scatter(partial_grads, ('seq', 'dp'), scatter_dimension=0, tiled...  15 us
    pallas_call x1, Pallas kernels, shards(): pl.pallas_call(expert_kernel, grid=(blocks,), out_shape=[sds((2, slots, h...  9.63 us
    pallas_call x1, Pallas kernels, shards(): pl.pallas_call(functools.partial(weight_grad_kernel, pairs, parts, 2), gr...  9.01 us
    pallas_call x1, Pallas kernels, shards(): pl.pallas_call(functools.partial(dact_kernel, pairs, parts), grid=(blocks...  6.28 us
  transfers between devices with their start and end apart: 17, of which 10 were waited for; matrix products, arithmetic and copies ran while one was open for 0% of the time, Pallas kernels for 25%

profile of v3, /device:TPU:2, one launch (start us, length us, event | category | flops | bytes accessed | tf_op | source)
XLA Modules:
  0.0 176.5 jit_solution(15438325105213843120)
XLA Ops:
  10.8 2.9 %collective-permute-start.1 = (bf16[384,256]{1,0:T(8,128)(2,1)}, bf16[384,256]{1,0:T(8,128)(2,1)S(1)}, u32[]{:S(2)}, u32[]{:S(2)}) collective-permute-start(bf16[384,256]{1,0:T(8,128)(2,1)} %get-tuple-element.45), channel_id=1, source_target_pairs={{0,64},{32,96},{64,0},{96,32},{1,65},{33,97},{65,1},{97,33},{2,66}... | collective-permute-start | bytes 589832 | tf_op jit(solution)/shard_map/ppermute | solution.py:384
  15.1 2.8 %place.1 = (bf16[2,3,256,128]{3,2,1,0:T(8,128)(2,1)}, bf16[32,96,128]{2,1,0:T(8,128)(2,1)}) custom-call(s32[2,128]{1,0:T(2,128)} %bitcast.30, f32[2,128]{1,0:T(2,128)} %bitcast.28, bf16[128,1024]{1,0:T(8,128)(2,1)} %bitcast.22), custom_call_target="tpu_custom_call" | custom-call | tf_op jit(solution)/shard_map/place/pallas_call | solution.py:408
  17.9 11.7 %all-to-all-start.1 = ((bf16[32,96,128]{2,1,0:T(8,128)(2,1)}), bf16[32,96,128]{2,1,0:T(8,128)(2,1)}, u32[]{:S(2)}, u32[]{:S(2)}) async-start(bf16[32,96,128]{2,1,0:T(8,128)(2,1)} %get-tuple-element.52), calls=%async_computation.1 | async-start | bytes 1572864 | tf_op jit(solution)/shard_map/all_to_all | solution.py:387
  29.7 5.5 %attend.1 = (bf16[128,256]{1,0:T(8,128)(2,1)}, bf16[128,256]{1,0:T(8,128)(2,1)}, bf16[128,256]{1,0:T(8,128)(2,1)}, bf16[128,256]{1,0:T(8,128)(2,1)}, f32[2,512,512]{2,1,0:T(8,128)}) custom-call(bf16[384,256]{1,0:T(8,128)(2,1)} %get-tuple-element.41.refs_0_, bf16[384,256]{1,0:T(8,128)(2,1)S(1)} %collective-permute-done.refs_1_, ...), custom_call_target="tpu_custom_call" | custom-call | flops 999999995904 | bytes 1000000 | tf_op jit(solution)/shard_map/attend/pallas_call | solution.py:417
  35.2 2.7 %collective-permute-start.4 = (bf16[128,256]{1,0:T(8,128)(2,1)}, bf16[128,256]{1,0:T(8,128)(2,1)S(1)}, u32[]{:S(2)}, u32[]{:S(2)}) collective-permute-start(bf16[128,256]{1,0:T(8,128)(2,1)} %get-tuple-element.49), channel_id=1, source_target_pairs={{0,64},{32,96},{64,0},{96,32},{1,65},{33,97},{65,1},{97,33},{2,66}... | collective-permute-start | bytes 196616 | tf_op jit(solution)/shard_map/ppermute | solution.py:384
  41.4 2.2 %collective-permute-done.5.refs_3_ = bf16[128,256]{1,0:T(8,128)(2,1)S(1)} collective-permute-done((bf16[128,256]{1,0:T(8,128)(2,1)}, bf16[128,256]{1,0:T(8,128)(2,1)S(1)}, u32[]{:S(2)}, u32[]{:S(2)}) %collective-permute-start.5) | collective-permute-done | bytes 65568 | tf_op jit(solution)/shard_map/ppermute | solution.py:384
  43.7 2.5 %norm_pack.1 = (bf16[128,1024]{1,0:T(8,128)(2,1)}, bf16[32,96,128]{2,1,0:T(8,128)(2,1)}) custom-call(s32[1]{0:T(128)} %bitcast.5.me_ref, bf16[2,3,256,128]{3,2,1,0:T(8,128)(2,1)} %get-tuple-element.43.place_ref, bf16[128,256]{1,0:T(8,128)(2,1)} %get-tuple-element.47.refs_0_, bf16[128,256]{1,0:T(8,128)(2,1)S(1)} %collective-permute-done.3.refs_1_, ...), custom_call_target="tpu_custom_call" | custom-call | tf_op jit(solution)/shard_map/norm_pack/pallas_call | solution.py:430
  46.1 3.4 %all-to-all-done.1.packed_ref = bf16[32,96,128]{2,1,0:T(8,128)(2,1)} async-done(((bf16[32,96,128]{2,1,0:T(8,128)(2,1)}), bf16[32,96,128]{2,1,0:T(8,128)(2,1)}, u32[]{:S(2)}, u32[]{:S(2)}) %all-to-all-start.1) | async-done | bytes 786464 | tf_op jit(solution)/shard_map/all_to_all | solution.py:387
  49.6 7.4 %all-to-all-start = ((bf16[32,96,128]{2,1,0:T(8,128)(2,1)}), bf16[32,96,128]{2,1,0:T(8,128)(2,1)S(1)}, u32[]{:S(2)}, u32[]{:S(2)}) async-start(bf16[32,96,128]{2,1,0:T(8,128)(2,1)} %get-tuple-element.51), calls=%async_computation | async-start | bytes 1572864 | tf_op jit(solution)/shard_map/all_to_all | solution.py:387
  56.9 6.3 %dact.1 = (f32[384,2048]{1,0:T(8,128)}, bf16[1024,384]{1,0:T(8,128)(2,1)}) custom-call(bf16[32,96,128]{2,1,0:T(8,128)(2,1)} %all-to-all-done.1.packed_ref, bf16[2048,1024]{1,0:T(8,128)(2,1)} %bitcast.19), custom_call_target="tpu_custom_call" | custom-call | tf_op jit(solution)/shard_map/dact/pallas_call | solution.py:442
  63.2 13.4 %all-to-all-done.packed_ref = bf16[32,96,128]{2,1,0:T(8,128)(2,1)S(1)} async-done(((bf16[32,96,128]{2,1,0:T(8,128)(2,1)}), bf16[32,96,128]{2,1,0:T(8,128)(2,1)S(1)}, u32[]{:S(2)}, u32[]{:S(2)}) %all-to-all-start) | async-done | bytes 786464 | tf_op jit(solution)/shard_map/all_to_all | solution.py:387
  76.6 9.6 %expert.1 = (bf16[2,384,2048]{2,1,0:T(8,128)(2,1)}, bf16[384,1024]{1,0:T(8,128)(2,1)}, bf16[32,96,128]{2,1,0:T(8,128)(2,1)}) custom-call(bf16[32,96,128]{2,1,0:T(8,128)(2,1)S(1)} %all-to-all-done.packed_ref, bf16[1024,2048]{1,0:T(8,128)(2,1)} %bitcast.21, f32[384,2048]{1,0:T(8,128)} %get-tuple-element.53.dact_ref), custom_call_target="tpu_custom_call" | custom-call | tf_op jit(solution)/shard_map/expert/pallas_call | solution.py:455
  86.2 7.5 %all-to-all-start.2 = ((bf16[32,96,128]{2,1,0:T(8,128)(2,1)}), bf16[32,96,128]{2,1,0:T(8,128)(2,1)S(1)}, u32[]{:S(2)}, u32[]{:S(2)}) async-start(bf16[32,96,128]{2,1,0:T(8,128)(2,1)} %get-tuple-element.54), calls=%async_computation.2 | async-start | bytes 1572864 | tf_op jit(solution)/shard_map/all_to_all | solution.py:387
  93.9 9.0 %weight_grads.1 = bf16[1024,4096]{1,0:T(8,128)(2,1)} custom-call(bf16[2,384,2048]{2,1,0:T(8,128)(2,1)} %get-tuple-element.58.hidden_ref, bf16[1024,384]{1,0:T(8,128)(2,1)} %get-tuple-element.56.turned_ref, bf16[384,1024]{1,0:T(8,128)(2,1)} %get-tuple-element.57.rows_ref), custom_call_target="tpu_custom_call" | custom-call | tf_op jit(solution)/shard_map/weight_grads/pallas_call | solution.py:476
  103.0 6.1 %expert_out.1 = bf16[32,96,128]{2,1,0:T(8,128)(2,1)} custom-call(bf16[2,384,2048]{2,1,0:T(8,128)(2,1)} %get-tuple-element.58.hidden_ref, bf16[2048,1024]{1,0:T(8,128)(2,1)} %bitcast.20), custom_call_target="tpu_custom_call" | custom-call | tf_op jit(solution)/shard_map/expert_out/pallas_call | solution.py:493
  109.1 4.3 %all-to-all-done.2.back_ref = bf16[32,96,128]{2,1,0:T(8,128)(2,1)S(1)} async-done(((bf16[32,96,128]{2,1,0:T(8,128)(2,1)}), bf16[32,96,128]{2,1,0:T(8,128)(2,1)S(1)}, u32[]{:S(2)}, u32[]{:S(2)}) %all-to-all-start.2) | async-done | bytes 786464 | tf_op jit(solution)/shard_map/all_to_all | solution.py:387
  113.4 2.5 %dattended.1 = (bf16[128,256]{1,0:T(8,128)(2,1)}, bf16[128,256]{1,0:T(8,128)(2,1)}, bf16[128,256]{1,0:T(8,128)(2,1)}, bf16[128,256]{1,0:T(8,128)(2,1)}) custom-call(s32[1]{0:T(128)} %bitcast.5.me_ref, bf16[2,3,256,128]{3,2,1,0:T(8,128)(2,1)} %get-tuple-element.43.place_ref, bf16[32,96,128]{2,1,0:T(8,128)(2,1)S(1)} %all-to-all-done.2.back_ref, ...), custom_call_target="tpu_custom_call" | custom-call | flops 999999995904 | bytes 1000000 | tf_op jit(solution)/shard_map/dattended/pallas_call | solution.py:508
  119.4 7.5 %all-to-all-start.3 = ((bf16[32,96,128]{2,1,0:T(8,128)(2,1)}), bf16[32,96,128]{2,1,0:T(8,128)(2,1)S(1)}, u32[]{:S(2)}, u32[]{:S(2)}) async-start(bf16[32,96,128]{2,1,0:T(8,128)(2,1)} %expert_out.1), calls=%async_computation.3 | async-start | bytes 1572864 | tf_op jit(solution)/shard_map/all_to_all | solution.py:387
  127.0 5.7 %attend_back.1 = (bf16[384,256]{1,0:T(8,128)(2,1)}, bf16[384,256]{1,0:T(8,128)(2,1)}, bf16[384,256]{1,0:T(8,128)(2,1)}, bf16[384,256]{1,0:T(8,128)(2,1)}) custom-call(bf16[384,256]{1,0:T(8,128)(2,1)} %get-tuple-element.41.refs_0_, bf16[384,256]{1,0:T(8,128)(2,1)S(1)} %copy-done.1, bf16[384,256]{1,0:T(8,128)(2,1)S(1)} %copy-done.3, ...), custom_call_target="tpu_custom_call" | custom-call | flops 40000000000 | bytes 1000000 | tf_op jit(solution)/shard_map/attend_back/pallas_call | solution.py:521
  136.8 6.1 %collective-permute-done.9.refs_1_ = bf16[384,256]{1,0:T(8,128)(2,1)S(1)} collective-permute-done((bf16[384,256]{1,0:T(8,128)(2,1)}, bf16[384,256]{1,0:T(8,128)(2,1)S(1)}, u32[]{:S(2)}, u32[]{:S(2)}) %collective-permute-start.9) | collective-permute-done | bytes 196640 | tf_op jit(solution)/shard_map/ppermute | solution.py:384
  142.9 2.9 %collective-permute-done.10.refs_2_ = bf16[384,256]{1,0:T(8,128)(2,1)S(1)} collective-permute-done((bf16[384,256]{1,0:T(8,128)(2,1)}, bf16[384,256]{1,0:T(8,128)(2,1)S(1)}, u32[]{:S(2)}, u32[]{:S(2)}) %collective-permute-start.10) | collective-permute-done | bytes 196640 | tf_op jit(solution)/shard_map/ppermute | solution.py:384
  149.6 2.3 %mix.1 = bf16[128,1024]{1,0:T(8,128)(2,1)} custom-call(bf16[2,3,256,128]{3,2,1,0:T(8,128)(2,1)} %get-tuple-element.43.place_ref, bf16[32,96,128]{2,1,0:T(8,128)(2,1)S(1)} %all-to-all-done.3.back_ref, bf16[128,1024]{1,0:T(8,128)(2,1)} %get-tuple-element.60.attended_ref, f32[2,128]{1,0:T(2,128)} %bitcast.29), custom_call_target="tpu_custom_call" | custom-call | tf_op jit(solution)/shard_map/mix/pallas_call | solution.py:534
  151.9 15.0 %reduce-scatter.2.cloned.1.call-done.sums_ref = bf16[128,4096]{1,0:T(8,128)(2,1)} async-done(((bf16[1024,4096]{1,0:T(8,128)(2,1)}), bf16[128,4096]{1,0:T(8,128)(2,1)}) %reduce-scatter.2.cloned.1.call-update) | async-done | bytes 1048592 | tf_op jit(solution)/shard_map/reduce_scatter | solution.py:490
  166.8 2.8 %widen.1 = (f32[128,2048]{1,0:T(8,128)}, f32[2048,128]{1,0:T(8,128)}) custom-call(bf16[128,4096]{1,0:T(8,128)(2,1)} %reduce-scatter.2.cloned.1.call-done.sums_ref), custom_call_target="tpu_custom_call" | custom-call | tf_op jit(solution)/shard_map/widen/pallas_call | solution.py:549
  (36 shorter events, 20.2 us)
Async XLA Ops:
  9.3 20.4 %collective-permute-start = (bf16[384,256]{1,0:T(8,128)(2,1)}, bf16[384,256]{1,0:T(8,128)(2,1)S(1)}, u32[]{:S(2)}, u32[]{:S(2)}) collective-permute-start(bf16[384,256]{1,0:T(8,128)(2,1)} %get-tuple-element.44), channel_id=1, source_target_pairs={{0,32},{32,64},{64,96},{96,0},{1,33},{33,65},{65,97},{97,1},{2,34}... | collective-permute-start | bytes 589832 | tf_op jit(solution)/shard_map/ppermute | solution.py:384
  10.8 18.8 %collective-permute-start.1 = (bf16[384,256]{1,0:T(8,128)(2,1)}, bf16[384,256]{1,0:T(8,128)(2,1)S(1)}, u32[]{:S(2)}, u32[]{:S(2)}) collective-permute-start(bf16[384,256]{1,0:T(8,128)(2,1)} %get-tuple-element.45), channel_id=1, source_target_pairs={{0,64},{32,96},{64,0},{96,32},{1,65},{33,97},{65,1},{97,33},{2,66}... | collective-permute-start | bytes 589832 | tf_op jit(solution)/shard_map/ppermute | solution.py:384
  13.7 15.9 %collective-permute-start.2 = (bf16[384,256]{1,0:T(8,128)(2,1)}, bf16[384,256]{1,0:T(8,128)(2,1)S(1)}, u32[]{:S(2)}, u32[]{:S(2)}) collective-permute-start(bf16[384,256]{1,0:T(8,128)(2,1)} %get-tuple-element.46), channel_id=1, source_target_pairs={{0,96},{32,0},{64,32},{96,64},{1,97},{33,1},{65,33},{97,65},{2,98}... | collective-permute-start | bytes 589832 | tf_op jit(solution)/shard_map/ppermute | solution.py:384
  17.9 31.6 %all-to-all-start.1 = ((bf16[32,96,128]{2,1,0:T(8,128)(2,1)}), bf16[32,96,128]{2,1,0:T(8,128)(2,1)}, u32[]{:S(2)}, u32[]{:S(2)}) async-start(bf16[32,96,128]{2,1,0:T(8,128)(2,1)} %get-tuple-element.52), calls=%async_computation.1 | async-start | bytes 1572864 | tf_op jit(solution)/shard_map/all_to_all | solution.py:387
  29.6 5.5 %copy-start = (bf16[384,256]{1,0:T(8,128)(2,1)}, bf16[384,256]{1,0:T(8,128)(2,1)S(1)}, u32[]{:S(2)}) copy-start(bf16[384,256]{1,0:T(8,128)(2,1)S(1)} %collective-permute-done.refs_1_) | copy-start | bytes 589828
  29.6 5.5 %copy-start.2 = (bf16[384,256]{1,0:T(8,128)(2,1)}, bf16[384,256]{1,0:T(8,128)(2,1)S(1)}, u32[]{:S(2)}) copy-start(bf16[384,256]{1,0:T(8,128)(2,1)S(1)} %collective-permute-done.1.refs_2_) | copy-start | bytes 589828
  29.7 5.5 %copy-start.4 = (bf16[384,256]{1,0:T(8,128)(2,1)}, bf16[384,256]{1,0:T(8,128)(2,1)S(1)}, u32[]{:S(2)}) copy-start(bf16[384,256]{1,0:T(8,128)(2,1)S(1)} %collective-permute-done.2.refs_3_) | copy-start | bytes 589828
  35.1 4.6 %collective-permute-start.3 = (bf16[128,256]{1,0:T(8,128)(2,1)}, bf16[128,256]{1,0:T(8,128)(2,1)S(1)}, u32[]{:S(2)}, u32[]{:S(2)}) collective-permute-start(bf16[128,256]{1,0:T(8,128)(2,1)} %get-tuple-element.48), channel_id=1, source_target_pairs={{0,96},{32,0},{64,32},{96,64},{1,97},{33,1},{65,33},{97,65},{2,98}... | collective-permute-start | bytes 196616 | tf_op jit(solution)/shard_map/ppermute | solution.py:384
  35.2 6.2 %collective-permute-start.4 = (bf16[128,256]{1,0:T(8,128)(2,1)}, bf16[128,256]{1,0:T(8,128)(2,1)S(1)}, u32[]{:S(2)}, u32[]{:S(2)}) collective-permute-start(bf16[128,256]{1,0:T(8,128)(2,1)} %get-tuple-element.49), channel_id=1, source_target_pairs={{0,64},{32,96},{64,0},{96,32},{1,65},{33,97},{65,1},{97,33},{2,66}... | collective-permute-start | bytes 196616 | tf_op jit(solution)/shard_map/ppermute | solution.py:384
  38.0 5.7 %collective-permute-start.5 = (bf16[128,256]{1,0:T(8,128)(2,1)}, bf16[128,256]{1,0:T(8,128)(2,1)S(1)}, u32[]{:S(2)}, u32[]{:S(2)}) collective-permute-start(bf16[128,256]{1,0:T(8,128)(2,1)} %get-tuple-element.50), channel_id=1, source_target_pairs={{0,32},{32,64},{64,96},{96,0},{1,33},{33,65},{65,97},{97,1},{2,34}... | collective-permute-start | bytes 196616 | tf_op jit(solution)/shard_map/ppermute | solution.py:384
  49.6 27.0 %all-to-all-start = ((bf16[32,96,128]{2,1,0:T(8,128)(2,1)}), bf16[32,96,128]{2,1,0:T(8,128)(2,1)S(1)}, u32[]{:S(2)}, u32[]{:S(2)}) async-start(bf16[32,96,128]{2,1,0:T(8,128)(2,1)} %get-tuple-element.51), calls=%async_computation | async-start | bytes 1572864 | tf_op jit(solution)/shard_map/all_to_all | solution.py:387
  86.2 27.1 %all-to-all-start.2 = ((bf16[32,96,128]{2,1,0:T(8,128)(2,1)}), bf16[32,96,128]{2,1,0:T(8,128)(2,1)S(1)}, u32[]{:S(2)}, u32[]{:S(2)}) async-start(bf16[32,96,128]{2,1,0:T(8,128)(2,1)} %get-tuple-element.54), calls=%async_computation.2 | async-start | bytes 1572864 | tf_op jit(solution)/shard_map/all_to_all | solution.py:387
  93.7 73.1 %reduce-scatter.2.cloned.1.call-start = ((), (), s32[]{:S(2)}) async-start(), calls=%async_computation.5 | async-start | bytes 9437184 | tf_op jit(solution)/shard_map/reduce_scatter | solution.py:490
  113.4 13.5 %copy-start.1 = (bf16[384,256]{1,0:T(8,128)(2,1)S(1)}, bf16[384,256]{1,0:T(8,128)(2,1)}, u32[]{:S(2)}) copy-start(bf16[384,256]{1,0:T(8,128)(2,1)} %copy-done) | copy-start | bytes 589828
  113.4 13.5 %copy-start.3 = (bf16[384,256]{1,0:T(8,128)(2,1)S(1)}, bf16[384,256]{1,0:T(8,128)(2,1)}, u32[]{:S(2)}) copy-start(bf16[384,256]{1,0:T(8,128)(2,1)} %copy-done.2) | copy-start | bytes 589828
  113.4 13.6 %copy-start.5 = (bf16[384,256]{1,0:T(8,128)(2,1)S(1)}, bf16[384,256]{1,0:T(8,128)(2,1)}, u32[]{:S(2)}) copy-start(bf16[384,256]{1,0:T(8,128)(2,1)} %copy-done.4) | copy-start | bytes 589828
  115.9 11.0 %collective-permute-start.6 = (bf16[128,256]{1,0:T(8,128)(2,1)}, bf16[128,256]{1,0:T(8,128)(2,1)S(1)}, u32[]{:S(2)}, u32[]{:S(2)}) collective-permute-start(bf16[128,256]{1,0:T(8,128)(2,1)} %get-tuple-element.63), channel_id=1, source_target_pairs={{0,32},{32,64},{64,96},{96,0},{1,33},{33,65},{65,97},{97,1},{2,34}... | collective-permute-start | bytes 196616 | tf_op jit(solution)/shard_map/ppermute | solution.py:384
  116.7 10.2 %collective-permute-start.7 = (bf16[128,256]{1,0:T(8,128)(2,1)}, bf16[128,256]{1,0:T(8,128)(2,1)S(1)}, u32[]{:S(2)}, u32[]{:S(2)}) collective-permute-start(bf16[128,256]{1,0:T(8,128)(2,1)} %get-tuple-element.64), channel_id=1, source_target_pairs={{0,64},{32,96},{64,0},{96,32},{1,65},{33,97},{65,1},{97,33},{2,66}... | collective-permute-start | bytes 196616 | tf_op jit(solution)/shard_map/ppermute | solution.py:384
  117.8 9.2 %collective-permute-start.8 = (bf16[128,256]{1,0:T(8,128)(2,1)}, bf16[128,256]{1,0:T(8,128)(2,1)S(1)}, u32[]{:S(2)}, u32[]{:S(2)}) collective-permute-start(bf16[128,256]{1,0:T(8,128)(2,1)} %get-tuple-element.65), channel_id=1, source_target_pairs={{0,96},{32,0},{64,32},{96,64},{1,97},{33,1},{65,33},{97,65},{2,98}... | collective-permute-start | bytes 196616 | tf_op jit(solution)/shard_map/ppermute | solution.py:384
  119.4 30.2 %all-to-all-start.3 = ((bf16[32,96,128]{2,1,0:T(8,128)(2,1)}), bf16[32,96,128]{2,1,0:T(8,128)(2,1)S(1)}, u32[]{:S(2)}, u32[]{:S(2)}) async-start(bf16[32,96,128]{2,1,0:T(8,128)(2,1)} %expert_out.1), calls=%async_computation.3 | async-start | bytes 1572864 | tf_op jit(solution)/shard_map/all_to_all | solution.py:387
  132.6 10.2 %collective-permute-start.9 = (bf16[384,256]{1,0:T(8,128)(2,1)}, bf16[384,256]{1,0:T(8,128)(2,1)S(1)}, u32[]{:S(2)}, u32[]{:S(2)}) collective-permute-start(bf16[384,256]{1,0:T(8,128)(2,1)} %get-tuple-element.68), channel_id=1, source_target_pairs={{0,96},{32,0},{64,32},{96,64},{1,97},{33,1},{65,33},{97,65},{2,98}... | collective-permute-start | bytes 589832 | tf_op jit(solution)/shard_map/ppermute | solution.py:384
  134.0 11.7 %collective-permute-start.10 = (bf16[384,256]{1,0:T(8,128)(2,1)}, bf16[384,256]{1,0:T(8,128)(2,1)S(1)}, u32[]{:S(2)}, u32[]{:S(2)}) collective-permute-start(bf16[384,256]{1,0:T(8,128)(2,1)} %get-tuple-element.69), channel_id=1, source_target_pairs={{0,64},{32,96},{64,0},{96,32},{1,65},{33,97},{65,1},{97,33},{2,66}... | collective-permute-start | bytes 589832 | tf_op jit(solution)/shard_map/ppermute | solution.py:384
  135.4 12.3 %collective-permute-start.11 = (bf16[384,256]{1,0:T(8,128)(2,1)}, bf16[384,256]{1,0:T(8,128)(2,1)S(1)}, u32[]{:S(2)}, u32[]{:S(2)}) collective-permute-start(bf16[384,256]{1,0:T(8,128)(2,1)} %get-tuple-element.70), channel_id=1, source_target_pairs={{0,32},{32,64},{64,96},{96,0},{1,33},{33,65},{65,97},{97,1},{2,34}... | collective-permute-start | bytes 589832 | tf_op jit(solution)/shard_map/ppermute | solution.py:384
Sparse Core Ops, SparseCore 0:
  103.1 63.6 reduce-scatter.1

commit v4 on v3

--- a/solution.py
+++ b/solution.py
@@ -77,8 +77,9 @@
             scores = dot(pieces[step][0:rows, lanes], keys[:, lanes], NT) * scaling
             exponent = jnp.exp(scores - jnp.max(scores, axis=-1, keepdims=True))
             probs = exponent / jnp.sum(exponent, axis=-1, keepdims=True)
-            probs_ref[head, step * rows:(step + 1) * rows, :] = probs
-            outs[step][:, lanes] = dot(probs.astype(BF), values[:, lanes]).astype(BF)
+            rounded = probs.astype(BF)
+            probs_ref[head, step * rows:(step + 1) * rows, :] = rounded
+            outs[step][:, lanes] = dot(rounded, values[:, lanes]).astype(BF)
 
 
 def attend_back_kernel(parts, *refs):
@@ -98,13 +99,14 @@
         for step in range(parts):
             query = pieces[step][0:rows, lanes]
             grad = grads[step][:, lanes]
-            probs = probs_ref[head, step * rows:(step + 1) * rows, :]
+            rounded = probs_ref[head, step * rows:(step + 1) * rows, :]
+            probs = rounded.astype(F32)
             grad_probs = dot(grad, values[:, lanes], NT)
             delta = jnp.sum(probs * grad_probs, axis=-1, keepdims=True)
             grad_scores = (probs * (grad_probs - delta) * scaling).astype(BF)
             outs[step][0:rows, lanes] = dot(grad_scores, keys[:, lanes]).astype(BF)
             key_part = dot(grad_scores, query, TN)
-            value_part = dot(probs.astype(BF), grad, TN)
+            value_part = dot(rounded, grad, TN)
             if step == 0:
                 grad_keys[:, lanes] = key_part
                 grad_values[:, lanes] = value_part
@@ -363,6 +365,13 @@
     up_out[...] = sums_ref[:, hidden:].astype(F32)
 
 
+def finish_kernel(parts, me_ref, sums_ref, place_ref, back_ref, attended_ref, gates_ref, *refs):
+    pieces, outs = refs[:parts], refs[parts:]
+    widen_kernel(sums_ref, *outs[4:])
+    mix_kernel(place_ref, back_ref, attended_ref, gates_ref, outs[0])
+    join_kernel(parts, me_ref, *pieces, *outs[1:4])
+
+
 def shards(query, key, value, routes, gates, up, down, cotangent):
     tokens, model = query.shape[1:]
     owners = lax.axis_size("expert")
@@ -416,7 +425,7 @@
 
     attended_pieces = pl.pallas_call(
         functools.partial(attend_kernel, parts),
-        out_shape=[single] * parts + [sds((heads, length, length), F32)],
+        out_shape=[single] * parts + [sds((heads, length, length), BF)],
         in_specs=[VMEM] * parts,
         out_specs=[VMEM] * (parts + 1),
         scratch_shapes=[pltpu.VMEM((length, width), BF)] * 2,
@@ -501,6 +510,7 @@
         out_specs=whole_wire,
         scratch_shapes=[pltpu.VMEM((slots, model), F32)],
         compiler_params=BIG,
+        cost_estimate=HEAVY,
         name="expert_out",
     )(both_late, down)
 
@@ -511,7 +521,6 @@
         in_specs=[SMEM] + [VMEM] * 4,
         out_specs=[VMEM] * parts,
         scratch_shapes=[pltpu.VMEM((tokens, model), BF)],
-        cost_estimate=HEAVY,
         name="dattended",
     )(me, place, dnormed_back, attended, cot)
     grad_pieces = exchange(grad_pieces, 1)
@@ -531,28 +540,15 @@
     )(*pieces, *grad_pieces, probs)
     back_pieces = exchange(back_pieces, -1)
 
-    layer_output = pl.pallas_call(
-        mix_kernel,
-        out_shape=sds((tokens, model), BF),
-        in_specs=[VMEM] * 4,
-        out_specs=VMEM,
-        name="mix",
-    )(place, produced_back, attended, gate)
-    grad_queries, grad_keys, grad_values = pl.pallas_call(
-        functools.partial(join_kernel, parts),
-        out_shape=[sds((tokens, model), BF)] * 3,
-        in_specs=[SMEM] + [VMEM] * parts,
-        out_specs=[VMEM] * 3,
-        name="join_grads",
-    )(me, *back_pieces)
     band = model // (pairs * parts)
-    grad_up, grad_down = pl.pallas_call(
-        widen_kernel,
-        out_shape=[sds((band, hidden), F32), sds((hidden, band), F32)],
-        in_specs=[VMEM],
-        out_specs=[VMEM] * 2,
-        name="widen",
-    )(sums)
+    layer_output, grad_queries, grad_keys, grad_values, grad_up, grad_down = pl.pallas_call(
+        functools.partial(finish_kernel, parts),
+        out_shape=[sds((tokens, model), BF)] * 4 + [sds((band, hidden), F32), sds((hidden, band), F32)],
+        in_specs=[SMEM] + [VMEM] * (parts + 5),
+        out_specs=[VMEM] * 6,
+        compiler_params=BIG,
+        name="finish",
+    )(me, sums, place, produced_back, attended, gate, *back_pieces)
     return (
         layer_output[None],
         grad_queries[None],

time: 179 us -> 169 us (0.944); the launches traced: 176 us -> 168 us
  waiting for transfers between devices: 52.7 us -> 48.4 us
  Pallas kernels: 59.1 us -> 55.4 us
    reduce_scatter x1, waiting for transfers between devices: 15 us -> 1.51 us  [shards(): lax.psum_scatter(partial_grads, ('seq', 'dp'), scatter_dimension=0, tiled...]
    all_to_all x4, waiting for transfers between devices: 21.1 us -> 30.3 us  [swap(): lax.all_to_all(packed, 'expert', split_axis=0, concat_axis=0, tiled=True)]
    pallas_call x3 -> x1, Pallas kernels: 6.95 us -> 3.67 us  [shards(): pl.pallas_call(functools.partial(finish_kernel, parts), out_shape=[sds((t...]
  transfers between devices with their start and end apart: 17 -> 17, of which waited for: 10 -> 10; matrix products, arithmetic and copies ran while one was open for 0% -> 0% of each run, Pallas kernels for 25% -> 18%
where the time goes in v4:
time: 169 us; the launch traced here: 168 us
  Pallas kernels  55.4 us (33%)
  starting transfers between devices  50.5 us (30%)
  waiting for transfers between devices  48.4 us (29%)
  between operations  14.2 us (8%)
    all_to_all x4, starting transfers between devices, swap(): lax.all_to_all(packed, 'expert', split_axis=0, concat_axis=0, tiled=True)  34 us
    all_to_all x4, waiting for transfers between devices, swap(): lax.all_to_all(packed, 'expert', split_axis=0, concat_axis=0, tiled=True)  30.3 us
    ppermute x12, waiting for transfers between devices, shift(): return near(lax.ppermute(piece, 'seq', pairs_of))  16.5 us
    ppermute x12, starting transfers between devices, shift(): return near(lax.ppermute(piece, 'seq', pairs_of))  16.3 us
    pallas_call x1, Pallas kernels, shards(): pl.pallas_call(expert_kernel, grid=(blocks,), out_shape=[sds((2, slots, h...  9.61 us
    pallas_call x1, Pallas kernels, shards(): pl.pallas_call(functools.partial(weight_grad_kernel, pairs, parts, 2), gr...  9 us
    pallas_call x1, Pallas kernels, shards(): pl.pallas_call(out_kernel, grid=(blocks,), out_shape=wire, in_specs=[pl.B...  6.47 us
    pallas_call x1, Pallas kernels, shards(): pl.pallas_call(functools.partial(dact_kernel, pairs, parts), grid=(blocks...  6.21 us
  transfers between devices with their start and end apart: 17, of which 10 were waited for; matrix products, arithmetic and copies ran while one was open for 0% of the time, Pallas kernels for 18%

profile of v4, /device:TPU:2, one launch (start us, length us, event | category | flops | bytes accessed | tf_op | source)
XLA Modules:
  0.0 168.5 jit_solution(4924952421710075695)
XLA Ops:
  7.2 2.1 %split_qkv.1 = (bf16[384,256]{1,0:T(8,128)(2,1)}, bf16[384,256]{1,0:T(8,128)(2,1)}, bf16[384,256]{1,0:T(8,128)(2,1)}, bf16[384,256]{1,0:T(8,128)(2,1)}) custom-call(s32[1]{0:T(128)} %bitcast.me_ref, bf16[128,1024]{1,0:T(8,128)(2,1)} %bitcast.24, bf16[128,1024]{1,0:T(8,128)(2,1)} %bitcast.25, bf16[128,1024]{1,0:T(8,128)(2,1)} %bitcast.26), custom_call_target="tpu_custom_call" | custom-call | tf_op jit(solution)/shard_map/split_qkv/pallas_call | solution.py:407
  10.8 2.9 %collective-permute-start.1 = (bf16[384,256]{1,0:T(8,128)(2,1)}, bf16[384,256]{1,0:T(8,128)(2,1)S(1)}, u32[]{:S(2)}, u32[]{:S(2)}) collective-permute-start(bf16[384,256]{1,0:T(8,128)(2,1)} %get-tuple-element.46), channel_id=1, source_target_pairs={{0,64},{32,96},{64,0},{96,32},{1,65},{33,97},{65,1},{97,33},{2,66}... | collective-permute-start | bytes 589832 | tf_op jit(solution)/shard_map/ppermute | solution.py:393
  15.1 2.8 %place.1 = (bf16[2,3,256,128]{3,2,1,0:T(8,128)(2,1)}, bf16[32,96,128]{2,1,0:T(8,128)(2,1)}) custom-call(s32[2,128]{1,0:T(2,128)} %bitcast.29, f32[2,128]{1,0:T(2,128)} %bitcast.27, bf16[128,1024]{1,0:T(8,128)(2,1)} %bitcast.22), custom_call_target="tpu_custom_call" | custom-call | tf_op jit(solution)/shard_map/place/pallas_call | solution.py:417
  17.9 11.7 %all-to-all-start.1 = ((bf16[32,96,128]{2,1,0:T(8,128)(2,1)}), bf16[32,96,128]{2,1,0:T(8,128)(2,1)}, u32[]{:S(2)}, u32[]{:S(2)}) async-start(bf16[32,96,128]{2,1,0:T(8,128)(2,1)} %get-tuple-element.53), calls=%async_computation.1 | async-start | bytes 1572864 | tf_op jit(solution)/shard_map/all_to_all | solution.py:396
  29.7 5.0 %attend.1 = (bf16[128,256]{1,0:T(8,128)(2,1)}, bf16[128,256]{1,0:T(8,128)(2,1)}, bf16[128,256]{1,0:T(8,128)(2,1)}, bf16[128,256]{1,0:T(8,128)(2,1)}, bf16[2,512,512]{2,1,0:T(8,128)(2,1)}) custom-call(bf16[384,256]{1,0:T(8,128)(2,1)} %get-tuple-element.42.refs_0_, bf16[384,256]{1,0:T(8,128)(2,1)S(1)} %collective-permute-done.refs_1_, ...), custom_call_target="tpu_custom_call" | custom-call | flops 999999995904 | bytes 1000000 | tf_op jit(solution)/shard_map/attend/pallas_call | solution.py:426
  34.8 2.7 %collective-permute-start.4 = (bf16[128,256]{1,0:T(8,128)(2,1)}, bf16[128,256]{1,0:T(8,128)(2,1)S(1)}, u32[]{:S(2)}, u32[]{:S(2)}) collective-permute-start(bf16[128,256]{1,0:T(8,128)(2,1)} %get-tuple-element.50), channel_id=1, source_target_pairs={{0,64},{32,96},{64,0},{96,32},{1,65},{33,97},{65,1},{97,33},{2,66}... | collective-permute-start | bytes 196616 | tf_op jit(solution)/shard_map/ppermute | solution.py:393
  41.0 2.2 %collective-permute-done.5.refs_3_ = bf16[128,256]{1,0:T(8,128)(2,1)S(1)} collective-permute-done((bf16[128,256]{1,0:T(8,128)(2,1)}, bf16[128,256]{1,0:T(8,128)(2,1)S(1)}, u32[]{:S(2)}, u32[]{:S(2)}) %collective-permute-start.5) | collective-permute-done | bytes 65568 | tf_op jit(solution)/shard_map/ppermute | solution.py:393
  43.2 2.5 %norm_pack.1 = (bf16[128,1024]{1,0:T(8,128)(2,1)}, bf16[32,96,128]{2,1,0:T(8,128)(2,1)}) custom-call(s32[1]{0:T(128)} %bitcast.me_ref, bf16[2,3,256,128]{3,2,1,0:T(8,128)(2,1)} %get-tuple-element.44.place_ref, bf16[128,256]{1,0:T(8,128)(2,1)} %get-tuple-element.48.refs_0_, bf16[128,256]{1,0:T(8,128)(2,1)S(1)} %collective-permute-done.3.refs_1_, ...), custom_call_target="tpu_custom_call" | custom-call | tf_op jit(solution)/shard_map/norm_pack/pallas_call | solution.py:439
  45.7 3.9 %all-to-all-done.1.packed_ref = bf16[32,96,128]{2,1,0:T(8,128)(2,1)} async-done(((bf16[32,96,128]{2,1,0:T(8,128)(2,1)}), bf16[32,96,128]{2,1,0:T(8,128)(2,1)}, u32[]{:S(2)}, u32[]{:S(2)}) %all-to-all-start.1) | async-done | bytes 786464 | tf_op jit(solution)/shard_map/all_to_all | solution.py:396
  49.6 7.4 %all-to-all-start = ((bf16[32,96,128]{2,1,0:T(8,128)(2,1)}), bf16[32,96,128]{2,1,0:T(8,128)(2,1)S(1)}, u32[]{:S(2)}, u32[]{:S(2)}) async-start(bf16[32,96,128]{2,1,0:T(8,128)(2,1)} %get-tuple-element.52), calls=%async_computation | async-start | bytes 1572864 | tf_op jit(solution)/shard_map/all_to_all | solution.py:396
  57.2 6.2 %dact.1 = (f32[384,2048]{1,0:T(8,128)}, bf16[1024,384]{1,0:T(8,128)(2,1)}) custom-call(bf16[32,96,128]{2,1,0:T(8,128)(2,1)} %all-to-all-done.1.packed_ref, bf16[2048,1024]{1,0:T(8,128)(2,1)} %bitcast.19), custom_call_target="tpu_custom_call" | custom-call | tf_op jit(solution)/shard_map/dact/pallas_call | solution.py:451
  63.4 13.2 %all-to-all-done.packed_ref = bf16[32,96,128]{2,1,0:T(8,128)(2,1)S(1)} async-done(((bf16[32,96,128]{2,1,0:T(8,128)(2,1)}), bf16[32,96,128]{2,1,0:T(8,128)(2,1)S(1)}, u32[]{:S(2)}, u32[]{:S(2)}) %all-to-all-start) | async-done | bytes 786464 | tf_op jit(solution)/shard_map/all_to_all | solution.py:396
  76.6 9.6 %expert.1 = (bf16[2,384,2048]{2,1,0:T(8,128)(2,1)}, bf16[384,1024]{1,0:T(8,128)(2,1)}, bf16[32,96,128]{2,1,0:T(8,128)(2,1)}) custom-call(bf16[32,96,128]{2,1,0:T(8,128)(2,1)S(1)} %all-to-all-done.packed_ref, bf16[1024,2048]{1,0:T(8,128)(2,1)} %bitcast.21, f32[384,2048]{1,0:T(8,128)} %get-tuple-element.54.dact_ref), custom_call_target="tpu_custom_call" | custom-call | tf_op jit(solution)/shard_map/expert/pallas_call | solution.py:464
  86.2 9.0 %weight_grads.1 = bf16[1024,4096]{1,0:T(8,128)(2,1)} custom-call(bf16[2,384,2048]{2,1,0:T(8,128)(2,1)} %get-tuple-element.59.hidden_ref, bf16[1024,384]{1,0:T(8,128)(2,1)} %get-tuple-element.56.turned_ref, bf16[384,1024]{1,0:T(8,128)(2,1)} %get-tuple-element.57.rows_ref), custom_call_target="tpu_custom_call" | custom-call | tf_op jit(solution)/shard_map/weight_grads/pallas_call | solution.py:485
  95.3 7.5 %all-to-all-start.2 = ((bf16[32,96,128]{2,1,0:T(8,128)(2,1)}), bf16[32,96,128]{2,1,0:T(8,128)(2,1)}, u32[]{:S(2)}, u32[]{:S(2)}) async-start(bf16[32,96,128]{2,1,0:T(8,128)(2,1)} %get-tuple-element.58), calls=%async_computation.3 | async-start | bytes 1572864 | tf_op jit(solution)/shard_map/all_to_all | solution.py:396
  102.8 6.5 %expert_out.1 = bf16[32,96,128]{2,1,0:T(8,128)(2,1)} custom-call(bf16[2,384,2048]{2,1,0:T(8,128)(2,1)} %get-tuple-element.59.hidden_ref, bf16[2048,1024]{1,0:T(8,128)(2,1)} %bitcast.20), custom_call_target="tpu_custom_call" | custom-call | flops 999999995904 | bytes 1000000 | tf_op jit(solution)/shard_map/expert_out/pallas_call | solution.py:502
  109.3 13.2 %all-to-all-done.2.back_ref = bf16[32,96,128]{2,1,0:T(8,128)(2,1)} async-done(((bf16[32,96,128]{2,1,0:T(8,128)(2,1)}), bf16[32,96,128]{2,1,0:T(8,128)(2,1)}, u32[]{:S(2)}, u32[]{:S(2)}) %all-to-all-start.2) | async-done | bytes 786464 | tf_op jit(solution)/shard_map/all_to_all | solution.py:396
  122.5 2.6 %dattended.1 = (bf16[128,256]{1,0:T(8,128)(2,1)}, bf16[128,256]{1,0:T(8,128)(2,1)}, bf16[128,256]{1,0:T(8,128)(2,1)}, bf16[128,256]{1,0:T(8,128)(2,1)}) custom-call(s32[1]{0:T(128)} %bitcast.me_ref, bf16[2,3,256,128]{3,2,1,0:T(8,128)(2,1)} %get-tuple-element.44.place_ref, bf16[32,96,128]{2,1,0:T(8,128)(2,1)} %all-to-all-done.2.back_ref, ...), custom_call_target="tpu_custom_call" | custom-call | tf_op jit(solution)/shard_map/dattended/pallas_call | solution.py:518
  128.6 7.5 %all-to-all-start.3 = ((bf16[32,96,128]{2,1,0:T(8,128)(2,1)}), bf16[32,96,128]{2,1,0:T(8,128)(2,1)S(1)}, u32[]{:S(2)}, u32[]{:S(2)}) async-start(bf16[32,96,128]{2,1,0:T(8,128)(2,1)} %expert_out.1), calls=%async_computation.4 | async-start | bytes 1572864 | tf_op jit(solution)/shard_map/all_to_all | solution.py:396
  136.1 5.3 %attend_back.1 = (bf16[384,256]{1,0:T(8,128)(2,1)}, bf16[384,256]{1,0:T(8,128)(2,1)}, bf16[384,256]{1,0:T(8,128)(2,1)}, bf16[384,256]{1,0:T(8,128)(2,1)}) custom-call(bf16[384,256]{1,0:T(8,128)(2,1)} %get-tuple-element.42.refs_0_, bf16[384,256]{1,0:T(8,128)(2,1)S(1)} %copy-done.1, bf16[384,256]{1,0:T(8,128)(2,1)S(1)} %copy-done.3, ...), custom_call_target="tpu_custom_call" | custom-call | flops 40000000000 | bytes 1000000 | tf_op jit(solution)/shard_map/attend_back/pallas_call | solution.py:530
  145.6 6.0 %collective-permute-done.9.refs_1_ = bf16[384,256]{1,0:T(8,128)(2,1)S(1)} collective-permute-done((bf16[384,256]{1,0:T(8,128)(2,1)}, bf16[384,256]{1,0:T(8,128)(2,1)S(1)}, u32[]{:S(2)}, u32[]{:S(2)}) %collective-permute-start.9) | collective-permute-done | bytes 196640 | tf_op jit(solution)/shard_map/ppermute | solution.py:393
  151.6 2.9 %collective-permute-done.10.refs_2_ = bf16[384,256]{1,0:T(8,128)(2,1)S(1)} collective-permute-done((bf16[384,256]{1,0:T(8,128)(2,1)}, bf16[384,256]{1,0:T(8,128)(2,1)S(1)}, u32[]{:S(2)}, u32[]{:S(2)}) %collective-permute-start.10) | collective-permute-done | bytes 196640 | tf_op jit(solution)/shard_map/ppermute | solution.py:393
  154.5 1.9 %collective-permute-done.11.refs_3_ = bf16[384,256]{1,0:T(8,128)(2,1)S(1)} collective-permute-done((bf16[384,256]{1,0:T(8,128)(2,1)}, bf16[384,256]{1,0:T(8,128)(2,1)S(1)}, u32[]{:S(2)}, u32[]{:S(2)}) %collective-permute-start.11) | collective-permute-done | bytes 196640 | tf_op jit(solution)/shard_map/ppermute | solution.py:393
  157.9 3.7 %finish.1 = (bf16[128,1024]{1,0:T(8,128)(2,1)}, bf16[128,1024]{1,0:T(8,128)(2,1)}, bf16[128,1024]{1,0:T(8,128)(2,1)}, bf16[128,1024]{1,0:T(8,128)(2,1)}, f32[128,2048]{1,0:T(8,128)}, /*index=5*/f32[2048,128]{1,0:T(8,128)}) custom-call(s32[1]{0:T(128)} %bitcast.me_ref, bf16[128,4096]{1,0:T(8,128)(2,1)} %reduce-scatter.2.cloned.1.call-done.sums_ref, ...), custom_call_target="tpu_custom_call" | custom-call | tf_op jit(solution)/shard_map/finish/pallas_call | solution.py:544
  (34 shorter events, 15.9 us)
Async XLA Ops:
  9.3 20.4 %collective-permute-start = (bf16[384,256]{1,0:T(8,128)(2,1)}, bf16[384,256]{1,0:T(8,128)(2,1)S(1)}, u32[]{:S(2)}, u32[]{:S(2)}) collective-permute-start(bf16[384,256]{1,0:T(8,128)(2,1)} %get-tuple-element.45), channel_id=1, source_target_pairs={{0,32},{32,64},{64,96},{96,0},{1,33},{33,65},{65,97},{97,1},{2,34}... | collective-permute-start | bytes 589832 | tf_op jit(solution)/shard_map/ppermute | solution.py:393
  10.8 18.8 %collective-permute-start.1 = (bf16[384,256]{1,0:T(8,128)(2,1)}, bf16[384,256]{1,0:T(8,128)(2,1)S(1)}, u32[]{:S(2)}, u32[]{:S(2)}) collective-permute-start(bf16[384,256]{1,0:T(8,128)(2,1)} %get-tuple-element.46), channel_id=1, source_target_pairs={{0,64},{32,96},{64,0},{96,32},{1,65},{33,97},{65,1},{97,33},{2,66}... | collective-permute-start | bytes 589832 | tf_op jit(solution)/shard_map/ppermute | solution.py:393
  13.7 15.9 %collective-permute-start.2 = (bf16[384,256]{1,0:T(8,128)(2,1)}, bf16[384,256]{1,0:T(8,128)(2,1)S(1)}, u32[]{:S(2)}, u32[]{:S(2)}) collective-permute-start(bf16[384,256]{1,0:T(8,128)(2,1)} %get-tuple-element.47), channel_id=1, source_target_pairs={{0,96},{32,0},{64,32},{96,64},{1,97},{33,1},{65,33},{97,65},{2,98}... | collective-permute-start | bytes 589832 | tf_op jit(solution)/shard_map/ppermute | solution.py:393
  17.9 31.6 %all-to-all-start.1 = ((bf16[32,96,128]{2,1,0:T(8,128)(2,1)}), bf16[32,96,128]{2,1,0:T(8,128)(2,1)}, u32[]{:S(2)}, u32[]{:S(2)}) async-start(bf16[32,96,128]{2,1,0:T(8,128)(2,1)} %get-tuple-element.53), calls=%async_computation.1 | async-start | bytes 1572864 | tf_op jit(solution)/shard_map/all_to_all | solution.py:396
  29.6 5.1 %copy-start = (bf16[384,256]{1,0:T(8,128)(2,1)}, bf16[384,256]{1,0:T(8,128)(2,1)S(1)}, u32[]{:S(2)}) copy-start(bf16[384,256]{1,0:T(8,128)(2,1)S(1)} %collective-permute-done.refs_1_) | copy-start | bytes 589828
  29.6 5.1 %copy-start.2 = (bf16[384,256]{1,0:T(8,128)(2,1)}, bf16[384,256]{1,0:T(8,128)(2,1)S(1)}, u32[]{:S(2)}) copy-start(bf16[384,256]{1,0:T(8,128)(2,1)S(1)} %collective-permute-done.1.refs_2_) | copy-start | bytes 589828
  29.7 5.0 %copy-start.4 = (bf16[384,256]{1,0:T(8,128)(2,1)}, bf16[384,256]{1,0:T(8,128)(2,1)S(1)}, u32[]{:S(2)}) copy-start(bf16[384,256]{1,0:T(8,128)(2,1)S(1)} %collective-permute-done.2.refs_3_) | copy-start | bytes 589828
  34.7 4.6 %collective-permute-start.3 = (bf16[128,256]{1,0:T(8,128)(2,1)}, bf16[128,256]{1,0:T(8,128)(2,1)S(1)}, u32[]{:S(2)}, u32[]{:S(2)}) collective-permute-start(bf16[128,256]{1,0:T(8,128)(2,1)} %get-tuple-element.49), channel_id=1, source_target_pairs={{0,96},{32,0},{64,32},{96,64},{1,97},{33,1},{65,33},{97,65},{2,98}... | collective-permute-start | bytes 196616 | tf_op jit(solution)/shard_map/ppermute | solution.py:393
  34.8 6.2 %collective-permute-start.4 = (bf16[128,256]{1,0:T(8,128)(2,1)}, bf16[128,256]{1,0:T(8,128)(2,1)S(1)}, u32[]{:S(2)}, u32[]{:S(2)}) collective-permute-start(bf16[128,256]{1,0:T(8,128)(2,1)} %get-tuple-element.50), channel_id=1, source_target_pairs={{0,64},{32,96},{64,0},{96,32},{1,65},{33,97},{65,1},{97,33},{2,66}... | collective-permute-start | bytes 196616 | tf_op jit(solution)/shard_map/ppermute | solution.py:393
  37.5 5.7 %collective-permute-start.5 = (bf16[128,256]{1,0:T(8,128)(2,1)}, bf16[128,256]{1,0:T(8,128)(2,1)S(1)}, u32[]{:S(2)}, u32[]{:S(2)}) collective-permute-start(bf16[128,256]{1,0:T(8,128)(2,1)} %get-tuple-element.51), channel_id=1, source_target_pairs={{0,32},{32,64},{64,96},{96,0},{1,33},{33,65},{65,97},{97,1},{2,34}... | collective-permute-start | bytes 196616 | tf_op jit(solution)/shard_map/ppermute | solution.py:393
  49.6 27.0 %all-to-all-start = ((bf16[32,96,128]{2,1,0:T(8,128)(2,1)}), bf16[32,96,128]{2,1,0:T(8,128)(2,1)S(1)}, u32[]{:S(2)}, u32[]{:S(2)}) async-start(bf16[32,96,128]{2,1,0:T(8,128)(2,1)} %get-tuple-element.52), calls=%async_computation | async-start | bytes 1572864 | tf_op jit(solution)/shard_map/all_to_all | solution.py:396
  56.9 101.0 %reduce-scatter.2.cloned.1.call-start = ((), (), s32[]{:S(2)}) async-start(), calls=%async_computation.5 | async-start | bytes 9437184 | tf_op jit(solution)/shard_map/reduce_scatter | solution.py:499
  95.3 27.3 %all-to-all-start.2 = ((bf16[32,96,128]{2,1,0:T(8,128)(2,1)}), bf16[32,96,128]{2,1,0:T(8,128)(2,1)}, u32[]{:S(2)}, u32[]{:S(2)}) async-start(bf16[32,96,128]{2,1,0:T(8,128)(2,1)} %get-tuple-element.58), calls=%async_computation.3 | async-start | bytes 1572864 | tf_op jit(solution)/shard_map/all_to_all | solution.py:396
  102.8 33.3 %copy-start.1 = (bf16[384,256]{1,0:T(8,128)(2,1)S(1)}, bf16[384,256]{1,0:T(8,128)(2,1)}, u32[]{:S(2)}) copy-start(bf16[384,256]{1,0:T(8,128)(2,1)} %copy-done) | copy-start | bytes 589828
  102.8 33.3 %copy-start.3 = (bf16[384,256]{1,0:T(8,128)(2,1)S(1)}, bf16[384,256]{1,0:T(8,128)(2,1)}, u32[]{:S(2)}) copy-start(bf16[384,256]{1,0:T(8,128)(2,1)} %copy-done.2) | copy-start | bytes 589828
  102.8 33.3 %copy-start.5 = (bf16[384,256]{1,0:T(8,128)(2,1)S(1)}, bf16[384,256]{1,0:T(8,128)(2,1)}, u32[]{:S(2)}) copy-start(bf16[384,256]{1,0:T(8,128)(2,1)} %copy-done.4) | copy-start | bytes 589828
  125.2 10.9 %collective-permute-start.6 = (bf16[128,256]{1,0:T(8,128)(2,1)}, bf16[128,256]{1,0:T(8,128)(2,1)S(1)}, u32[]{:S(2)}, u32[]{:S(2)}) collective-permute-start(bf16[128,256]{1,0:T(8,128)(2,1)} %get-tuple-element.64), channel_id=1, source_target_pairs={{0,32},{32,64},{64,96},{96,0},{1,33},{33,65},{65,97},{97,1},{2,34}... | collective-permute-start | bytes 196616 | tf_op jit(solution)/shard_map/ppermute | solution.py:393
  125.8 10.2 %collective-permute-start.7 = (bf16[128,256]{1,0:T(8,128)(2,1)}, bf16[128,256]{1,0:T(8,128)(2,1)S(1)}, u32[]{:S(2)}, u32[]{:S(2)}) collective-permute-start(bf16[128,256]{1,0:T(8,128)(2,1)} %get-tuple-element.65), channel_id=1, source_target_pairs={{0,64},{32,96},{64,0},{96,32},{1,65},{33,97},{65,1},{97,33},{2,66}... | collective-permute-start | bytes 196616 | tf_op jit(solution)/shard_map/ppermute | solution.py:393
  127.1 8.9 %collective-permute-start.8 = (bf16[128,256]{1,0:T(8,128)(2,1)}, bf16[128,256]{1,0:T(8,128)(2,1)S(1)}, u32[]{:S(2)}, u32[]{:S(2)}) collective-permute-start(bf16[128,256]{1,0:T(8,128)(2,1)} %get-tuple-element.66), channel_id=1, source_target_pairs={{0,96},{32,0},{64,32},{96,64},{1,97},{33,1},{65,33},{97,65},{2,98}... | collective-permute-start | bytes 196616 | tf_op jit(solution)/shard_map/ppermute | solution.py:393
  128.6 27.9 %all-to-all-start.3 = ((bf16[32,96,128]{2,1,0:T(8,128)(2,1)}), bf16[32,96,128]{2,1,0:T(8,128)(2,1)S(1)}, u32[]{:S(2)}, u32[]{:S(2)}) async-start(bf16[32,96,128]{2,1,0:T(8,128)(2,1)} %expert_out.1), calls=%async_computation.4 | async-start | bytes 1572864 | tf_op jit(solution)/shard_map/all_to_all | solution.py:396
  141.4 10.2 %collective-permute-start.9 = (bf16[384,256]{1,0:T(8,128)(2,1)}, bf16[384,256]{1,0:T(8,128)(2,1)S(1)}, u32[]{:S(2)}, u32[]{:S(2)}) collective-permute-start(bf16[384,256]{1,0:T(8,128)(2,1)} %get-tuple-element.69), channel_id=1, source_target_pairs={{0,96},{32,0},{64,32},{96,64},{1,97},{33,1},{65,33},{97,65},{2,98}... | collective-permute-start | bytes 589832 | tf_op jit(solution)/shard_map/ppermute | solution.py:393
  142.8 11.7 %collective-permute-start.10 = (bf16[384,256]{1,0:T(8,128)(2,1)}, bf16[384,256]{1,0:T(8,128)(2,1)S(1)}, u32[]{:S(2)}, u32[]{:S(2)}) collective-permute-start(bf16[384,256]{1,0:T(8,128)(2,1)} %get-tuple-element.70), channel_id=1, source_target_pairs={{0,64},{32,96},{64,0},{96,32},{1,65},{33,97},{65,1},{97,33},{2,66}... | collective-permute-start | bytes 589832 | tf_op jit(solution)/shard_map/ppermute | solution.py:393
  144.2 12.2 %collective-permute-start.11 = (bf16[384,256]{1,0:T(8,128)(2,1)}, bf16[384,256]{1,0:T(8,128)(2,1)S(1)}, u32[]{:S(2)}, u32[]{:S(2)}) collective-permute-start(bf16[384,256]{1,0:T(8,128)(2,1)} %get-tuple-element.71), channel_id=1, source_target_pairs={{0,32},{32,64},{64,96},{96,0},{1,33},{33,65},{65,97},{97,1},{2,34}... | collective-permute-start | bytes 589832 | tf_op jit(solution)/shard_map/ppermute | solution.py:393
Sparse Core Ops, SparseCore 0:
  95.4 62.5 reduce-scatter.1

commit v5 on v4

--- a/solution.py
+++ b/solution.py
@@ -269,21 +269,25 @@
     out_ref[...] = dot(rows[...], down_ref[...], NT)
 
 
-def expert_kernel(packed_ref, up_ref, dact_ref, hidden_ref, rows_ref, dnormed_ref, total):
+def expert_kernel(pairs, parts, packed_ref, up_ref, dact_ref, grads_turned_ref, act_ref, grads_ref, dnormed_ref, rows, turned, total):
     step = pl.program_id(0)
 
     @pl.when(step == 0)
     def _():
-        unpack_rows(packed_ref, rows_ref)
-
-    pre = dot(rows_ref[...], up_ref[...])
+        unpack_rows(packed_ref, rows)
+        turn_rows(pairs, parts, rows, turned)
+
+    chunk = up_ref.shape[1]
+    pre = dot(rows[...], up_ref[...])
     square = pre * pre
     half = 0.5 + 0.5 * jnp.tanh(pre * (GELU_COEF + (GELU_COEF * 0.044715) * square))
     act = pre * half
-    hidden_ref[0] = act.astype(BF)
+    act_rounded = act.astype(BF)
+    act_ref[...] = act_rounded
     slope = half + act * (1.0 - half) * (2.0 * GELU_COEF + (6.0 * GELU_COEF * 0.044715) * square)
     dpre = (dact_ref[...] * slope).astype(BF)
-    hidden_ref[1] = dpre
+    grads_ref[:, 0:chunk] = dot(grads_turned_ref[...], act_rounded).astype(BF)
+    grads_ref[:, chunk:] = dot(turned[...], dpre).astype(BF)
     part = dot(dpre, up_ref[...], NT)
 
     @pl.when(step == 0)
@@ -297,27 +301,11 @@
     @pl.when(step == pl.num_programs(0) - 1)
     def _():
         pack_rows(total[...], dnormed_ref)
-
-
-def weight_grad_kernel(pairs, parts, blocks, hidden_ref, turned_ref, rows_ref, grads_ref, turned):
-    step = pl.program_id(0)
-
-    @pl.when(step < blocks)
-    def _():
-        grads_ref[...] = dot(turned_ref[...], hidden_ref[0]).astype(BF)
-
-    @pl.when(step == 0)
-    def _():
-        turn_rows(pairs, parts, rows_ref, turned)
-
-    @pl.when(step >= blocks)
-    def _():
-        grads_ref[...] = dot(turned[...], hidden_ref[0]).astype(BF)
 
 
 def out_kernel(hidden_ref, weight_ref, packed_ref, total):
     step = pl.program_id(0)
-    part = dot(hidden_ref[0], weight_ref[...])
+    part = dot(hidden_ref[...], weight_ref[...])
 
     @pl.when(step == 0)
     def _():
@@ -359,15 +347,18 @@
     out_ref[...] = (attended_ref[...].astype(F32) + mix).astype(BF)
 
 
-def widen_kernel(sums_ref, up_out, down_out):
-    hidden = up_out.shape[1]
-    down_out[...] = sums_ref[:, 0:hidden].astype(F32).T
-    up_out[...] = sums_ref[:, hidden:].astype(F32)
-
-
-def finish_kernel(parts, me_ref, sums_ref, place_ref, back_ref, attended_ref, gates_ref, *refs):
+def widen_kernel(blocks, sums_ref, up_out, down_out):
+    chunk = up_out.shape[1] // blocks
+    for i in range(blocks):
+        start = 2 * i * chunk
+        rows = slice(i * chunk, (i + 1) * chunk)
+        down_out[rows, :] = sums_ref[:, start:start + chunk].astype(F32).T
+        up_out[:, rows] = sums_ref[:, start + chunk:start + 2 * chunk].astype(F32)
+
+
+def finish_kernel(parts, blocks, me_ref, sums_ref, place_ref, back_ref, attended_ref, gates_ref, *refs):
     pieces, outs = refs[:parts], refs[parts:]
-    widen_kernel(sums_ref, *outs[4:])
+    widen_kernel(blocks, sums_ref, *outs[4:])
     mix_kernel(place_ref, back_ref, attended_ref, gates_ref, outs[0])
     join_kernel(parts, me_ref, *pieces, *outs[1:4])
 
@@ -461,50 +452,38 @@
         compiler_params=BIG,
         name="dact",
     )(grad_wire, down)
-    both, rows, dnormed = pl.pallas_call(
-        expert_kernel,
+    act, partial_grads, dnormed = pl.pallas_call(
+        functools.partial(expert_kernel, pairs, parts),
         grid=(blocks,),
-        out_shape=[sds((2, slots, hidden), BF), sds((slots, model), BF), wire],
+        out_shape=[sds((slots, hidden), BF), sds((model, 2 * hidden), BF), wire],
         in_specs=[
             VMEM,
             pl.BlockSpec((model, chunk), lambda i: (0, i)),
             pl.BlockSpec((slots, chunk), lambda i: (0, i)),
+            pl.BlockSpec((model, slots), lambda i: (0, 0)),
         ],
         out_specs=[
-            pl.BlockSpec((2, slots, chunk), lambda i: (0, 0, i)),
-            pl.BlockSpec((slots, model), lambda i: (0, 0)),
+            pl.BlockSpec((slots, chunk), lambda i: (0, i)),
+            pl.BlockSpec((model, 2 * chunk), lambda i: (0, i)),
             whole_wire,
         ],
-        scratch_shapes=[pltpu.VMEM((slots, model), F32)],
+        scratch_shapes=[
+            pltpu.VMEM((slots, model), BF),
+            pltpu.VMEM((model, slots), BF),
+            pltpu.VMEM((slots, model), F32),
+        ],
         compiler_params=BIG,
         name="expert",
-    )(wire_rows, up, dact)
+    )(wire_rows, up, dact, turned)
+    sums = lax.psum_scatter(partial_grads, ("seq", "dp"), scatter_dimension=0, tiled=True)
     dnormed_back = swap(dnormed)
-
-    half = hidden // 2
-    partial_grads = pl.pallas_call(
-        functools.partial(weight_grad_kernel, pairs, parts, 2),
-        grid=(4,),
-        out_shape=sds((model, 2 * hidden), BF),
-        in_specs=[
-            pl.BlockSpec((1, slots, half), lambda i: (lax.div(i, 2), 0, lax.rem(i, 2))),
-            pl.BlockSpec((model, slots), lambda i: (0, 0)),
-            pl.BlockSpec((slots, model), lambda i: (0, 0)),
-        ],
-        out_specs=pl.BlockSpec((model, half), lambda i: (0, i)),
-        scratch_shapes=[pltpu.VMEM((model, slots), BF)],
-        compiler_params=BIG,
-        name="weight_grads",
-    )(both, turned, rows)
-    sums = lax.psum_scatter(partial_grads, ("seq", "dp"), scatter_dimension=0, tiled=True)
-
-    both_late, _ = lax.optimization_barrier((both, partial_grads))
+    act_late, _ = lax.optimization_barrier((act, partial_grads))
     produced = pl.pallas_call(
         out_kernel,
         grid=(blocks,),
         out_shape=wire,
         in_specs=[
-            pl.BlockSpec((1, slots, chunk), lambda i: (0, 0, i)),
+            pl.BlockSpec((slots, chunk), lambda i: (0, i)),
             pl.BlockSpec((chunk, model), lambda i: (i, 0)),
         ],
         out_specs=whole_wire,
@@ -512,7 +491,7 @@
         compiler_params=BIG,
         cost_estimate=HEAVY,
         name="expert_out",
-    )(both_late, down)
+    )(act_late, down)
 
     dnormed_back, produced = lax.optimization_barrier((dnormed_back, produced))
     grad_pieces = pl.pallas_call(
@@ -542,7 +521,7 @@
 
     band = model // (pairs * parts)
     layer_output, grad_queries, grad_keys, grad_values, grad_up, grad_down = pl.pallas_call(
-        functools.partial(finish_kernel, parts),
+        functools.partial(finish_kernel, parts, blocks),
         out_shape=[sds((tokens, model), BF)] * 4 + [sds((band, hidden), F32), sds((hidden, band), F32)],
         in_specs=[SMEM] + [VMEM] * (parts + 5),
         out_specs=[VMEM] * 6,

time: 169 us -> 165 us (0.976)
  Pallas kernels: 55.4 us -> 51.4 us
    pallas_call x3 -> x2, Pallas kernels: 22.3 us -> 18.2 us  [the longest x1 14.5 us: shards(): pl.pallas_call(functools.partial(expert_kernel, pairs, parts), grid=(bloc...]
  transfers between devices with their start and end apart: 17 -> 17, of which waited for: 10 -> 10; matrix products, arithmetic and copies ran while one was open for 0% -> 0% of each run, Pallas kernels for 18% -> 19%
where the time goes in v5:
time: 165 us; the launch traced here: 164 us
  Pallas kernels  51.4 us (31%)
  starting transfers between devices  50.3 us (30%)
  waiting for transfers between devices  48.5 us (29%)
  between operations  14.2 us (9%)
    all_to_all x4, starting transfers between devices, swap(): lax.all_to_all(packed, 'expert', split_axis=0, concat_axis=0, tiled=True)  34 us
    all_to_all x4, waiting for transfers between devices, swap(): lax.all_to_all(packed, 'expert', split_axis=0, concat_axis=0, tiled=True)  30.5 us
    ppermute x12, waiting for transfers between devices, shift(): return near(lax.ppermute(piece, 'seq', pairs_of))  16.5 us
    ppermute x12, starting transfers between devices, shift(): return near(lax.ppermute(piece, 'seq', pairs_of))  16.3 us
    pallas_call x1, Pallas kernels, shards(): pl.pallas_call(functools.partial(expert_kernel, pairs, parts), grid=(bloc...  14.5 us
    pallas_call x1, Pallas kernels, shards(): pl.pallas_call(out_kernel, grid=(blocks,), out_shape=wire, in_specs=[pl.B...  6.47 us
    pallas_call x1, Pallas kernels, shards(): pl.pallas_call(functools.partial(dact_kernel, pairs, parts), grid=(blocks...  6.28 us
    pallas_call x1, Pallas kernels, shards(): pl.pallas_call(functools.partial(attend_back_kernel, parts), out_shape=[t...  5.32 us
  transfers between devices with their start and end apart: 17, of which 10 were waited for; matrix products, arithmetic and copies ran while one was open for 0% of the time, Pallas kernels for 19%

profile of v5, /device:TPU:2, one launch (start us, length us, event | category | flops | bytes accessed | tf_op | source)
XLA Modules:
  0.0 164.4 jit_solution(15024563537840273598)
XLA Ops:
  7.2 2.1 %split_qkv.1 = (bf16[384,256]{1,0:T(8,128)(2,1)}, bf16[384,256]{1,0:T(8,128)(2,1)}, bf16[384,256]{1,0:T(8,128)(2,1)}, bf16[384,256]{1,0:T(8,128)(2,1)}) custom-call(s32[1]{0:T(128)} %bitcast.me_ref, bf16[128,1024]{1,0:T(8,128)(2,1)} %bitcast.24, bf16[128,1024]{1,0:T(8,128)(2,1)} %bitcast.25, bf16[128,1024]{1,0:T(8,128)(2,1)} %bitcast.26), custom_call_target="tpu_custom_call" | custom-call | tf_op jit(solution)/shard_map/split_qkv/pallas_call | solution.py:398
  10.8 2.9 %collective-permute-start.1 = (bf16[384,256]{1,0:T(8,128)(2,1)}, bf16[384,256]{1,0:T(8,128)(2,1)S(1)}, u32[]{:S(2)}, u32[]{:S(2)}) collective-permute-start(bf16[384,256]{1,0:T(8,128)(2,1)} %get-tuple-element.46), channel_id=1, source_target_pairs={{0,64},{32,96},{64,0},{96,32},{1,65},{33,97},{65,1},{97,33},{2,66}... | collective-permute-start | bytes 589832 | tf_op jit(solution)/shard_map/ppermute | solution.py:384
  15.1 2.8 %place.1 = (bf16[2,3,256,128]{3,2,1,0:T(8,128)(2,1)}, bf16[32,96,128]{2,1,0:T(8,128)(2,1)}) custom-call(s32[2,128]{1,0:T(2,128)} %bitcast.29, f32[2,128]{1,0:T(2,128)} %bitcast.27, bf16[128,1024]{1,0:T(8,128)(2,1)} %bitcast.22), custom_call_target="tpu_custom_call" | custom-call | tf_op jit(solution)/shard_map/place/pallas_call | solution.py:408
  17.9 11.7 %all-to-all-start.1 = ((bf16[32,96,128]{2,1,0:T(8,128)(2,1)}), bf16[32,96,128]{2,1,0:T(8,128)(2,1)}, u32[]{:S(2)}, u32[]{:S(2)}) async-start(bf16[32,96,128]{2,1,0:T(8,128)(2,1)} %get-tuple-element.53), calls=%async_computation.1 | async-start | bytes 1572864 | tf_op jit(solution)/shard_map/all_to_all | solution.py:387
  29.7 5.0 %attend.1 = (bf16[128,256]{1,0:T(8,128)(2,1)}, bf16[128,256]{1,0:T(8,128)(2,1)}, bf16[128,256]{1,0:T(8,128)(2,1)}, bf16[128,256]{1,0:T(8,128)(2,1)}, bf16[2,512,512]{2,1,0:T(8,128)(2,1)}) custom-call(bf16[384,256]{1,0:T(8,128)(2,1)} %get-tuple-element.42.refs_0_, bf16[384,256]{1,0:T(8,128)(2,1)S(1)} %collective-permute-done.refs_1_, ...), custom_call_target="tpu_custom_call" | custom-call | flops 999999995904 | bytes 1000000 | tf_op jit(solution)/shard_map/attend/pallas_call | solution.py:417
  34.8 2.7 %collective-permute-start.4 = (bf16[128,256]{1,0:T(8,128)(2,1)}, bf16[128,256]{1,0:T(8,128)(2,1)S(1)}, u32[]{:S(2)}, u32[]{:S(2)}) collective-permute-start(bf16[128,256]{1,0:T(8,128)(2,1)} %get-tuple-element.50), channel_id=1, source_target_pairs={{0,64},{32,96},{64,0},{96,32},{1,65},{33,97},{65,1},{97,33},{2,66}... | collective-permute-start | bytes 196616 | tf_op jit(solution)/shard_map/ppermute | solution.py:384
  39.3 1.8 %collective-permute-done.4.refs_2_ = bf16[128,256]{1,0:T(8,128)(2,1)S(1)} collective-permute-done((bf16[128,256]{1,0:T(8,128)(2,1)}, bf16[128,256]{1,0:T(8,128)(2,1)S(1)}, u32[]{:S(2)}, u32[]{:S(2)}) %collective-permute-start.4) | collective-permute-done | bytes 65568 | tf_op jit(solution)/shard_map/ppermute | solution.py:384
  41.0 2.2 %collective-permute-done.5.refs_3_ = bf16[128,256]{1,0:T(8,128)(2,1)S(1)} collective-permute-done((bf16[128,256]{1,0:T(8,128)(2,1)}, bf16[128,256]{1,0:T(8,128)(2,1)S(1)}, u32[]{:S(2)}, u32[]{:S(2)}) %collective-permute-start.5) | collective-permute-done | bytes 65568 | tf_op jit(solution)/shard_map/ppermute | solution.py:384
  43.2 2.5 %norm_pack.1 = (bf16[128,1024]{1,0:T(8,128)(2,1)}, bf16[32,96,128]{2,1,0:T(8,128)(2,1)}) custom-call(s32[1]{0:T(128)} %bitcast.me_ref, bf16[2,3,256,128]{3,2,1,0:T(8,128)(2,1)} %get-tuple-element.44.place_ref, bf16[128,256]{1,0:T(8,128)(2,1)} %get-tuple-element.48.refs_0_, bf16[128,256]{1,0:T(8,128)(2,1)S(1)} %collective-permute-done.3.refs_1_, ...), custom_call_target="tpu_custom_call" | custom-call | tf_op jit(solution)/shard_map/norm_pack/pallas_call | solution.py:430
  45.7 3.8 %all-to-all-done.1.packed_ref = bf16[32,96,128]{2,1,0:T(8,128)(2,1)} async-done(((bf16[32,96,128]{2,1,0:T(8,128)(2,1)}), bf16[32,96,128]{2,1,0:T(8,128)(2,1)}, u32[]{:S(2)}, u32[]{:S(2)}) %all-to-all-start.1) | async-done | bytes 786464 | tf_op jit(solution)/shard_map/all_to_all | solution.py:387
  49.6 7.4 %all-to-all-start = ((bf16[32,96,128]{2,1,0:T(8,128)(2,1)}), bf16[32,96,128]{2,1,0:T(8,128)(2,1)S(1)}, u32[]{:S(2)}, u32[]{:S(2)}) async-start(bf16[32,96,128]{2,1,0:T(8,128)(2,1)} %get-tuple-element.52), calls=%async_computation | async-start | bytes 1572864 | tf_op jit(solution)/shard_map/all_to_all | solution.py:387
  57.0 6.3 %dact.1 = (f32[384,2048]{1,0:T(8,128)}, bf16[1024,384]{1,0:T(8,128)(2,1)}) custom-call(bf16[32,96,128]{2,1,0:T(8,128)(2,1)} %all-to-all-done.1.packed_ref, bf16[2048,1024]{1,0:T(8,128)(2,1)} %bitcast.19), custom_call_target="tpu_custom_call" | custom-call | tf_op jit(solution)/shard_map/dact/pallas_call | solution.py:442
  63.3 13.4 %all-to-all-done.packed_ref = bf16[32,96,128]{2,1,0:T(8,128)(2,1)S(1)} async-done(((bf16[32,96,128]{2,1,0:T(8,128)(2,1)}), bf16[32,96,128]{2,1,0:T(8,128)(2,1)S(1)}, u32[]{:S(2)}, u32[]{:S(2)}) %all-to-all-start) | async-done | bytes 786464 | tf_op jit(solution)/shard_map/all_to_all | solution.py:387
  76.6 14.5 %expert.1 = (bf16[384,2048]{1,0:T(8,128)(2,1)}, bf16[1024,4096]{1,0:T(8,128)(2,1)}, bf16[32,96,128]{2,1,0:T(8,128)(2,1)}) custom-call(bf16[32,96,128]{2,1,0:T(8,128)(2,1)S(1)} %all-to-all-done.packed_ref, bf16[1024,2048]{1,0:T(8,128)(2,1)} %bitcast.21, f32[384,2048]{1,0:T(8,128)} %get-tuple-element.54.dact_ref, ...), custom_call_target="tpu_custom_call" | custom-call | tf_op jit(solution)/shard_map/expert/pallas_call | solution.py:455
  91.2 7.5 %all-to-all-start.2 = ((bf16[32,96,128]{2,1,0:T(8,128)(2,1)}), bf16[32,96,128]{2,1,0:T(8,128)(2,1)}, u32[]{:S(2)}, u32[]{:S(2)}) async-start(bf16[32,96,128]{2,1,0:T(8,128)(2,1)} %get-tuple-element.57), calls=%async_computation.3 | async-start | bytes 1572864 | tf_op jit(solution)/shard_map/all_to_all | solution.py:387
  98.8 6.5 %expert_out.1 = bf16[32,96,128]{2,1,0:T(8,128)(2,1)} custom-call(bf16[384,2048]{1,0:T(8,128)(2,1)} %get-tuple-element.59.hidden_ref, bf16[2048,1024]{1,0:T(8,128)(2,1)} %bitcast.20), custom_call_target="tpu_custom_call" | custom-call | flops 999999995904 | bytes 1000000 | tf_op jit(solution)/shard_map/expert_out/pallas_call | solution.py:481
  105.2 13.3 %all-to-all-done.2.back_ref = bf16[32,96,128]{2,1,0:T(8,128)(2,1)} async-done(((bf16[32,96,128]{2,1,0:T(8,128)(2,1)}), bf16[32,96,128]{2,1,0:T(8,128)(2,1)}, u32[]{:S(2)}, u32[]{:S(2)}) %all-to-all-start.2) | async-done | bytes 786464 | tf_op jit(solution)/shard_map/all_to_all | solution.py:387
  118.5 2.6 %dattended.1 = (bf16[128,256]{1,0:T(8,128)(2,1)}, bf16[128,256]{1,0:T(8,128)(2,1)}, bf16[128,256]{1,0:T(8,128)(2,1)}, bf16[128,256]{1,0:T(8,128)(2,1)}) custom-call(s32[1]{0:T(128)} %bitcast.me_ref, bf16[2,3,256,128]{3,2,1,0:T(8,128)(2,1)} %get-tuple-element.44.place_ref, bf16[32,96,128]{2,1,0:T(8,128)(2,1)} %all-to-all-done.2.back_ref, ...), custom_call_target="tpu_custom_call" | custom-call | tf_op jit(solution)/shard_map/dattended/pallas_call | solution.py:497
  124.5 7.4 %all-to-all-start.3 = ((bf16[32,96,128]{2,1,0:T(8,128)(2,1)}), bf16[32,96,128]{2,1,0:T(8,128)(2,1)S(1)}, u32[]{:S(2)}, u32[]{:S(2)}) async-start(bf16[32,96,128]{2,1,0:T(8,128)(2,1)} %expert_out.1), calls=%async_computation.4 | async-start | bytes 1572864 | tf_op jit(solution)/shard_map/all_to_all | solution.py:387
  132.0 5.3 %attend_back.1 = (bf16[384,256]{1,0:T(8,128)(2,1)}, bf16[384,256]{1,0:T(8,128)(2,1)}, bf16[384,256]{1,0:T(8,128)(2,1)}, bf16[384,256]{1,0:T(8,128)(2,1)}) custom-call(bf16[384,256]{1,0:T(8,128)(2,1)} %get-tuple-element.42.refs_0_, bf16[384,256]{1,0:T(8,128)(2,1)S(1)} %copy-done.1, bf16[384,256]{1,0:T(8,128)(2,1)S(1)} %copy-done.3, ...), custom_call_target="tpu_custom_call" | custom-call | flops 40000000000 | bytes 1000000 | tf_op jit(solution)/shard_map/attend_back/pallas_call | solution.py:509
  141.5 6.0 %collective-permute-done.9.refs_1_ = bf16[384,256]{1,0:T(8,128)(2,1)S(1)} collective-permute-done((bf16[384,256]{1,0:T(8,128)(2,1)}, bf16[384,256]{1,0:T(8,128)(2,1)S(1)}, u32[]{:S(2)}, u32[]{:S(2)}) %collective-permute-start.9) | collective-permute-done | bytes 196640 | tf_op jit(solution)/shard_map/ppermute | solution.py:384
  147.6 2.9 %collective-permute-done.10.refs_2_ = bf16[384,256]{1,0:T(8,128)(2,1)S(1)} collective-permute-done((bf16[384,256]{1,0:T(8,128)(2,1)}, bf16[384,256]{1,0:T(8,128)(2,1)S(1)}, u32[]{:S(2)}, u32[]{:S(2)}) %collective-permute-start.10) | collective-permute-done | bytes 196640 | tf_op jit(solution)/shard_map/ppermute | solution.py:384
  150.4 2.0 %collective-permute-done.11.refs_3_ = bf16[384,256]{1,0:T(8,128)(2,1)S(1)} collective-permute-done((bf16[384,256]{1,0:T(8,128)(2,1)}, bf16[384,256]{1,0:T(8,128)(2,1)S(1)}, u32[]{:S(2)}, u32[]{:S(2)}) %collective-permute-start.11) | collective-permute-done | bytes 196640 | tf_op jit(solution)/shard_map/ppermute | solution.py:384
  153.9 3.7 %finish.1 = (bf16[128,1024]{1,0:T(8,128)(2,1)}, bf16[128,1024]{1,0:T(8,128)(2,1)}, bf16[128,1024]{1,0:T(8,128)(2,1)}, bf16[128,1024]{1,0:T(8,128)(2,1)}, f32[128,2048]{1,0:T(8,128)}, /*index=5*/f32[2048,128]{1,0:T(8,128)}) custom-call(s32[1]{0:T(128)} %bitcast.me_ref, bf16[128,4096]{1,0:T(8,128)(2,1)} %reduce-scatter.2.cloned.1.call-done.sums_ref, ...), custom_call_target="tpu_custom_call" | custom-call | tf_op jit(solution)/shard_map/finish/pallas_call | solution.py:523
  (33 shorter events, 14.0 us)
Async XLA Ops:
  9.3 20.4 %collective-permute-start = (bf16[384,256]{1,0:T(8,128)(2,1)}, bf16[384,256]{1,0:T(8,128)(2,1)S(1)}, u32[]{:S(2)}, u32[]{:S(2)}) collective-permute-start(bf16[384,256]{1,0:T(8,128)(2,1)} %get-tuple-element.45), channel_id=1, source_target_pairs={{0,32},{32,64},{64,96},{96,0},{1,33},{33,65},{65,97},{97,1},{2,34}... | collective-permute-start | bytes 589832 | tf_op jit(solution)/shard_map/ppermute | solution.py:384
  10.8 18.8 %collective-permute-start.1 = (bf16[384,256]{1,0:T(8,128)(2,1)}, bf16[384,256]{1,0:T(8,128)(2,1)S(1)}, u32[]{:S(2)}, u32[]{:S(2)}) collective-permute-start(bf16[384,256]{1,0:T(8,128)(2,1)} %get-tuple-element.46), channel_id=1, source_target_pairs={{0,64},{32,96},{64,0},{96,32},{1,65},{33,97},{65,1},{97,33},{2,66}... | collective-permute-start | bytes 589832 | tf_op jit(solution)/shard_map/ppermute | solution.py:384
  13.7 15.9 %collective-permute-start.2 = (bf16[384,256]{1,0:T(8,128)(2,1)}, bf16[384,256]{1,0:T(8,128)(2,1)S(1)}, u32[]{:S(2)}, u32[]{:S(2)}) collective-permute-start(bf16[384,256]{1,0:T(8,128)(2,1)} %get-tuple-element.47), channel_id=1, source_target_pairs={{0,96},{32,0},{64,32},{96,64},{1,97},{33,1},{65,33},{97,65},{2,98}... | collective-permute-start | bytes 589832 | tf_op jit(solution)/shard_map/ppermute | solution.py:384
  17.9 31.6 %all-to-all-start.1 = ((bf16[32,96,128]{2,1,0:T(8,128)(2,1)}), bf16[32,96,128]{2,1,0:T(8,128)(2,1)}, u32[]{:S(2)}, u32[]{:S(2)}) async-start(bf16[32,96,128]{2,1,0:T(8,128)(2,1)} %get-tuple-element.53), calls=%async_computation.1 | async-start | bytes 1572864 | tf_op jit(solution)/shard_map/all_to_all | solution.py:387
  29.6 5.1 %copy-start = (bf16[384,256]{1,0:T(8,128)(2,1)}, bf16[384,256]{1,0:T(8,128)(2,1)S(1)}, u32[]{:S(2)}) copy-start(bf16[384,256]{1,0:T(8,128)(2,1)S(1)} %collective-permute-done.refs_1_) | copy-start | bytes 589828
  29.6 5.1 %copy-start.2 = (bf16[384,256]{1,0:T(8,128)(2,1)}, bf16[384,256]{1,0:T(8,128)(2,1)S(1)}, u32[]{:S(2)}) copy-start(bf16[384,256]{1,0:T(8,128)(2,1)S(1)} %collective-permute-done.1.refs_2_) | copy-start | bytes 589828
  29.7 5.0 %copy-start.4 = (bf16[384,256]{1,0:T(8,128)(2,1)}, bf16[384,256]{1,0:T(8,128)(2,1)S(1)}, u32[]{:S(2)}) copy-start(bf16[384,256]{1,0:T(8,128)(2,1)S(1)} %collective-permute-done.2.refs_3_) | copy-start | bytes 589828
  34.7 4.6 %collective-permute-start.3 = (bf16[128,256]{1,0:T(8,128)(2,1)}, bf16[128,256]{1,0:T(8,128)(2,1)S(1)}, u32[]{:S(2)}, u32[]{:S(2)}) collective-permute-start(bf16[128,256]{1,0:T(8,128)(2,1)} %get-tuple-element.49), channel_id=1, source_target_pairs={{0,96},{32,0},{64,32},{96,64},{1,97},{33,1},{65,33},{97,65},{2,98}... | collective-permute-start | bytes 196616 | tf_op jit(solution)/shard_map/ppermute | solution.py:384
  34.8 6.2 %collective-permute-start.4 = (bf16[128,256]{1,0:T(8,128)(2,1)}, bf16[128,256]{1,0:T(8,128)(2,1)S(1)}, u32[]{:S(2)}, u32[]{:S(2)}) collective-permute-start(bf16[128,256]{1,0:T(8,128)(2,1)} %get-tuple-element.50), channel_id=1, source_target_pairs={{0,64},{32,96},{64,0},{96,32},{1,65},{33,97},{65,1},{97,33},{2,66}... | collective-permute-start | bytes 196616 | tf_op jit(solution)/shard_map/ppermute | solution.py:384
  37.5 5.7 %collective-permute-start.5 = (bf16[128,256]{1,0:T(8,128)(2,1)}, bf16[128,256]{1,0:T(8,128)(2,1)S(1)}, u32[]{:S(2)}, u32[]{:S(2)}) collective-permute-start(bf16[128,256]{1,0:T(8,128)(2,1)} %get-tuple-element.51), channel_id=1, source_target_pairs={{0,32},{32,64},{64,96},{96,0},{1,33},{33,65},{65,97},{97,1},{2,34}... | collective-permute-start | bytes 196616 | tf_op jit(solution)/shard_map/ppermute | solution.py:384
  49.6 27.0 %all-to-all-start = ((bf16[32,96,128]{2,1,0:T(8,128)(2,1)}), bf16[32,96,128]{2,1,0:T(8,128)(2,1)S(1)}, u32[]{:S(2)}, u32[]{:S(2)}) async-start(bf16[32,96,128]{2,1,0:T(8,128)(2,1)} %get-tuple-element.52), calls=%async_computation | async-start | bytes 1572864 | tf_op jit(solution)/shard_map/all_to_all | solution.py:387
  56.9 96.9 %reduce-scatter.2.cloned.1.call-start = ((), (), s32[]{:S(2)}) async-start(), calls=%async_computation.5 | async-start | bytes 9437184 | tf_op jit(solution)/shard_map/reduce_scatter | solution.py:478
  91.2 27.3 %all-to-all-start.2 = ((bf16[32,96,128]{2,1,0:T(8,128)(2,1)}), bf16[32,96,128]{2,1,0:T(8,128)(2,1)}, u32[]{:S(2)}, u32[]{:S(2)}) async-start(bf16[32,96,128]{2,1,0:T(8,128)(2,1)} %get-tuple-element.57), calls=%async_computation.3 | async-start | bytes 1572864 | tf_op jit(solution)/shard_map/all_to_all | solution.py:387
  98.7 33.3 %copy-start.1 = (bf16[384,256]{1,0:T(8,128)(2,1)S(1)}, bf16[384,256]{1,0:T(8,128)(2,1)}, u32[]{:S(2)}) copy-start(bf16[384,256]{1,0:T(8,128)(2,1)} %copy-done) | copy-start | bytes 589828
  98.7 33.3 %copy-start.3 = (bf16[384,256]{1,0:T(8,128)(2,1)S(1)}, bf16[384,256]{1,0:T(8,128)(2,1)}, u32[]{:S(2)}) copy-start(bf16[384,256]{1,0:T(8,128)(2,1)} %copy-done.2) | copy-start | bytes 589828
  98.7 33.3 %copy-start.5 = (bf16[384,256]{1,0:T(8,128)(2,1)S(1)}, bf16[384,256]{1,0:T(8,128)(2,1)}, u32[]{:S(2)}) copy-start(bf16[384,256]{1,0:T(8,128)(2,1)} %copy-done.4) | copy-start | bytes 589828
  121.1 10.8 %collective-permute-start.6 = (bf16[128,256]{1,0:T(8,128)(2,1)}, bf16[128,256]{1,0:T(8,128)(2,1)S(1)}, u32[]{:S(2)}, u32[]{:S(2)}) collective-permute-start(bf16[128,256]{1,0:T(8,128)(2,1)} %get-tuple-element.64), channel_id=1, source_target_pairs={{0,32},{32,64},{64,96},{96,0},{1,33},{33,65},{65,97},{97,1},{2,34}... | collective-permute-start | bytes 196616 | tf_op jit(solution)/shard_map/ppermute | solution.py:384
  121.8 10.2 %collective-permute-start.7 = (bf16[128,256]{1,0:T(8,128)(2,1)}, bf16[128,256]{1,0:T(8,128)(2,1)S(1)}, u32[]{:S(2)}, u32[]{:S(2)}) collective-permute-start(bf16[128,256]{1,0:T(8,128)(2,1)} %get-tuple-element.65), channel_id=1, source_target_pairs={{0,64},{32,96},{64,0},{96,32},{1,65},{33,97},{65,1},{97,33},{2,66}... | collective-permute-start | bytes 196616 | tf_op jit(solution)/shard_map/ppermute | solution.py:384
  123.1 8.9 %collective-permute-start.8 = (bf16[128,256]{1,0:T(8,128)(2,1)}, bf16[128,256]{1,0:T(8,128)(2,1)S(1)}, u32[]{:S(2)}, u32[]{:S(2)}) collective-permute-start(bf16[128,256]{1,0:T(8,128)(2,1)} %get-tuple-element.66), channel_id=1, source_target_pairs={{0,96},{32,0},{64,32},{96,64},{1,97},{33,1},{65,33},{97,65},{2,98}... | collective-permute-start | bytes 196616 | tf_op jit(solution)/shard_map/ppermute | solution.py:384
  124.5 27.8 %all-to-all-start.3 = ((bf16[32,96,128]{2,1,0:T(8,128)(2,1)}), bf16[32,96,128]{2,1,0:T(8,128)(2,1)S(1)}, u32[]{:S(2)}, u32[]{:S(2)}) async-start(bf16[32,96,128]{2,1,0:T(8,128)(2,1)} %expert_out.1), calls=%async_computation.4 | async-start | bytes 1572864 | tf_op jit(solution)/shard_map/all_to_all | solution.py:387
  137.3 10.2 %collective-permute-start.9 = (bf16[384,256]{1,0:T(8,128)(2,1)}, bf16[384,256]{1,0:T(8,128)(2,1)S(1)}, u32[]{:S(2)}, u32[]{:S(2)}) collective-permute-start(bf16[384,256]{1,0:T(8,128)(2,1)} %get-tuple-element.69), channel_id=1, source_target_pairs={{0,96},{32,0},{64,32},{96,64},{1,97},{33,1},{65,33},{97,65},{2,98}... | collective-permute-start | bytes 589832 | tf_op jit(solution)/shard_map/ppermute | solution.py:384
  138.7 11.7 %collective-permute-start.10 = (bf16[384,256]{1,0:T(8,128)(2,1)}, bf16[384,256]{1,0:T(8,128)(2,1)S(1)}, u32[]{:S(2)}, u32[]{:S(2)}) collective-permute-start(bf16[384,256]{1,0:T(8,128)(2,1)} %get-tuple-element.70), channel_id=1, source_target_pairs={{0,64},{32,96},{64,0},{96,32},{1,65},{33,97},{65,1},{97,33},{2,66}... | collective-permute-start | bytes 589832 | tf_op jit(solution)/shard_map/ppermute | solution.py:384
  140.1 12.2 %collective-permute-start.11 = (bf16[384,256]{1,0:T(8,128)(2,1)}, bf16[384,256]{1,0:T(8,128)(2,1)S(1)}, u32[]{:S(2)}, u32[]{:S(2)}) collective-permute-start(bf16[384,256]{1,0:T(8,128)(2,1)} %get-tuple-element.71), channel_id=1, source_target_pairs={{0,32},{32,64},{64,96},{96,0},{1,33},{33,65},{65,97},{97,1},{2,34}... | collective-permute-start | bytes 589832 | tf_op jit(solution)/shard_map/ppermute | solution.py:384
Sparse Core Ops, SparseCore 0:
  91.3 62.5 reduce-scatter.1

commit v6 on v5

--- a/solution.py
+++ b/solution.py
@@ -228,6 +228,11 @@
     pack_tokens(places, arrays, packed_ref)
 
 
+def entry_kernel(parts, experts, me_ref, q_ref, k_ref, v_ref, routes_ref, gates_ref, cot_ref, *outs):
+    split_kernel(parts, me_ref, q_ref, k_ref, v_ref, *outs[:parts])
+    place_kernel(experts, routes_ref, gates_ref, cot_ref, *outs[parts:])
+
+
 def inverse_rms_of(attended):
     return lax.rsqrt(jnp.mean(attended * attended, axis=-1, keepdims=True) + EPSILON)
 
@@ -395,23 +400,14 @@
     triple = sds((3 * tokens, width), BF)
     single = sds((tokens, width), BF)
     wire = sds((owners, capacity * model // 128, 128), BF)
-    sent = pl.pallas_call(
-        functools.partial(split_kernel, parts),
-        out_shape=[triple] * parts,
-        in_specs=[SMEM] + [VMEM] * 3,
-        out_specs=[VMEM] * parts,
-        name="split_qkv",
-    )(me, query[0], key[0], value[0])
+    *sent, place, packed_grads = pl.pallas_call(
+        functools.partial(entry_kernel, parts, owners),
+        out_shape=[triple] * parts + [sds((TOP, 3, owners * 8, tokens), BF), wire],
+        in_specs=[SMEM] + [VMEM] * 6,
+        out_specs=[VMEM] * (parts + 2),
+        name="entry",
+    )(me, query[0], key[0], value[0], route, gate, cot)
     pieces = exchange(sent, 1)
-
-    cot_late, _ = lax.optimization_barrier((cot, sent[0]))
-    place, packed_grads = pl.pallas_call(
-        functools.partial(place_kernel, owners),
-        out_shape=[sds((TOP, 3, owners * 8, tokens), BF), wire],
-        in_specs=[VMEM] * 3,
-        out_specs=[VMEM] * 2,
-        name="place",
-    )(route, gate, cot_late)
     grad_wire = swap(packed_grads)
 
     attended_pieces = pl.pallas_call(

time: 165 us -> 164 us (level)
    pallas_call x2 -> x1, Pallas kernels: 4.93 us -> 3.44 us  [shards(): pl.pallas_call(functools.partial(entry_kernel, parts, owners), out_shape=...]
  transfers between devices with their start and end apart: 17 -> 17, of which waited for: 10 -> 10; matrix products, arithmetic and copies ran while one was open for 0% -> 0% of each run, Pallas kernels for 19% -> 17%
where the time goes in v6:
time: 164 us; the launch traced here: 163 us
  starting transfers between devices  50.2 us (31%)
  Pallas kernels  49.9 us (30%)
  waiting for transfers between devices  48.5 us (30%)
  between operations  14.2 us (9%)
    all_to_all x4, starting transfers between devices, swap(): lax.all_to_all(packed, 'expert', split_axis=0, concat_axis=0, tiled=True)  33.9 us
    all_to_all x4, waiting for transfers between devices, swap(): lax.all_to_all(packed, 'expert', split_axis=0, concat_axis=0, tiled=True)  30.5 us
    ppermute x12, waiting for transfers between devices, shift(): return near(lax.ppermute(piece, 'seq', pairs_of))  16.5 us
    ppermute x12, starting transfers between devices, shift(): return near(lax.ppermute(piece, 'seq', pairs_of))  16.3 us
    pallas_call x1, Pallas kernels, shards(): pl.pallas_call(functools.partial(expert_kernel, pairs, parts), grid=(bloc...  14.6 us
    pallas_call x1, Pallas kernels, shards(): pl.pallas_call(out_kernel, grid=(blocks,), out_shape=wire, in_specs=[pl.B...  6.47 us
    pallas_call x1, Pallas kernels, shards(): pl.pallas_call(functools.partial(dact_kernel, pairs, parts), grid=(blocks...  6.23 us
    pallas_call x1, Pallas kernels, shards(): pl.pallas_call(functools.partial(attend_back_kernel, parts), out_shape=[t...  5.32 us
  transfers between devices with their start and end apart: 17, of which 10 were waited for; matrix products, arithmetic and copies ran while one was open for 0% of the time, Pallas kernels for 17%

profile of v6, /device:TPU:2, one launch (start us, length us, event | category | flops | bytes accessed | tf_op | source)
XLA Modules:
  0.0 162.9 jit_solution(11203635378764435182)
XLA Ops:
  7.2 3.4 %entry.1 = (bf16[384,256]{1,0:T(8,128)(2,1)}, bf16[384,256]{1,0:T(8,128)(2,1)}, bf16[384,256]{1,0:T(8,128)(2,1)}, bf16[384,256]{1,0:T(8,128)(2,1)}, bf16[2,3,256...) custom-call(s32[1]{0:T(128)} %bitcast.me_ref, bf16[128,1024]{1,0:T(8,128)(2,1)} %bitcast.24, ...), custom_call_target="tpu_custom_call" | custom-call | tf_op jit(solution)/shard_map/entry/pallas_call | solution.py:403
  12.2 2.9 %collective-permute-start.1 = (bf16[384,256]{1,0:T(8,128)(2,1)}, bf16[384,256]{1,0:T(8,128)(2,1)S(1)}, u32[]{:S(2)}, u32[]{:S(2)}) collective-permute-start(bf16[384,256]{1,0:T(8,128)(2,1)} %get-tuple-element.44), channel_id=1, source_target_pairs={{0,64},{32,96},{64,0},{96,32},{1,65},{33,97},{65,1},{97,33},{2,66}... | collective-permute-start | bytes 589832 | tf_op jit(solution)/shard_map/ppermute | solution.py:389
  16.4 11.7 %all-to-all-start.1 = ((bf16[32,96,128]{2,1,0:T(8,128)(2,1)}), bf16[32,96,128]{2,1,0:T(8,128)(2,1)}, u32[]{:S(2)}, u32[]{:S(2)}) async-start(bf16[32,96,128]{2,1,0:T(8,128)(2,1)} %get-tuple-element.51), calls=%async_computation.1 | async-start | bytes 1572864 | tf_op jit(solution)/shard_map/all_to_all | solution.py:392
  28.2 5.0 %attend.1 = (bf16[128,256]{1,0:T(8,128)(2,1)}, bf16[128,256]{1,0:T(8,128)(2,1)}, bf16[128,256]{1,0:T(8,128)(2,1)}, bf16[128,256]{1,0:T(8,128)(2,1)}, bf16[2,512,512]{2,1,0:T(8,128)(2,1)}) custom-call(bf16[384,256]{1,0:T(8,128)(2,1)} %get-tuple-element.42.refs_0_, bf16[384,256]{1,0:T(8,128)(2,1)S(1)} %collective-permute-done.refs_1_, ...), custom_call_target="tpu_custom_call" | custom-call | flops 999999995904 | bytes 1000000 | tf_op jit(solution)/shard_map/attend/pallas_call | solution.py:413
  33.3 2.7 %collective-permute-start.4 = (bf16[128,256]{1,0:T(8,128)(2,1)}, bf16[128,256]{1,0:T(8,128)(2,1)S(1)}, u32[]{:S(2)}, u32[]{:S(2)}) collective-permute-start(bf16[128,256]{1,0:T(8,128)(2,1)} %get-tuple-element.48), channel_id=1, source_target_pairs={{0,64},{32,96},{64,0},{96,32},{1,65},{33,97},{65,1},{97,33},{2,66}... | collective-permute-start | bytes 196616 | tf_op jit(solution)/shard_map/ppermute | solution.py:389
  36.1 1.7 %collective-permute-done.3.refs_1_ = bf16[128,256]{1,0:T(8,128)(2,1)S(1)} collective-permute-done((bf16[128,256]{1,0:T(8,128)(2,1)}, bf16[128,256]{1,0:T(8,128)(2,1)S(1)}, u32[]{:S(2)}, u32[]{:S(2)}) %collective-permute-start.3) | collective-permute-done | bytes 65568 | tf_op jit(solution)/shard_map/ppermute | solution.py:389
  37.8 1.7 %collective-permute-done.4.refs_2_ = bf16[128,256]{1,0:T(8,128)(2,1)S(1)} collective-permute-done((bf16[128,256]{1,0:T(8,128)(2,1)}, bf16[128,256]{1,0:T(8,128)(2,1)S(1)}, u32[]{:S(2)}, u32[]{:S(2)}) %collective-permute-start.4) | collective-permute-done | bytes 65568 | tf_op jit(solution)/shard_map/ppermute | solution.py:389
  39.5 2.2 %collective-permute-done.5.refs_3_ = bf16[128,256]{1,0:T(8,128)(2,1)S(1)} collective-permute-done((bf16[128,256]{1,0:T(8,128)(2,1)}, bf16[128,256]{1,0:T(8,128)(2,1)S(1)}, u32[]{:S(2)}, u32[]{:S(2)}) %collective-permute-start.5) | collective-permute-done | bytes 65568 | tf_op jit(solution)/shard_map/ppermute | solution.py:389
  41.7 2.5 %norm_pack.1 = (bf16[128,1024]{1,0:T(8,128)(2,1)}, bf16[32,96,128]{2,1,0:T(8,128)(2,1)}) custom-call(s32[1]{0:T(128)} %bitcast.me_ref, bf16[2,3,256,128]{3,2,1,0:T(8,128)(2,1)} %get-tuple-element.41.place_ref, bf16[128,256]{1,0:T(8,128)(2,1)} %get-tuple-element.46.refs_0_, bf16[128,256]{1,0:T(8,128)(2,1)S(1)} %collective-permute-done.3.refs_1_, ...), custom_call_target="tpu_custom_call" | custom-call | tf_op jit(solution)/shard_map/norm_pack/pallas_call | solution.py:426
  44.3 3.8 %all-to-all-done.1.packed_ref = bf16[32,96,128]{2,1,0:T(8,128)(2,1)} async-done(((bf16[32,96,128]{2,1,0:T(8,128)(2,1)}), bf16[32,96,128]{2,1,0:T(8,128)(2,1)}, u32[]{:S(2)}, u32[]{:S(2)}) %all-to-all-start.1) | async-done | bytes 786464 | tf_op jit(solution)/shard_map/all_to_all | solution.py:392
  48.1 7.3 %all-to-all-start = ((bf16[32,96,128]{2,1,0:T(8,128)(2,1)}), bf16[32,96,128]{2,1,0:T(8,128)(2,1)S(1)}, u32[]{:S(2)}, u32[]{:S(2)}) async-start(bf16[32,96,128]{2,1,0:T(8,128)(2,1)} %get-tuple-element.50), calls=%async_computation | async-start | bytes 1572864 | tf_op jit(solution)/shard_map/all_to_all | solution.py:392
  55.5 6.2 %dact.1 = (f32[384,2048]{1,0:T(8,128)}, bf16[1024,384]{1,0:T(8,128)(2,1)}) custom-call(bf16[32,96,128]{2,1,0:T(8,128)(2,1)} %all-to-all-done.1.packed_ref, bf16[2048,1024]{1,0:T(8,128)(2,1)} %bitcast.19), custom_call_target="tpu_custom_call" | custom-call | tf_op jit(solution)/shard_map/dact/pallas_call | solution.py:438
  61.7 13.4 %all-to-all-done.packed_ref = bf16[32,96,128]{2,1,0:T(8,128)(2,1)S(1)} async-done(((bf16[32,96,128]{2,1,0:T(8,128)(2,1)}), bf16[32,96,128]{2,1,0:T(8,128)(2,1)S(1)}, u32[]{:S(2)}, u32[]{:S(2)}) %all-to-all-start) | async-done | bytes 786464 | tf_op jit(solution)/shard_map/all_to_all | solution.py:392
  75.1 14.6 %expert.1 = (bf16[384,2048]{1,0:T(8,128)(2,1)}, bf16[1024,4096]{1,0:T(8,128)(2,1)}, bf16[32,96,128]{2,1,0:T(8,128)(2,1)}) custom-call(bf16[32,96,128]{2,1,0:T(8,128)(2,1)S(1)} %all-to-all-done.packed_ref, bf16[1024,2048]{1,0:T(8,128)(2,1)} %bitcast.21, f32[384,2048]{1,0:T(8,128)} %get-tuple-element.52.dact_ref, ...), custom_call_target="tpu_custom_call" | custom-call | tf_op jit(solution)/shard_map/expert/pallas_call | solution.py:451
  89.7 7.5 %all-to-all-start.2 = ((bf16[32,96,128]{2,1,0:T(8,128)(2,1)}), bf16[32,96,128]{2,1,0:T(8,128)(2,1)}, u32[]{:S(2)}, u32[]{:S(2)}) async-start(bf16[32,96,128]{2,1,0:T(8,128)(2,1)} %get-tuple-element.55), calls=%async_computation.3 | async-start | bytes 1572864 | tf_op jit(solution)/shard_map/all_to_all | solution.py:392
  97.3 6.5 %expert_out.1 = bf16[32,96,128]{2,1,0:T(8,128)(2,1)} custom-call(bf16[384,2048]{1,0:T(8,128)(2,1)} %get-tuple-element.57.hidden_ref, bf16[2048,1024]{1,0:T(8,128)(2,1)} %bitcast.20), custom_call_target="tpu_custom_call" | custom-call | flops 999999995904 | bytes 1000000 | tf_op jit(solution)/shard_map/expert_out/pallas_call | solution.py:477
  103.7 13.3 %all-to-all-done.2.back_ref = bf16[32,96,128]{2,1,0:T(8,128)(2,1)} async-done(((bf16[32,96,128]{2,1,0:T(8,128)(2,1)}), bf16[32,96,128]{2,1,0:T(8,128)(2,1)}, u32[]{:S(2)}, u32[]{:S(2)}) %all-to-all-start.2) | async-done | bytes 786464 | tf_op jit(solution)/shard_map/all_to_all | solution.py:392
  117.0 2.7 %dattended.1 = (bf16[128,256]{1,0:T(8,128)(2,1)}, bf16[128,256]{1,0:T(8,128)(2,1)}, bf16[128,256]{1,0:T(8,128)(2,1)}, bf16[128,256]{1,0:T(8,128)(2,1)}) custom-call(s32[1]{0:T(128)} %bitcast.me_ref, bf16[2,3,256,128]{3,2,1,0:T(8,128)(2,1)} %get-tuple-element.41.place_ref, bf16[32,96,128]{2,1,0:T(8,128)(2,1)} %all-to-all-done.2.back_ref, ...), custom_call_target="tpu_custom_call" | custom-call | tf_op jit(solution)/shard_map/dattended/pallas_call | solution.py:493
  123.1 7.4 %all-to-all-start.3 = ((bf16[32,96,128]{2,1,0:T(8,128)(2,1)}), bf16[32,96,128]{2,1,0:T(8,128)(2,1)S(1)}, u32[]{:S(2)}, u32[]{:S(2)}) async-start(bf16[32,96,128]{2,1,0:T(8,128)(2,1)} %expert_out.1), calls=%async_computation.4 | async-start | bytes 1572864 | tf_op jit(solution)/shard_map/all_to_all | solution.py:392
  130.5 5.3 %attend_back.1 = (bf16[384,256]{1,0:T(8,128)(2,1)}, bf16[384,256]{1,0:T(8,128)(2,1)}, bf16[384,256]{1,0:T(8,128)(2,1)}, bf16[384,256]{1,0:T(8,128)(2,1)}) custom-call(bf16[384,256]{1,0:T(8,128)(2,1)} %get-tuple-element.42.refs_0_, bf16[384,256]{1,0:T(8,128)(2,1)S(1)} %copy-done.1, bf16[384,256]{1,0:T(8,128)(2,1)S(1)} %copy-done.3, ...), custom_call_target="tpu_custom_call" | custom-call | flops 40000000000 | bytes 1000000 | tf_op jit(solution)/shard_map/attend_back/pallas_call | solution.py:505
  140.1 6.0 %collective-permute-done.9.refs_1_ = bf16[384,256]{1,0:T(8,128)(2,1)S(1)} collective-permute-done((bf16[384,256]{1,0:T(8,128)(2,1)}, bf16[384,256]{1,0:T(8,128)(2,1)S(1)}, u32[]{:S(2)}, u32[]{:S(2)}) %collective-permute-start.9) | collective-permute-done | bytes 196640 | tf_op jit(solution)/shard_map/ppermute | solution.py:389
  146.1 2.9 %collective-permute-done.10.refs_2_ = bf16[384,256]{1,0:T(8,128)(2,1)S(1)} collective-permute-done((bf16[384,256]{1,0:T(8,128)(2,1)}, bf16[384,256]{1,0:T(8,128)(2,1)S(1)}, u32[]{:S(2)}, u32[]{:S(2)}) %collective-permute-start.10) | collective-permute-done | bytes 196640 | tf_op jit(solution)/shard_map/ppermute | solution.py:389
  148.9 1.9 %collective-permute-done.11.refs_3_ = bf16[384,256]{1,0:T(8,128)(2,1)S(1)} collective-permute-done((bf16[384,256]{1,0:T(8,128)(2,1)}, bf16[384,256]{1,0:T(8,128)(2,1)S(1)}, u32[]{:S(2)}, u32[]{:S(2)}) %collective-permute-start.11) | collective-permute-done | bytes 196640 | tf_op jit(solution)/shard_map/ppermute | solution.py:389
  152.4 3.7 %finish.1 = (bf16[128,1024]{1,0:T(8,128)(2,1)}, bf16[128,1024]{1,0:T(8,128)(2,1)}, bf16[128,1024]{1,0:T(8,128)(2,1)}, bf16[128,1024]{1,0:T(8,128)(2,1)}, f32[128,2048]{1,0:T(8,128)}, /*index=5*/f32[2048,128]{1,0:T(8,128)}) custom-call(s32[1]{0:T(128)} %bitcast.me_ref, bf16[128,4096]{1,0:T(8,128)(2,1)} %reduce-scatter.2.cloned.1.call-done.sums_ref, ...), custom_call_target="tpu_custom_call" | custom-call | tf_op jit(solution)/shard_map/finish/pallas_call | solution.py:519
  (32 shorter events, 12.2 us)
Async XLA Ops:
  10.6 17.5 %collective-permute-start = (bf16[384,256]{1,0:T(8,128)(2,1)}, bf16[384,256]{1,0:T(8,128)(2,1)S(1)}, u32[]{:S(2)}, u32[]{:S(2)}) collective-permute-start(bf16[384,256]{1,0:T(8,128)(2,1)} %get-tuple-element.43), channel_id=1, source_target_pairs={{0,32},{32,64},{64,96},{96,0},{1,33},{33,65},{65,97},{97,1},{2,34}... | collective-permute-start | bytes 589832 | tf_op jit(solution)/shard_map/ppermute | solution.py:389
  12.2 15.9 %collective-permute-start.1 = (bf16[384,256]{1,0:T(8,128)(2,1)}, bf16[384,256]{1,0:T(8,128)(2,1)S(1)}, u32[]{:S(2)}, u32[]{:S(2)}) collective-permute-start(bf16[384,256]{1,0:T(8,128)(2,1)} %get-tuple-element.44), channel_id=1, source_target_pairs={{0,64},{32,96},{64,0},{96,32},{1,65},{33,97},{65,1},{97,33},{2,66}... | collective-permute-start | bytes 589832 | tf_op jit(solution)/shard_map/ppermute | solution.py:389
  15.1 13.1 %collective-permute-start.2 = (bf16[384,256]{1,0:T(8,128)(2,1)}, bf16[384,256]{1,0:T(8,128)(2,1)S(1)}, u32[]{:S(2)}, u32[]{:S(2)}) collective-permute-start(bf16[384,256]{1,0:T(8,128)(2,1)} %get-tuple-element.45), channel_id=1, source_target_pairs={{0,96},{32,0},{64,32},{96,64},{1,97},{33,1},{65,33},{97,65},{2,98}... | collective-permute-start | bytes 589832 | tf_op jit(solution)/shard_map/ppermute | solution.py:389
  16.4 31.6 %all-to-all-start.1 = ((bf16[32,96,128]{2,1,0:T(8,128)(2,1)}), bf16[32,96,128]{2,1,0:T(8,128)(2,1)}, u32[]{:S(2)}, u32[]{:S(2)}) async-start(bf16[32,96,128]{2,1,0:T(8,128)(2,1)} %get-tuple-element.51), calls=%async_computation.1 | async-start | bytes 1572864 | tf_op jit(solution)/shard_map/all_to_all | solution.py:392
  28.1 5.1 %copy-start = (bf16[384,256]{1,0:T(8,128)(2,1)}, bf16[384,256]{1,0:T(8,128)(2,1)S(1)}, u32[]{:S(2)}) copy-start(bf16[384,256]{1,0:T(8,128)(2,1)S(1)} %collective-permute-done.refs_1_) | copy-start | bytes 589828
  28.1 5.1 %copy-start.2 = (bf16[384,256]{1,0:T(8,128)(2,1)}, bf16[384,256]{1,0:T(8,128)(2,1)S(1)}, u32[]{:S(2)}) copy-start(bf16[384,256]{1,0:T(8,128)(2,1)S(1)} %collective-permute-done.1.refs_2_) | copy-start | bytes 589828
  28.2 5.1 %copy-start.4 = (bf16[384,256]{1,0:T(8,128)(2,1)}, bf16[384,256]{1,0:T(8,128)(2,1)S(1)}, u32[]{:S(2)}) copy-start(bf16[384,256]{1,0:T(8,128)(2,1)S(1)} %collective-permute-done.2.refs_3_) | copy-start | bytes 589828
  33.2 4.6 %collective-permute-start.3 = (bf16[128,256]{1,0:T(8,128)(2,1)}, bf16[128,256]{1,0:T(8,128)(2,1)S(1)}, u32[]{:S(2)}, u32[]{:S(2)}) collective-permute-start(bf16[128,256]{1,0:T(8,128)(2,1)} %get-tuple-element.47), channel_id=1, source_target_pairs={{0,96},{32,0},{64,32},{96,64},{1,97},{33,1},{65,33},{97,65},{2,98}... | collective-permute-start | bytes 196616 | tf_op jit(solution)/shard_map/ppermute | solution.py:389
  33.3 6.2 %collective-permute-start.4 = (bf16[128,256]{1,0:T(8,128)(2,1)}, bf16[128,256]{1,0:T(8,128)(2,1)S(1)}, u32[]{:S(2)}, u32[]{:S(2)}) collective-permute-start(bf16[128,256]{1,0:T(8,128)(2,1)} %get-tuple-element.48), channel_id=1, source_target_pairs={{0,64},{32,96},{64,0},{96,32},{1,65},{33,97},{65,1},{97,33},{2,66}... | collective-permute-start | bytes 196616 | tf_op jit(solution)/shard_map/ppermute | solution.py:389
  36.0 5.7 %collective-permute-start.5 = (bf16[128,256]{1,0:T(8,128)(2,1)}, bf16[128,256]{1,0:T(8,128)(2,1)S(1)}, u32[]{:S(2)}, u32[]{:S(2)}) collective-permute-start(bf16[128,256]{1,0:T(8,128)(2,1)} %get-tuple-element.49), channel_id=1, source_target_pairs={{0,32},{32,64},{64,96},{96,0},{1,33},{33,65},{65,97},{97,1},{2,34}... | collective-permute-start | bytes 196616 | tf_op jit(solution)/shard_map/ppermute | solution.py:389
  48.1 27.0 %all-to-all-start = ((bf16[32,96,128]{2,1,0:T(8,128)(2,1)}), bf16[32,96,128]{2,1,0:T(8,128)(2,1)S(1)}, u32[]{:S(2)}, u32[]{:S(2)}) async-start(bf16[32,96,128]{2,1,0:T(8,128)(2,1)} %get-tuple-element.50), calls=%async_computation | async-start | bytes 1572864 | tf_op jit(solution)/shard_map/all_to_all | solution.py:392
  55.4 96.9 %reduce-scatter.2.cloned.1.call-start = ((), (), s32[]{:S(2)}) async-start(), calls=%async_computation.5 | async-start | bytes 9437184 | tf_op jit(solution)/shard_map/reduce_scatter | solution.py:474
  89.7 27.3 %all-to-all-start.2 = ((bf16[32,96,128]{2,1,0:T(8,128)(2,1)}), bf16[32,96,128]{2,1,0:T(8,128)(2,1)}, u32[]{:S(2)}, u32[]{:S(2)}) async-start(bf16[32,96,128]{2,1,0:T(8,128)(2,1)} %get-tuple-element.55), calls=%async_computation.3 | async-start | bytes 1572864 | tf_op jit(solution)/shard_map/all_to_all | solution.py:392
  97.2 33.3 %copy-start.1 = (bf16[384,256]{1,0:T(8,128)(2,1)S(1)}, bf16[384,256]{1,0:T(8,128)(2,1)}, u32[]{:S(2)}) copy-start(bf16[384,256]{1,0:T(8,128)(2,1)} %copy-done) | copy-start | bytes 589828
  97.3 33.3 %copy-start.3 = (bf16[384,256]{1,0:T(8,128)(2,1)S(1)}, bf16[384,256]{1,0:T(8,128)(2,1)}, u32[]{:S(2)}) copy-start(bf16[384,256]{1,0:T(8,128)(2,1)} %copy-done.2) | copy-start | bytes 589828
  97.3 33.3 %copy-start.5 = (bf16[384,256]{1,0:T(8,128)(2,1)S(1)}, bf16[384,256]{1,0:T(8,128)(2,1)}, u32[]{:S(2)}) copy-start(bf16[384,256]{1,0:T(8,128)(2,1)} %copy-done.4) | copy-start | bytes 589828
  119.7 10.8 %collective-permute-start.6 = (bf16[128,256]{1,0:T(8,128)(2,1)}, bf16[128,256]{1,0:T(8,128)(2,1)S(1)}, u32[]{:S(2)}, u32[]{:S(2)}) collective-permute-start(bf16[128,256]{1,0:T(8,128)(2,1)} %get-tuple-element.62), channel_id=1, source_target_pairs={{0,32},{32,64},{64,96},{96,0},{1,33},{33,65},{65,97},{97,1},{2,34}... | collective-permute-start | bytes 196616 | tf_op jit(solution)/shard_map/ppermute | solution.py:389
  120.4 10.1 %collective-permute-start.7 = (bf16[128,256]{1,0:T(8,128)(2,1)}, bf16[128,256]{1,0:T(8,128)(2,1)S(1)}, u32[]{:S(2)}, u32[]{:S(2)}) collective-permute-start(bf16[128,256]{1,0:T(8,128)(2,1)} %get-tuple-element.63), channel_id=1, source_target_pairs={{0,64},{32,96},{64,0},{96,32},{1,65},{33,97},{65,1},{97,33},{2,66}... | collective-permute-start | bytes 196616 | tf_op jit(solution)/shard_map/ppermute | solution.py:389
  121.6 8.9 %collective-permute-start.8 = (bf16[128,256]{1,0:T(8,128)(2,1)}, bf16[128,256]{1,0:T(8,128)(2,1)S(1)}, u32[]{:S(2)}, u32[]{:S(2)}) collective-permute-start(bf16[128,256]{1,0:T(8,128)(2,1)} %get-tuple-element.64), channel_id=1, source_target_pairs={{0,96},{32,0},{64,32},{96,64},{1,97},{33,1},{65,33},{97,65},{2,98}... | collective-permute-start | bytes 196616 | tf_op jit(solution)/shard_map/ppermute | solution.py:389
  123.1 27.8 %all-to-all-start.3 = ((bf16[32,96,128]{2,1,0:T(8,128)(2,1)}), bf16[32,96,128]{2,1,0:T(8,128)(2,1)S(1)}, u32[]{:S(2)}, u32[]{:S(2)}) async-start(bf16[32,96,128]{2,1,0:T(8,128)(2,1)} %expert_out.1), calls=%async_computation.4 | async-start | bytes 1572864 | tf_op jit(solution)/shard_map/all_to_all | solution.py:392
  135.9 10.2 %collective-permute-start.9 = (bf16[384,256]{1,0:T(8,128)(2,1)}, bf16[384,256]{1,0:T(8,128)(2,1)S(1)}, u32[]{:S(2)}, u32[]{:S(2)}) collective-permute-start(bf16[384,256]{1,0:T(8,128)(2,1)} %get-tuple-element.67), channel_id=1, source_target_pairs={{0,96},{32,0},{64,32},{96,64},{1,97},{33,1},{65,33},{97,65},{2,98}... | collective-permute-start | bytes 589832 | tf_op jit(solution)/shard_map/ppermute | solution.py:389
  137.2 11.7 %collective-permute-start.10 = (bf16[384,256]{1,0:T(8,128)(2,1)}, bf16[384,256]{1,0:T(8,128)(2,1)S(1)}, u32[]{:S(2)}, u32[]{:S(2)}) collective-permute-start(bf16[384,256]{1,0:T(8,128)(2,1)} %get-tuple-element.68), channel_id=1, source_target_pairs={{0,64},{32,96},{64,0},{96,32},{1,65},{33,97},{65,1},{97,33},{2,66}... | collective-permute-start | bytes 589832 | tf_op jit(solution)/shard_map/ppermute | solution.py:389
  138.6 12.2 %collective-permute-start.11 = (bf16[384,256]{1,0:T(8,128)(2,1)}, bf16[384,256]{1,0:T(8,128)(2,1)S(1)}, u32[]{:S(2)}, u32[]{:S(2)}) collective-permute-start(bf16[384,256]{1,0:T(8,128)(2,1)} %get-tuple-element.69), channel_id=1, source_target_pairs={{0,32},{32,64},{64,96},{96,0},{1,33},{33,65},{65,97},{97,1},{2,34}... | collective-permute-start | bytes 589832 | tf_op jit(solution)/shard_map/ppermute | solution.py:389
Sparse Core Ops, SparseCore 0:
  89.8 62.4 reduce-scatter.1

commit v7 on v6

--- a/solution.py
+++ b/solution.py
@@ -497,7 +497,7 @@
         out_specs=[VMEM] * parts,
         scratch_shapes=[pltpu.VMEM((tokens, model), BF)],
         name="dattended",
-    )(me, place, dnormed_back, attended, cot)
+    )(me, near(place), dnormed_back, near(attended), near(cot))
     grad_pieces = exchange(grad_pieces, 1)
 
     produced_back = swap(produced)
@@ -523,7 +523,7 @@
         out_specs=[VMEM] * 6,
         compiler_params=BIG,
         name="finish",
-    )(me, sums, place, produced_back, attended, gate, *back_pieces)
+    )(me, sums, near(place), produced_back, near(attended), gate, *back_pieces)
     return (
         layer_output[None],
         grad_queries[None],

time: 164 us -> 163 us (level)
  no operation moved by 1% of the time
where the time goes in v7:
time: 163 us
  starting transfers between devices  50.3 us (31%)
  Pallas kernels  49.3 us (30%)
  waiting for transfers between devices  48.8 us (30%)
  between operations  14.2 us (9%)
    all_to_all x4, starting transfers between devices, swap(): lax.all_to_all(packed, 'expert', split_axis=0, concat_axis=0, tiled=True)  34 us
    all_to_all x4, waiting for transfers between devices, swap(): lax.all_to_all(packed, 'expert', split_axis=0, concat_axis=0, tiled=True)  30.5 us
    ppermute x12, waiting for transfers between devices, shift(): return near(lax.ppermute(piece, 'seq', pairs_of))  16.5 us
    ppermute x12, starting transfers between devices, shift(): return near(lax.ppermute(piece, 'seq', pairs_of))  16.3 us
    pallas_call x1, Pallas kernels, shards(): pl.pallas_call(functools.partial(expert_kernel, pairs, parts), grid=(bloc...  14.6 us
    pallas_call x1, Pallas kernels, shards(): pl.pallas_call(out_kernel, grid=(blocks,), out_shape=wire, in_specs=[pl.B...  6.45 us
    pallas_call x1, Pallas kernels, shards(): pl.pallas_call(functools.partial(dact_kernel, pairs, parts), grid=(blocks...  6.27 us
    pallas_call x1, Pallas kernels, shards(): pl.pallas_call(functools.partial(attend_back_kernel, parts), out_shape=[t...  5.3 us
  transfers between devices with their start and end apart: 17, of which 10 were waited for; matrix products, arithmetic and copies ran while one was open for 0% of the time, Pallas kernels for 17%

profile of v7, /device:TPU:2, one launch (start us, length us, event | category | flops | bytes accessed | tf_op | source)
XLA Modules:
  0.0 162.6 jit_solution(7422146649082368328)
XLA Ops:
  7.2 3.4 %entry.1 = (bf16[384,256]{1,0:T(8,128)(2,1)}, bf16[384,256]{1,0:T(8,128)(2,1)}, bf16[384,256]{1,0:T(8,128)(2,1)}, bf16[384,256]{1,0:T(8,128)(2,1)}, bf16[2,3,256...) custom-call(s32[1]{0:T(128)} %bitcast.me_ref, bf16[128,1024]{1,0:T(8,128)(2,1)} %bitcast.24, ...), custom_call_target="tpu_custom_call" | custom-call | tf_op jit(solution)/shard_map/entry/pallas_call | solution.py:403
  12.2 2.9 %collective-permute-start.1 = (bf16[384,256]{1,0:T(8,128)(2,1)}, bf16[384,256]{1,0:T(8,128)(2,1)S(1)}, u32[]{:S(2)}, u32[]{:S(2)}) collective-permute-start(bf16[384,256]{1,0:T(8,128)(2,1)} %get-tuple-element.44), channel_id=1, source_target_pairs={{0,64},{32,96},{64,0},{96,32},{1,65},{33,97},{65,1},{97,33},{2,66}... | collective-permute-start | bytes 589832 | tf_op jit(solution)/shard_map/ppermute | solution.py:389
  16.4 11.7 %all-to-all-start.1 = ((bf16[32,96,128]{2,1,0:T(8,128)(2,1)}), bf16[32,96,128]{2,1,0:T(8,128)(2,1)}, u32[]{:S(2)}, u32[]{:S(2)}) async-start(bf16[32,96,128]{2,1,0:T(8,128)(2,1)} %get-tuple-element.51), calls=%async_computation.1 | async-start | bytes 1572864 | tf_op jit(solution)/shard_map/all_to_all | solution.py:392
  28.2 5.0 %attend.1 = (bf16[128,256]{1,0:T(8,128)(2,1)}, bf16[128,256]{1,0:T(8,128)(2,1)}, bf16[128,256]{1,0:T(8,128)(2,1)}, bf16[128,256]{1,0:T(8,128)(2,1)}, bf16[2,512,512]{2,1,0:T(8,128)(2,1)}) custom-call(bf16[384,256]{1,0:T(8,128)(2,1)} %get-tuple-element.42.refs_0_, bf16[384,256]{1,0:T(8,128)(2,1)S(1)} %collective-permute-done.refs_1_, ...), custom_call_target="tpu_custom_call" | custom-call | flops 999999995904 | bytes 1000000 | tf_op jit(solution)/shard_map/attend/pallas_call | solution.py:413
  33.3 2.7 %collective-permute-start.4 = (bf16[128,256]{1,0:T(8,128)(2,1)}, bf16[128,256]{1,0:T(8,128)(2,1)S(1)}, u32[]{:S(2)}, u32[]{:S(2)}) collective-permute-start(bf16[128,256]{1,0:T(8,128)(2,1)} %get-tuple-element.48), channel_id=1, source_target_pairs={{0,64},{32,96},{64,0},{96,32},{1,65},{33,97},{65,1},{97,33},{2,66}... | collective-permute-start | bytes 196616 | tf_op jit(solution)/shard_map/ppermute | solution.py:389
  37.8 1.7 %collective-permute-done.4.refs_2_ = bf16[128,256]{1,0:T(8,128)(2,1)S(1)} collective-permute-done((bf16[128,256]{1,0:T(8,128)(2,1)}, bf16[128,256]{1,0:T(8,128)(2,1)S(1)}, u32[]{:S(2)}, u32[]{:S(2)}) %collective-permute-start.4) | collective-permute-done | bytes 65568 | tf_op jit(solution)/shard_map/ppermute | solution.py:389
  39.5 2.2 %collective-permute-done.5.refs_3_ = bf16[128,256]{1,0:T(8,128)(2,1)S(1)} collective-permute-done((bf16[128,256]{1,0:T(8,128)(2,1)}, bf16[128,256]{1,0:T(8,128)(2,1)S(1)}, u32[]{:S(2)}, u32[]{:S(2)}) %collective-permute-start.5) | collective-permute-done | bytes 65568 | tf_op jit(solution)/shard_map/ppermute | solution.py:389
  41.7 2.5 %norm_pack.1 = (bf16[128,1024]{1,0:T(8,128)(2,1)}, bf16[32,96,128]{2,1,0:T(8,128)(2,1)}) custom-call(s32[1]{0:T(128)} %bitcast.me_ref, bf16[2,3,256,128]{3,2,1,0:T(8,128)(2,1)} %get-tuple-element.41.place_ref, bf16[128,256]{1,0:T(8,128)(2,1)} %get-tuple-element.46.refs_0_, bf16[128,256]{1,0:T(8,128)(2,1)S(1)} %collective-permute-done.3.refs_1_, ...), custom_call_target="tpu_custom_call" | custom-call | tf_op jit(solution)/shard_map/norm_pack/pallas_call | solution.py:426
  44.2 3.8 %all-to-all-done.1.packed_ref = bf16[32,96,128]{2,1,0:T(8,128)(2,1)} async-done(((bf16[32,96,128]{2,1,0:T(8,128)(2,1)}), bf16[32,96,128]{2,1,0:T(8,128)(2,1)}, u32[]{:S(2)}, u32[]{:S(2)}) %all-to-all-start.1) | async-done | bytes 786464 | tf_op jit(solution)/shard_map/all_to_all | solution.py:392
  48.1 7.3 %all-to-all-start = ((bf16[32,96,128]{2,1,0:T(8,128)(2,1)}), bf16[32,96,128]{2,1,0:T(8,128)(2,1)S(1)}, u32[]{:S(2)}, u32[]{:S(2)}) async-start(bf16[32,96,128]{2,1,0:T(8,128)(2,1)} %get-tuple-element.50), calls=%async_computation | async-start | bytes 1572864 | tf_op jit(solution)/shard_map/all_to_all | solution.py:392
  55.5 6.3 %dact.1 = (f32[384,2048]{1,0:T(8,128)}, bf16[1024,384]{1,0:T(8,128)(2,1)}) custom-call(bf16[32,96,128]{2,1,0:T(8,128)(2,1)} %all-to-all-done.1.packed_ref, bf16[2048,1024]{1,0:T(8,128)(2,1)} %bitcast.21), custom_call_target="tpu_custom_call" | custom-call | tf_op jit(solution)/shard_map/dact/pallas_call | solution.py:438
  61.7 13.4 %all-to-all-done.packed_ref = bf16[32,96,128]{2,1,0:T(8,128)(2,1)S(1)} async-done(((bf16[32,96,128]{2,1,0:T(8,128)(2,1)}), bf16[32,96,128]{2,1,0:T(8,128)(2,1)S(1)}, u32[]{:S(2)}, u32[]{:S(2)}) %all-to-all-start) | async-done | bytes 786464 | tf_op jit(solution)/shard_map/all_to_all | solution.py:392
  75.1 14.6 %expert.1 = (bf16[384,2048]{1,0:T(8,128)(2,1)}, bf16[1024,4096]{1,0:T(8,128)(2,1)}, bf16[32,96,128]{2,1,0:T(8,128)(2,1)}) custom-call(bf16[32,96,128]{2,1,0:T(8,128)(2,1)S(1)} %all-to-all-done.packed_ref, bf16[1024,2048]{1,0:T(8,128)(2,1)} %bitcast.23, f32[384,2048]{1,0:T(8,128)} %get-tuple-element.52.dact_ref, ...), custom_call_target="tpu_custom_call" | custom-call | tf_op jit(solution)/shard_map/expert/pallas_call | solution.py:451
  89.8 7.5 %all-to-all-start.2 = ((bf16[32,96,128]{2,1,0:T(8,128)(2,1)}), bf16[32,96,128]{2,1,0:T(8,128)(2,1)}, u32[]{:S(2)}, u32[]{:S(2)}) async-start(bf16[32,96,128]{2,1,0:T(8,128)(2,1)} %get-tuple-element.55), calls=%async_computation.3 | async-start | bytes 1572864 | tf_op jit(solution)/shard_map/all_to_all | solution.py:392
  97.4 6.4 %expert_out.1 = bf16[32,96,128]{2,1,0:T(8,128)(2,1)} custom-call(bf16[384,2048]{1,0:T(8,128)(2,1)} %get-tuple-element.57.hidden_ref, bf16[2048,1024]{1,0:T(8,128)(2,1)} %bitcast.22), custom_call_target="tpu_custom_call" | custom-call | flops 999999995904 | bytes 1000000 | tf_op jit(solution)/shard_map/expert_out/pallas_call | solution.py:477
  103.8 13.2 %all-to-all-done.2.back_ref = bf16[32,96,128]{2,1,0:T(8,128)(2,1)} async-done(((bf16[32,96,128]{2,1,0:T(8,128)(2,1)}), bf16[32,96,128]{2,1,0:T(8,128)(2,1)}, u32[]{:S(2)}, u32[]{:S(2)}) %all-to-all-start.2) | async-done | bytes 786464 | tf_op jit(solution)/shard_map/all_to_all | solution.py:392
  117.1 2.4 %dattended.1 = (bf16[128,256]{1,0:T(8,128)(2,1)}, bf16[128,256]{1,0:T(8,128)(2,1)}, bf16[128,256]{1,0:T(8,128)(2,1)}, bf16[128,256]{1,0:T(8,128)(2,1)}) custom-call(s32[1]{0:T(128)} %bitcast.me_ref, bf16[2,3,256,128]{3,2,1,0:T(8,128)(2,1)S(1)} %copy-done, bf16[32,96,128]{2,1,0:T(8,128)(2,1)} %all-to-all-done.2.back_ref, bf16[128,1024]{1,0:T(8,128)(2,1)S(1)} %copy-done.1, ...), custom_call_target="tpu_custom_call" | custom-call | tf_op jit(solution)/shard_map/dattended/pallas_call | solution.py:493
  122.8 7.4 %all-to-all-start.3 = ((bf16[32,96,128]{2,1,0:T(8,128)(2,1)}), bf16[32,96,128]{2,1,0:T(8,128)(2,1)S(1)}, u32[]{:S(2)}, u32[]{:S(2)}) async-start(bf16[32,96,128]{2,1,0:T(8,128)(2,1)} %expert_out.1), calls=%async_computation.4 | async-start | bytes 1572864 | tf_op jit(solution)/shard_map/all_to_all | solution.py:392
  130.3 5.3 %attend_back.1 = (bf16[384,256]{1,0:T(8,128)(2,1)}, bf16[384,256]{1,0:T(8,128)(2,1)}, bf16[384,256]{1,0:T(8,128)(2,1)}, bf16[384,256]{1,0:T(8,128)(2,1)}) custom-call(bf16[384,256]{1,0:T(8,128)(2,1)} %get-tuple-element.42.refs_0_, bf16[384,256]{1,0:T(8,128)(2,1)S(1)} %copy-done.4, bf16[384,256]{1,0:T(8,128)(2,1)S(1)} %copy-done.6, ...), custom_call_target="tpu_custom_call" | custom-call | flops 40000000000 | bytes 1000000 | tf_op jit(solution)/shard_map/attend_back/pallas_call | solution.py:505
  139.8 6.0 %collective-permute-done.9.refs_1_ = bf16[384,256]{1,0:T(8,128)(2,1)S(1)} collective-permute-done((bf16[384,256]{1,0:T(8,128)(2,1)}, bf16[384,256]{1,0:T(8,128)(2,1)S(1)}, u32[]{:S(2)}, u32[]{:S(2)}) %collective-permute-start.9) | collective-permute-done | bytes 196640 | tf_op jit(solution)/shard_map/ppermute | solution.py:389
  145.8 2.9 %collective-permute-done.10.refs_2_ = bf16[384,256]{1,0:T(8,128)(2,1)S(1)} collective-permute-done((bf16[384,256]{1,0:T(8,128)(2,1)}, bf16[384,256]{1,0:T(8,128)(2,1)S(1)}, u32[]{:S(2)}, u32[]{:S(2)}) %collective-permute-start.10) | collective-permute-done | bytes 196640 | tf_op jit(solution)/shard_map/ppermute | solution.py:389
  148.7 1.9 %collective-permute-done.11.refs_3_ = bf16[384,256]{1,0:T(8,128)(2,1)S(1)} collective-permute-done((bf16[384,256]{1,0:T(8,128)(2,1)}, bf16[384,256]{1,0:T(8,128)(2,1)S(1)}, u32[]{:S(2)}, u32[]{:S(2)}) %collective-permute-start.11) | collective-permute-done | bytes 196640 | tf_op jit(solution)/shard_map/ppermute | solution.py:389
  150.6 1.8 %reduce-scatter.2.cloned.1.call-done.sums_ref = bf16[128,4096]{1,0:T(8,128)(2,1)} async-done(((bf16[1024,4096]{1,0:T(8,128)(2,1)}), bf16[128,4096]{1,0:T(8,128)(2,1)}) %reduce-scatter.2.cloned.1.call-update) | async-done | bytes 1048592 | tf_op jit(solution)/shard_map/reduce_scatter | solution.py:474
  152.4 3.3 %finish.1 = (bf16[128,1024]{1,0:T(8,128)(2,1)}, bf16[128,1024]{1,0:T(8,128)(2,1)}, bf16[128,1024]{1,0:T(8,128)(2,1)}, bf16[128,1024]{1,0:T(8,128)(2,1)}, f32[128,2048]{1,0:T(8,128)}, /*index=5*/f32[2048,128]{1,0:T(8,128)}) custom-call(s32[1]{0:T(128)} %bitcast.me_ref, bf16[128,4096]{1,0:T(8,128)(2,1)} %reduce-scatter.2.cloned.1.call-done.sums_ref, ...), custom_call_target="tpu_custom_call" | custom-call | tf_op jit(solution)/shard_map/finish/pallas_call | solution.py:519
  (38 shorter events, 12.5 us)
Async XLA Ops:
  10.6 17.5 %collective-permute-start = (bf16[384,256]{1,0:T(8,128)(2,1)}, bf16[384,256]{1,0:T(8,128)(2,1)S(1)}, u32[]{:S(2)}, u32[]{:S(2)}) collective-permute-start(bf16[384,256]{1,0:T(8,128)(2,1)} %get-tuple-element.43), channel_id=1, source_target_pairs={{0,32},{32,64},{64,96},{96,0},{1,33},{33,65},{65,97},{97,1},{2,34}... | collective-permute-start | bytes 589832 | tf_op jit(solution)/shard_map/ppermute | solution.py:389
  12.2 15.9 %collective-permute-start.1 = (bf16[384,256]{1,0:T(8,128)(2,1)}, bf16[384,256]{1,0:T(8,128)(2,1)S(1)}, u32[]{:S(2)}, u32[]{:S(2)}) collective-permute-start(bf16[384,256]{1,0:T(8,128)(2,1)} %get-tuple-element.44), channel_id=1, source_target_pairs={{0,64},{32,96},{64,0},{96,32},{1,65},{33,97},{65,1},{97,33},{2,66}... | collective-permute-start | bytes 589832 | tf_op jit(solution)/shard_map/ppermute | solution.py:389
  15.1 13.1 %collective-permute-start.2 = (bf16[384,256]{1,0:T(8,128)(2,1)}, bf16[384,256]{1,0:T(8,128)(2,1)S(1)}, u32[]{:S(2)}, u32[]{:S(2)}) collective-permute-start(bf16[384,256]{1,0:T(8,128)(2,1)} %get-tuple-element.45), channel_id=1, source_target_pairs={{0,96},{32,0},{64,32},{96,64},{1,97},{33,1},{65,33},{97,65},{2,98}... | collective-permute-start | bytes 589832 | tf_op jit(solution)/shard_map/ppermute | solution.py:389
  16.4 31.6 %all-to-all-start.1 = ((bf16[32,96,128]{2,1,0:T(8,128)(2,1)}), bf16[32,96,128]{2,1,0:T(8,128)(2,1)}, u32[]{:S(2)}, u32[]{:S(2)}) async-start(bf16[32,96,128]{2,1,0:T(8,128)(2,1)} %get-tuple-element.51), calls=%async_computation.1 | async-start | bytes 1572864 | tf_op jit(solution)/shard_map/all_to_all | solution.py:392
  28.1 5.1 %copy-start.3 = (bf16[384,256]{1,0:T(8,128)(2,1)}, bf16[384,256]{1,0:T(8,128)(2,1)S(1)}, u32[]{:S(2)}) copy-start(bf16[384,256]{1,0:T(8,128)(2,1)S(1)} %collective-permute-done.refs_1_) | copy-start | bytes 589828
  33.2 4.6 %collective-permute-start.3 = (bf16[128,256]{1,0:T(8,128)(2,1)}, bf16[128,256]{1,0:T(8,128)(2,1)S(1)}, u32[]{:S(2)}, u32[]{:S(2)}) collective-permute-start(bf16[128,256]{1,0:T(8,128)(2,1)} %get-tuple-element.47), channel_id=1, source_target_pairs={{0,96},{32,0},{64,32},{96,64},{1,97},{33,1},{65,33},{97,65},{2,98}... | collective-permute-start | bytes 196616 | tf_op jit(solution)/shard_map/ppermute | solution.py:389
  33.3 6.2 %collective-permute-start.4 = (bf16[128,256]{1,0:T(8,128)(2,1)}, bf16[128,256]{1,0:T(8,128)(2,1)S(1)}, u32[]{:S(2)}, u32[]{:S(2)}) collective-permute-start(bf16[128,256]{1,0:T(8,128)(2,1)} %get-tuple-element.48), channel_id=1, source_target_pairs={{0,64},{32,96},{64,0},{96,32},{1,65},{33,97},{65,1},{97,33},{2,66}... | collective-permute-start | bytes 196616 | tf_op jit(solution)/shard_map/ppermute | solution.py:389
  36.0 5.7 %collective-permute-start.5 = (bf16[128,256]{1,0:T(8,128)(2,1)}, bf16[128,256]{1,0:T(8,128)(2,1)S(1)}, u32[]{:S(2)}, u32[]{:S(2)}) collective-permute-start(bf16[128,256]{1,0:T(8,128)(2,1)} %get-tuple-element.49), channel_id=1, source_target_pairs={{0,32},{32,64},{64,96},{96,0},{1,33},{33,65},{65,97},{97,1},{2,34}... | collective-permute-start | bytes 196616 | tf_op jit(solution)/shard_map/ppermute | solution.py:389
  48.1 27.0 %all-to-all-start = ((bf16[32,96,128]{2,1,0:T(8,128)(2,1)}), bf16[32,96,128]{2,1,0:T(8,128)(2,1)S(1)}, u32[]{:S(2)}, u32[]{:S(2)}) async-start(bf16[32,96,128]{2,1,0:T(8,128)(2,1)} %get-tuple-element.50), calls=%async_computation | async-start | bytes 1572864 | tf_op jit(solution)/shard_map/all_to_all | solution.py:392
  55.4 97.0 %reduce-scatter.2.cloned.1.call-start = ((), (), s32[]{:S(2)}) async-start(), calls=%async_computation.5 | async-start | bytes 9437184 | tf_op jit(solution)/shard_map/reduce_scatter | solution.py:474
  89.8 27.3 %all-to-all-start.2 = ((bf16[32,96,128]{2,1,0:T(8,128)(2,1)}), bf16[32,96,128]{2,1,0:T(8,128)(2,1)}, u32[]{:S(2)}, u32[]{:S(2)}) async-start(bf16[32,96,128]{2,1,0:T(8,128)(2,1)} %get-tuple-element.55), calls=%async_computation.3 | async-start | bytes 1572864 | tf_op jit(solution)/shard_map/all_to_all | solution.py:392
  97.3 19.8 %copy-start = (bf16[2,3,256,128]{3,2,1,0:T(8,128)(2,1)S(1)}, bf16[2,3,256,128]{3,2,1,0:T(8,128)(2,1)}, u32[]{:S(2)}) copy-start(bf16[2,3,256,128]{3,2,1,0:T(8,128)(2,1)} %get-tuple-element.41.place_ref) | copy-start | bytes 1179652
  97.3 19.8 %copy-start.1 = (bf16[128,1024]{1,0:T(8,128)(2,1)S(1)}, bf16[128,1024]{1,0:T(8,128)(2,1)}, u32[]{:S(2)}) copy-start(bf16[128,1024]{1,0:T(8,128)(2,1)} %get-tuple-element.59.attended_ref) | copy-start | bytes 786436
  97.3 19.7 %copy-start.2 = (bf16[1,128,1024]{2,1,0:T(8,128)(2,1)S(1)}, bf16[1,128,1024]{2,1,0:T(8,128)(2,1)}, u32[]{:S(2)}) copy-start(bf16[1,128,1024]{2,1,0:T(8,128)(2,1)} %param.15) | copy-start | bytes 786436
  97.3 32.9 %copy-start.4 = (bf16[384,256]{1,0:T(8,128)(2,1)S(1)}, bf16[384,256]{1,0:T(8,128)(2,1)}, u32[]{:S(2)}) copy-start(bf16[384,256]{1,0:T(8,128)(2,1)} %copy-done.3) | copy-start | bytes 589828
  97.3 32.9 %copy-start.6 = (bf16[384,256]{1,0:T(8,128)(2,1)S(1)}, bf16[384,256]{1,0:T(8,128)(2,1)}, u32[]{:S(2)}) copy-start(bf16[384,256]{1,0:T(8,128)(2,1)} %copy-done.5) | copy-start | bytes 589828
  97.4 32.9 %copy-start.8 = (bf16[384,256]{1,0:T(8,128)(2,1)S(1)}, bf16[384,256]{1,0:T(8,128)(2,1)}, u32[]{:S(2)}) copy-start(bf16[384,256]{1,0:T(8,128)(2,1)} %copy-done.7) | copy-start | bytes 589828
  119.4 10.8 %collective-permute-start.6 = (bf16[128,256]{1,0:T(8,128)(2,1)}, bf16[128,256]{1,0:T(8,128)(2,1)S(1)}, u32[]{:S(2)}, u32[]{:S(2)}) collective-permute-start(bf16[128,256]{1,0:T(8,128)(2,1)} %get-tuple-element.62), channel_id=1, source_target_pairs={{0,32},{32,64},{64,96},{96,0},{1,33},{33,65},{65,97},{97,1},{2,34}... | collective-permute-start | bytes 196616 | tf_op jit(solution)/shard_map/ppermute | solution.py:389
  120.1 10.1 %collective-permute-start.7 = (bf16[128,256]{1,0:T(8,128)(2,1)}, bf16[128,256]{1,0:T(8,128)(2,1)S(1)}, u32[]{:S(2)}, u32[]{:S(2)}) collective-permute-start(bf16[128,256]{1,0:T(8,128)(2,1)} %get-tuple-element.63), channel_id=1, source_target_pairs={{0,64},{32,96},{64,0},{96,32},{1,65},{33,97},{65,1},{97,33},{2,66}... | collective-permute-start | bytes 196616 | tf_op jit(solution)/shard_map/ppermute | solution.py:389
  121.4 8.9 %collective-permute-start.8 = (bf16[128,256]{1,0:T(8,128)(2,1)}, bf16[128,256]{1,0:T(8,128)(2,1)S(1)}, u32[]{:S(2)}, u32[]{:S(2)}) collective-permute-start(bf16[128,256]{1,0:T(8,128)(2,1)} %get-tuple-element.64), channel_id=1, source_target_pairs={{0,96},{32,0},{64,32},{96,64},{1,97},{33,1},{65,33},{97,65},{2,98}... | collective-permute-start | bytes 196616 | tf_op jit(solution)/shard_map/ppermute | solution.py:389
  122.8 27.9 %all-to-all-start.3 = ((bf16[32,96,128]{2,1,0:T(8,128)(2,1)}), bf16[32,96,128]{2,1,0:T(8,128)(2,1)S(1)}, u32[]{:S(2)}, u32[]{:S(2)}) async-start(bf16[32,96,128]{2,1,0:T(8,128)(2,1)} %expert_out.1), calls=%async_computation.4 | async-start | bytes 1572864 | tf_op jit(solution)/shard_map/all_to_all | solution.py:392
  135.6 10.2 %collective-permute-start.9 = (bf16[384,256]{1,0:T(8,128)(2,1)}, bf16[384,256]{1,0:T(8,128)(2,1)S(1)}, u32[]{:S(2)}, u32[]{:S(2)}) collective-permute-start(bf16[384,256]{1,0:T(8,128)(2,1)} %get-tuple-element.67), channel_id=1, source_target_pairs={{0,96},{32,0},{64,32},{96,64},{1,97},{33,1},{65,33},{97,65},{2,98}... | collective-permute-start | bytes 589832 | tf_op jit(solution)/shard_map/ppermute | solution.py:389
  137.0 11.7 %collective-permute-start.10 = (bf16[384,256]{1,0:T(8,128)(2,1)}, bf16[384,256]{1,0:T(8,128)(2,1)S(1)}, u32[]{:S(2)}, u32[]{:S(2)}) collective-permute-start(bf16[384,256]{1,0:T(8,128)(2,1)} %get-tuple-element.68), channel_id=1, source_target_pairs={{0,64},{32,96},{64,0},{96,32},{1,65},{33,97},{65,1},{97,33},{2,66}... | collective-permute-start | bytes 589832 | tf_op jit(solution)/shard_map/ppermute | solution.py:389
  138.4 12.2 %collective-permute-start.11 = (bf16[384,256]{1,0:T(8,128)(2,1)}, bf16[384,256]{1,0:T(8,128)(2,1)S(1)}, u32[]{:S(2)}, u32[]{:S(2)}) collective-permute-start(bf16[384,256]{1,0:T(8,128)(2,1)} %get-tuple-element.69), channel_id=1, source_target_pairs={{0,32},{32,64},{64,96},{96,0},{1,33},{33,65},{65,97},{97,1},{2,34}... | collective-permute-start | bytes 589832 | tf_op jit(solution)/shard_map/ppermute | solution.py:389
  (2 other events, 10.1 us)
Sparse Core Ops, SparseCore 0:
  89.9 62.4 reduce-scatter.1

commit v8 on v6

--- a/solution.py
+++ b/solution.py
@@ -271,7 +271,7 @@
         unpack_rows(packed_ref, rows)
         turn_rows(pairs, parts, rows, turned_ref)
 
-    out_ref[...] = dot(rows[...], down_ref[...], NT)
+    out_ref[...] = dot(rows[...], down_ref[...], NT).astype(BF)
 
 
 def expert_kernel(pairs, parts, packed_ref, up_ref, dact_ref, grads_turned_ref, act_ref, grads_ref, dnormed_ref, rows, turned, total):
@@ -290,7 +290,7 @@
     act_rounded = act.astype(BF)
     act_ref[...] = act_rounded
     slope = half + act * (1.0 - half) * (2.0 * GELU_COEF + (6.0 * GELU_COEF * 0.044715) * square)
-    dpre = (dact_ref[...] * slope).astype(BF)
+    dpre = (dact_ref[...].astype(F32) * slope).astype(BF)
     grads_ref[:, 0:chunk] = dot(grads_turned_ref[...], act_rounded).astype(BF)
     grads_ref[:, chunk:] = dot(turned[...], dpre).astype(BF)
     part = dot(dpre, up_ref[...], NT)
@@ -438,7 +438,7 @@
     dact, turned = pl.pallas_call(
         functools.partial(dact_kernel, pairs, parts),
         grid=(blocks,),
-        out_shape=[sds((slots, hidden), F32), sds((model, slots), BF)],
+        out_shape=[sds((slots, hidden), BF), sds((model, slots), BF)],
         in_specs=[VMEM, pl.BlockSpec((chunk, model), lambda i: (i, 0))],
         out_specs=[
             pl.BlockSpec((slots, chunk), lambda i: (0, i)),

time: 164 us -> 163 us (level)
  no operation moved by 1% of the time
where the time goes in v8:
time: 163 us
  starting transfers between devices  50.3 us (31%)
  Pallas kernels  49.4 us (30%)
  waiting for transfers between devices  48.7 us (30%)
  between operations  14.2 us (9%)
    all_to_all x4, starting transfers between devices, swap(): lax.all_to_all(packed, 'expert', split_axis=0, concat_axis=0, tiled=True)  33.9 us
    all_to_all x4, waiting for transfers between devices, swap(): lax.all_to_all(packed, 'expert', split_axis=0, concat_axis=0, tiled=True)  30.8 us
    ppermute x12, waiting for transfers between devices, shift(): return near(lax.ppermute(piece, 'seq', pairs_of))  16.5 us
    ppermute x12, starting transfers between devices, shift(): return near(lax.ppermute(piece, 'seq', pairs_of))  16.3 us
    pallas_call x1, Pallas kernels, shards(): pl.pallas_call(functools.partial(expert_kernel, pairs, parts), grid=(bloc...  14.4 us
    pallas_call x1, Pallas kernels, shards(): pl.pallas_call(out_kernel, grid=(blocks,), out_shape=wire, in_specs=[pl.B...  6.46 us
    pallas_call x1, Pallas kernels, shards(): pl.pallas_call(functools.partial(dact_kernel, pairs, parts), grid=(blocks...  5.96 us
    pallas_call x1, Pallas kernels, shards(): pl.pallas_call(functools.partial(attend_back_kernel, parts), out_shape=[t...  5.31 us
  transfers between devices with their start and end apart: 17, of which 10 were waited for; matrix products, arithmetic and copies ran while one was open for 0% of the time, Pallas kernels for 17%

profile of v8, /device:TPU:2, one launch (start us, length us, event | category | flops | bytes accessed | tf_op | source)
XLA Modules:
  0.0 162.7 jit_solution(1410051539135193985)
XLA Ops:
  7.2 3.4 %entry.1 = (bf16[384,256]{1,0:T(8,128)(2,1)}, bf16[384,256]{1,0:T(8,128)(2,1)}, bf16[384,256]{1,0:T(8,128)(2,1)}, bf16[384,256]{1,0:T(8,128)(2,1)}, bf16[2,3,256...) custom-call(s32[1]{0:T(128)} %bitcast.me_ref, bf16[128,1024]{1,0:T(8,128)(2,1)} %bitcast.24, ...), custom_call_target="tpu_custom_call" | custom-call | tf_op jit(solution)/shard_map/entry/pallas_call | solution.py:403
  12.2 2.9 %collective-permute-start.1 = (bf16[384,256]{1,0:T(8,128)(2,1)}, bf16[384,256]{1,0:T(8,128)(2,1)S(1)}, u32[]{:S(2)}, u32[]{:S(2)}) collective-permute-start(bf16[384,256]{1,0:T(8,128)(2,1)} %get-tuple-element.44), channel_id=1, source_target_pairs={{0,64},{32,96},{64,0},{96,32},{1,65},{33,97},{65,1},{97,33},{2,66}... | collective-permute-start | bytes 589832 | tf_op jit(solution)/shard_map/ppermute | solution.py:389
  16.4 11.7 %all-to-all-start.1 = ((bf16[32,96,128]{2,1,0:T(8,128)(2,1)}), bf16[32,96,128]{2,1,0:T(8,128)(2,1)}, u32[]{:S(2)}, u32[]{:S(2)}) async-start(bf16[32,96,128]{2,1,0:T(8,128)(2,1)} %get-tuple-element.51), calls=%async_computation.1 | async-start | bytes 1572864 | tf_op jit(solution)/shard_map/all_to_all | solution.py:392
  28.2 5.0 %attend.1 = (bf16[128,256]{1,0:T(8,128)(2,1)}, bf16[128,256]{1,0:T(8,128)(2,1)}, bf16[128,256]{1,0:T(8,128)(2,1)}, bf16[128,256]{1,0:T(8,128)(2,1)}, bf16[2,512,512]{2,1,0:T(8,128)(2,1)}) custom-call(bf16[384,256]{1,0:T(8,128)(2,1)} %get-tuple-element.42.refs_0_, bf16[384,256]{1,0:T(8,128)(2,1)S(1)} %collective-permute-done.refs_1_, ...), custom_call_target="tpu_custom_call" | custom-call | flops 999999995904 | bytes 1000000 | tf_op jit(solution)/shard_map/attend/pallas_call | solution.py:413
  33.3 2.7 %collective-permute-start.4 = (bf16[128,256]{1,0:T(8,128)(2,1)}, bf16[128,256]{1,0:T(8,128)(2,1)S(1)}, u32[]{:S(2)}, u32[]{:S(2)}) collective-permute-start(bf16[128,256]{1,0:T(8,128)(2,1)} %get-tuple-element.48), channel_id=1, source_target_pairs={{0,64},{32,96},{64,0},{96,32},{1,65},{33,97},{65,1},{97,33},{2,66}... | collective-permute-start | bytes 196616 | tf_op jit(solution)/shard_map/ppermute | solution.py:389
  36.1 1.7 %collective-permute-done.3.refs_1_ = bf16[128,256]{1,0:T(8,128)(2,1)S(1)} collective-permute-done((bf16[128,256]{1,0:T(8,128)(2,1)}, bf16[128,256]{1,0:T(8,128)(2,1)S(1)}, u32[]{:S(2)}, u32[]{:S(2)}) %collective-permute-start.3) | collective-permute-done | bytes 65568 | tf_op jit(solution)/shard_map/ppermute | solution.py:389
  37.8 1.7 %collective-permute-done.4.refs_2_ = bf16[128,256]{1,0:T(8,128)(2,1)S(1)} collective-permute-done((bf16[128,256]{1,0:T(8,128)(2,1)}, bf16[128,256]{1,0:T(8,128)(2,1)S(1)}, u32[]{:S(2)}, u32[]{:S(2)}) %collective-permute-start.4) | collective-permute-done | bytes 65568 | tf_op jit(solution)/shard_map/ppermute | solution.py:389
  39.5 2.2 %collective-permute-done.5.refs_3_ = bf16[128,256]{1,0:T(8,128)(2,1)S(1)} collective-permute-done((bf16[128,256]{1,0:T(8,128)(2,1)}, bf16[128,256]{1,0:T(8,128)(2,1)S(1)}, u32[]{:S(2)}, u32[]{:S(2)}) %collective-permute-start.5) | collective-permute-done | bytes 65568 | tf_op jit(solution)/shard_map/ppermute | solution.py:389
  41.7 2.5 %norm_pack.1 = (bf16[128,1024]{1,0:T(8,128)(2,1)}, bf16[32,96,128]{2,1,0:T(8,128)(2,1)}) custom-call(s32[1]{0:T(128)} %bitcast.me_ref, bf16[2,3,256,128]{3,2,1,0:T(8,128)(2,1)} %get-tuple-element.41.place_ref, bf16[128,256]{1,0:T(8,128)(2,1)} %get-tuple-element.46.refs_0_, bf16[128,256]{1,0:T(8,128)(2,1)S(1)} %collective-permute-done.3.refs_1_, ...), custom_call_target="tpu_custom_call" | custom-call | tf_op jit(solution)/shard_map/norm_pack/pallas_call | solution.py:426
  44.3 3.8 %all-to-all-done.1.packed_ref = bf16[32,96,128]{2,1,0:T(8,128)(2,1)} async-done(((bf16[32,96,128]{2,1,0:T(8,128)(2,1)}), bf16[32,96,128]{2,1,0:T(8,128)(2,1)}, u32[]{:S(2)}, u32[]{:S(2)}) %all-to-all-start.1) | async-done | bytes 786464 | tf_op jit(solution)/shard_map/all_to_all | solution.py:392
  48.1 7.3 %all-to-all-start = ((bf16[32,96,128]{2,1,0:T(8,128)(2,1)}), bf16[32,96,128]{2,1,0:T(8,128)(2,1)S(1)}, u32[]{:S(2)}, u32[]{:S(2)}) async-start(bf16[32,96,128]{2,1,0:T(8,128)(2,1)} %get-tuple-element.50), calls=%async_computation | async-start | bytes 1572864 | tf_op jit(solution)/shard_map/all_to_all | solution.py:392
  55.5 6.0 %dact.1 = (bf16[384,2048]{1,0:T(8,128)(2,1)}, bf16[1024,384]{1,0:T(8,128)(2,1)}) custom-call(bf16[32,96,128]{2,1,0:T(8,128)(2,1)} %all-to-all-done.1.packed_ref, bf16[2048,1024]{1,0:T(8,128)(2,1)} %bitcast.20), custom_call_target="tpu_custom_call" | custom-call | tf_op jit(solution)/shard_map/dact/pallas_call | solution.py:438
  61.4 13.7 %all-to-all-done.packed_ref = bf16[32,96,128]{2,1,0:T(8,128)(2,1)S(1)} async-done(((bf16[32,96,128]{2,1,0:T(8,128)(2,1)}), bf16[32,96,128]{2,1,0:T(8,128)(2,1)S(1)}, u32[]{:S(2)}, u32[]{:S(2)}) %all-to-all-start) | async-done | bytes 786464 | tf_op jit(solution)/shard_map/all_to_all | solution.py:392
  75.1 14.4 %expert.1 = (bf16[384,2048]{1,0:T(8,128)(2,1)}, bf16[1024,4096]{1,0:T(8,128)(2,1)}, bf16[32,96,128]{2,1,0:T(8,128)(2,1)}) custom-call(bf16[32,96,128]{2,1,0:T(8,128)(2,1)S(1)} %all-to-all-done.packed_ref, bf16[1024,2048]{1,0:T(8,128)(2,1)} %bitcast.19, bf16[384,2048]{1,0:T(8,128)(2,1)} %get-tuple-element.52.dact_ref, ...), custom_call_target="tpu_custom_call" | custom-call | tf_op jit(solution)/shard_map/expert/pallas_call | solution.py:451
  89.5 7.5 %all-to-all-start.2 = ((bf16[32,96,128]{2,1,0:T(8,128)(2,1)}), bf16[32,96,128]{2,1,0:T(8,128)(2,1)}, u32[]{:S(2)}, u32[]{:S(2)}) async-start(bf16[32,96,128]{2,1,0:T(8,128)(2,1)} %get-tuple-element.55), calls=%async_computation.3 | async-start | bytes 1572864 | tf_op jit(solution)/shard_map/all_to_all | solution.py:392
  97.1 6.5 %expert_out.1 = bf16[32,96,128]{2,1,0:T(8,128)(2,1)} custom-call(bf16[384,2048]{1,0:T(8,128)(2,1)} %get-tuple-element.57.hidden_ref, bf16[2048,1024]{1,0:T(8,128)(2,1)} %bitcast.21), custom_call_target="tpu_custom_call" | custom-call | flops 999999995904 | bytes 1000000 | tf_op jit(solution)/shard_map/expert_out/pallas_call | solution.py:477
  103.5 13.3 %all-to-all-done.2.back_ref = bf16[32,96,128]{2,1,0:T(8,128)(2,1)} async-done(((bf16[32,96,128]{2,1,0:T(8,128)(2,1)}), bf16[32,96,128]{2,1,0:T(8,128)(2,1)}, u32[]{:S(2)}, u32[]{:S(2)}) %all-to-all-start.2) | async-done | bytes 786464 | tf_op jit(solution)/shard_map/all_to_all | solution.py:392
  116.8 2.7 %dattended.1 = (bf16[128,256]{1,0:T(8,128)(2,1)}, bf16[128,256]{1,0:T(8,128)(2,1)}, bf16[128,256]{1,0:T(8,128)(2,1)}, bf16[128,256]{1,0:T(8,128)(2,1)}) custom-call(s32[1]{0:T(128)} %bitcast.me_ref, bf16[2,3,256,128]{3,2,1,0:T(8,128)(2,1)} %get-tuple-element.41.place_ref, bf16[32,96,128]{2,1,0:T(8,128)(2,1)} %all-to-all-done.2.back_ref, ...), custom_call_target="tpu_custom_call" | custom-call | tf_op jit(solution)/shard_map/dattended/pallas_call | solution.py:493
  122.9 7.4 %all-to-all-start.3 = ((bf16[32,96,128]{2,1,0:T(8,128)(2,1)}), bf16[32,96,128]{2,1,0:T(8,128)(2,1)S(1)}, u32[]{:S(2)}, u32[]{:S(2)}) async-start(bf16[32,96,128]{2,1,0:T(8,128)(2,1)} %expert_out.1), calls=%async_computation.4 | async-start | bytes 1572864 | tf_op jit(solution)/shard_map/all_to_all | solution.py:392
  130.4 5.3 %attend_back.1 = (bf16[384,256]{1,0:T(8,128)(2,1)}, bf16[384,256]{1,0:T(8,128)(2,1)}, bf16[384,256]{1,0:T(8,128)(2,1)}, bf16[384,256]{1,0:T(8,128)(2,1)}) custom-call(bf16[384,256]{1,0:T(8,128)(2,1)} %get-tuple-element.42.refs_0_, bf16[384,256]{1,0:T(8,128)(2,1)S(1)} %copy-done.1, bf16[384,256]{1,0:T(8,128)(2,1)S(1)} %copy-done.3, ...), custom_call_target="tpu_custom_call" | custom-call | flops 40000000000 | bytes 1000000 | tf_op jit(solution)/shard_map/attend_back/pallas_call | solution.py:505
  139.9 6.0 %collective-permute-done.9.refs_1_ = bf16[384,256]{1,0:T(8,128)(2,1)S(1)} collective-permute-done((bf16[384,256]{1,0:T(8,128)(2,1)}, bf16[384,256]{1,0:T(8,128)(2,1)S(1)}, u32[]{:S(2)}, u32[]{:S(2)}) %collective-permute-start.9) | collective-permute-done | bytes 196640 | tf_op jit(solution)/shard_map/ppermute | solution.py:389
  145.9 2.8 %collective-permute-done.10.refs_2_ = bf16[384,256]{1,0:T(8,128)(2,1)S(1)} collective-permute-done((bf16[384,256]{1,0:T(8,128)(2,1)}, bf16[384,256]{1,0:T(8,128)(2,1)S(1)}, u32[]{:S(2)}, u32[]{:S(2)}) %collective-permute-start.10) | collective-permute-done | bytes 196640 | tf_op jit(solution)/shard_map/ppermute | solution.py:389
  148.7 2.0 %collective-permute-done.11.refs_3_ = bf16[384,256]{1,0:T(8,128)(2,1)S(1)} collective-permute-done((bf16[384,256]{1,0:T(8,128)(2,1)}, bf16[384,256]{1,0:T(8,128)(2,1)S(1)}, u32[]{:S(2)}, u32[]{:S(2)}) %collective-permute-start.11) | collective-permute-done | bytes 196640 | tf_op jit(solution)/shard_map/ppermute | solution.py:389
  152.1 3.7 %finish.1 = (bf16[128,1024]{1,0:T(8,128)(2,1)}, bf16[128,1024]{1,0:T(8,128)(2,1)}, bf16[128,1024]{1,0:T(8,128)(2,1)}, bf16[128,1024]{1,0:T(8,128)(2,1)}, f32[128,2048]{1,0:T(8,128)}, /*index=5*/f32[2048,128]{1,0:T(8,128)}) custom-call(s32[1]{0:T(128)} %bitcast.me_ref, bf16[128,4096]{1,0:T(8,128)(2,1)} %reduce-scatter.2.cloned.1.call-done.sums_ref, ...), custom_call_target="tpu_custom_call" | custom-call | tf_op jit(solution)/shard_map/finish/pallas_call | solution.py:519
  (32 shorter events, 12.2 us)
Async XLA Ops:
  10.6 17.5 %collective-permute-start = (bf16[384,256]{1,0:T(8,128)(2,1)}, bf16[384,256]{1,0:T(8,128)(2,1)S(1)}, u32[]{:S(2)}, u32[]{:S(2)}) collective-permute-start(bf16[384,256]{1,0:T(8,128)(2,1)} %get-tuple-element.43), channel_id=1, source_target_pairs={{0,32},{32,64},{64,96},{96,0},{1,33},{33,65},{65,97},{97,1},{2,34}... | collective-permute-start | bytes 589832 | tf_op jit(solution)/shard_map/ppermute | solution.py:389
  12.2 15.9 %collective-permute-start.1 = (bf16[384,256]{1,0:T(8,128)(2,1)}, bf16[384,256]{1,0:T(8,128)(2,1)S(1)}, u32[]{:S(2)}, u32[]{:S(2)}) collective-permute-start(bf16[384,256]{1,0:T(8,128)(2,1)} %get-tuple-element.44), channel_id=1, source_target_pairs={{0,64},{32,96},{64,0},{96,32},{1,65},{33,97},{65,1},{97,33},{2,66}... | collective-permute-start | bytes 589832 | tf_op jit(solution)/shard_map/ppermute | solution.py:389
  15.1 13.1 %collective-permute-start.2 = (bf16[384,256]{1,0:T(8,128)(2,1)}, bf16[384,256]{1,0:T(8,128)(2,1)S(1)}, u32[]{:S(2)}, u32[]{:S(2)}) collective-permute-start(bf16[384,256]{1,0:T(8,128)(2,1)} %get-tuple-element.45), channel_id=1, source_target_pairs={{0,96},{32,0},{64,32},{96,64},{1,97},{33,1},{65,33},{97,65},{2,98}... | collective-permute-start | bytes 589832 | tf_op jit(solution)/shard_map/ppermute | solution.py:389
  16.4 31.6 %all-to-all-start.1 = ((bf16[32,96,128]{2,1,0:T(8,128)(2,1)}), bf16[32,96,128]{2,1,0:T(8,128)(2,1)}, u32[]{:S(2)}, u32[]{:S(2)}) async-start(bf16[32,96,128]{2,1,0:T(8,128)(2,1)} %get-tuple-element.51), calls=%async_computation.1 | async-start | bytes 1572864 | tf_op jit(solution)/shard_map/all_to_all | solution.py:392
  28.1 5.1 %copy-start = (bf16[384,256]{1,0:T(8,128)(2,1)}, bf16[384,256]{1,0:T(8,128)(2,1)S(1)}, u32[]{:S(2)}) copy-start(bf16[384,256]{1,0:T(8,128)(2,1)S(1)} %collective-permute-done.refs_1_) | copy-start | bytes 589828
  28.1 5.1 %copy-start.2 = (bf16[384,256]{1,0:T(8,128)(2,1)}, bf16[384,256]{1,0:T(8,128)(2,1)S(1)}, u32[]{:S(2)}) copy-start(bf16[384,256]{1,0:T(8,128)(2,1)S(1)} %collective-permute-done.1.refs_2_) | copy-start | bytes 589828
  28.2 5.1 %copy-start.4 = (bf16[384,256]{1,0:T(8,128)(2,1)}, bf16[384,256]{1,0:T(8,128)(2,1)S(1)}, u32[]{:S(2)}) copy-start(bf16[384,256]{1,0:T(8,128)(2,1)S(1)} %collective-permute-done.2.refs_3_) | copy-start | bytes 589828
  33.2 4.6 %collective-permute-start.3 = (bf16[128,256]{1,0:T(8,128)(2,1)}, bf16[128,256]{1,0:T(8,128)(2,1)S(1)}, u32[]{:S(2)}, u32[]{:S(2)}) collective-permute-start(bf16[128,256]{1,0:T(8,128)(2,1)} %get-tuple-element.47), channel_id=1, source_target_pairs={{0,96},{32,0},{64,32},{96,64},{1,97},{33,1},{65,33},{97,65},{2,98}... | collective-permute-start | bytes 196616 | tf_op jit(solution)/shard_map/ppermute | solution.py:389
  33.3 6.2 %collective-permute-start.4 = (bf16[128,256]{1,0:T(8,128)(2,1)}, bf16[128,256]{1,0:T(8,128)(2,1)S(1)}, u32[]{:S(2)}, u32[]{:S(2)}) collective-permute-start(bf16[128,256]{1,0:T(8,128)(2,1)} %get-tuple-element.48), channel_id=1, source_target_pairs={{0,64},{32,96},{64,0},{96,32},{1,65},{33,97},{65,1},{97,33},{2,66}... | collective-permute-start | bytes 196616 | tf_op jit(solution)/shard_map/ppermute | solution.py:389
  36.0 5.7 %collective-permute-start.5 = (bf16[128,256]{1,0:T(8,128)(2,1)}, bf16[128,256]{1,0:T(8,128)(2,1)S(1)}, u32[]{:S(2)}, u32[]{:S(2)}) collective-permute-start(bf16[128,256]{1,0:T(8,128)(2,1)} %get-tuple-element.49), channel_id=1, source_target_pairs={{0,32},{32,64},{64,96},{96,0},{1,33},{33,65},{65,97},{97,1},{2,34}... | collective-permute-start | bytes 196616 | tf_op jit(solution)/shard_map/ppermute | solution.py:389
  48.1 27.0 %all-to-all-start = ((bf16[32,96,128]{2,1,0:T(8,128)(2,1)}), bf16[32,96,128]{2,1,0:T(8,128)(2,1)S(1)}, u32[]{:S(2)}, u32[]{:S(2)}) async-start(bf16[32,96,128]{2,1,0:T(8,128)(2,1)} %get-tuple-element.50), calls=%async_computation | async-start | bytes 1572864 | tf_op jit(solution)/shard_map/all_to_all | solution.py:392
  55.4 96.7 %reduce-scatter.2.cloned.1.call-start = ((), (), s32[]{:S(2)}) async-start(), calls=%async_computation.5 | async-start | bytes 9437184 | tf_op jit(solution)/shard_map/reduce_scatter | solution.py:474
  89.5 27.3 %all-to-all-start.2 = ((bf16[32,96,128]{2,1,0:T(8,128)(2,1)}), bf16[32,96,128]{2,1,0:T(8,128)(2,1)}, u32[]{:S(2)}, u32[]{:S(2)}) async-start(bf16[32,96,128]{2,1,0:T(8,128)(2,1)} %get-tuple-element.55), calls=%async_computation.3 | async-start | bytes 1572864 | tf_op jit(solution)/shard_map/all_to_all | solution.py:392
  97.0 33.3 %copy-start.1 = (bf16[384,256]{1,0:T(8,128)(2,1)S(1)}, bf16[384,256]{1,0:T(8,128)(2,1)}, u32[]{:S(2)}) copy-start(bf16[384,256]{1,0:T(8,128)(2,1)} %copy-done) | copy-start | bytes 589828
  97.0 33.3 %copy-start.3 = (bf16[384,256]{1,0:T(8,128)(2,1)S(1)}, bf16[384,256]{1,0:T(8,128)(2,1)}, u32[]{:S(2)}) copy-start(bf16[384,256]{1,0:T(8,128)(2,1)} %copy-done.2) | copy-start | bytes 589828
  97.1 33.3 %copy-start.5 = (bf16[384,256]{1,0:T(8,128)(2,1)S(1)}, bf16[384,256]{1,0:T(8,128)(2,1)}, u32[]{:S(2)}) copy-start(bf16[384,256]{1,0:T(8,128)(2,1)} %copy-done.4) | copy-start | bytes 589828
  119.4 10.8 %collective-permute-start.6 = (bf16[128,256]{1,0:T(8,128)(2,1)}, bf16[128,256]{1,0:T(8,128)(2,1)S(1)}, u32[]{:S(2)}, u32[]{:S(2)}) collective-permute-start(bf16[128,256]{1,0:T(8,128)(2,1)} %get-tuple-element.62), channel_id=1, source_target_pairs={{0,32},{32,64},{64,96},{96,0},{1,33},{33,65},{65,97},{97,1},{2,34}... | collective-permute-start | bytes 196616 | tf_op jit(solution)/shard_map/ppermute | solution.py:389
  120.2 10.1 %collective-permute-start.7 = (bf16[128,256]{1,0:T(8,128)(2,1)}, bf16[128,256]{1,0:T(8,128)(2,1)S(1)}, u32[]{:S(2)}, u32[]{:S(2)}) collective-permute-start(bf16[128,256]{1,0:T(8,128)(2,1)} %get-tuple-element.63), channel_id=1, source_target_pairs={{0,64},{32,96},{64,0},{96,32},{1,65},{33,97},{65,1},{97,33},{2,66}... | collective-permute-start | bytes 196616 | tf_op jit(solution)/shard_map/ppermute | solution.py:389
  121.4 8.9 %collective-permute-start.8 = (bf16[128,256]{1,0:T(8,128)(2,1)}, bf16[128,256]{1,0:T(8,128)(2,1)S(1)}, u32[]{:S(2)}, u32[]{:S(2)}) collective-permute-start(bf16[128,256]{1,0:T(8,128)(2,1)} %get-tuple-element.64), channel_id=1, source_target_pairs={{0,96},{32,0},{64,32},{96,64},{1,97},{33,1},{65,33},{97,65},{2,98}... | collective-permute-start | bytes 196616 | tf_op jit(solution)/shard_map/ppermute | solution.py:389
  122.9 27.8 %all-to-all-start.3 = ((bf16[32,96,128]{2,1,0:T(8,128)(2,1)}), bf16[32,96,128]{2,1,0:T(8,128)(2,1)S(1)}, u32[]{:S(2)}, u32[]{:S(2)}) async-start(bf16[32,96,128]{2,1,0:T(8,128)(2,1)} %expert_out.1), calls=%async_computation.4 | async-start | bytes 1572864 | tf_op jit(solution)/shard_map/all_to_all | solution.py:392
  135.7 10.2 %collective-permute-start.9 = (bf16[384,256]{1,0:T(8,128)(2,1)}, bf16[384,256]{1,0:T(8,128)(2,1)S(1)}, u32[]{:S(2)}, u32[]{:S(2)}) collective-permute-start(bf16[384,256]{1,0:T(8,128)(2,1)} %get-tuple-element.67), channel_id=1, source_target_pairs={{0,96},{32,0},{64,32},{96,64},{1,97},{33,1},{65,33},{97,65},{2,98}... | collective-permute-start | bytes 589832 | tf_op jit(solution)/shard_map/ppermute | solution.py:389
  137.0 11.7 %collective-permute-start.10 = (bf16[384,256]{1,0:T(8,128)(2,1)}, bf16[384,256]{1,0:T(8,128)(2,1)S(1)}, u32[]{:S(2)}, u32[]{:S(2)}) collective-permute-start(bf16[384,256]{1,0:T(8,128)(2,1)} %get-tuple-element.68), channel_id=1, source_target_pairs={{0,64},{32,96},{64,0},{96,32},{1,65},{33,97},{65,1},{97,33},{2,66}... | collective-permute-start | bytes 589832 | tf_op jit(solution)/shard_map/ppermute | solution.py:389
  138.5 12.2 %collective-permute-start.11 = (bf16[384,256]{1,0:T(8,128)(2,1)}, bf16[384,256]{1,0:T(8,128)(2,1)S(1)}, u32[]{:S(2)}, u32[]{:S(2)}) collective-permute-start(bf16[384,256]{1,0:T(8,128)(2,1)} %get-tuple-element.69), channel_id=1, source_target_pairs={{0,32},{32,64},{64,96},{96,0},{1,33},{33,65},{65,97},{97,1},{2,34}... | collective-permute-start | bytes 589832 | tf_op jit(solution)/shard_map/ppermute | solution.py:389
Sparse Core Ops, SparseCore 0:
  89.6 62.4 reduce-scatter.1
